TPU v7x, 32 devices: a whole 2x2x4 slice. The times are simulated.
32 devices in a mesh: dp: 4 (over y, x), expert: 4 (over z), context: 2 (over core).
Axes of the slice: x: 2, y: 2, z: 4, core: 2. Of those that a mesh axis runs over, the one named last changes fastest.
Arguments:
- inputs: bfloat16 [48, 592, 512], P(('dp', 'expert'), 'context'), may hold values from -6 to 6
- key_mask: int32 [48, 592], P(('dp', 'expert')), may hold values from 0 to 1, as said below
- routes: int32 [16, 2, 888, 2], P(('dp', 'expert'), 'context'), may hold values from 0 to 7, all different within a row; in each aligned block of 888 rows (0 to 887, 888 to 1775, ..., all dimensions but the last counted through in order) at most 666 rows name the same one
- priority: int32 [16, 2, 888], P(('dp', 'expert'), 'context'), may hold values from 0 to 65535
- vectors: float32 [7, 512], P(None, 'dp'), may hold values from -1 to 2.1, as said below
- w_qkv: float32 [512, 1536], P('dp'), may hold values from -0.25 to 0.25
- w_out: float32 [512, 512], P('dp'), may hold values from -1.5 to 1.5
- w_router: float32 [512, 8], P('dp'), may hold values from -0.1875 to 0.1875
- w_in: float32 [8, 512, 2048], P('expert', 'dp'), may hold values from -0.25 to 0.25
- b_in: float32 [8, 2048], P('expert', 'dp'), may hold values from -3 to 3
- w_back: float32 [8, 2048, 512], P('expert', 'dp'), may hold values from -2 to 2
- b_back: float32 [8, 512], P('expert', 'dp'), may hold values from -6 to 6
- cotangent: bfloat16 [48, 592, 512], P(('dp', 'expert'), 'context'), may hold values from -6 to 6
Outputs:
- output: bfloat16 [48, 592, 512], P(('dp', 'expert'), 'context')
- grad_inputs: bfloat16 [48, 592, 512], P(('dp', 'expert'), 'context')
- grad_vectors: float32 [7, 512], P(None, 'dp')
- grad_w_qkv: float32 [512, 1536], P('dp')
- grad_w_out: float32 [512, 512], P('dp')
- grad_w_router: float32 [512, 8], P('dp')
- grad_w_in: float32 [8, 512, 2048], P('expert', 'dp')
- grad_b_in: float32 [8, 2048], P('expert', 'dp')
- grad_w_back: float32 [8, 2048, 512], P('expert', 'dp')
- grad_b_back: float32 [8, 512], P('expert', 'dp')
Inputs may be any that keep to these rules, and one draw needn't show every extreme that they name: `key_mask`: each image's row is 1 on its first L positions and 0 after, with L from three quarters of 577, rounded down, to 577; some image has L = 577. `routes`: each row names two different experts and every expert is named; among the rows of one device no expert is named by more than 666 rows, a bound that some block reaches. `vectors`: rows 0 and 5 are positive.
All inputs are finite; a program needn't handle non-finite values.
Results may differ from a plain program's by a relative error of at most 0.02.
Values may be sent and summed in bfloat16 or wider, within the bound.
A program may use at most 256 MiB of HBM per device.

v0:
```python
from functools import partial

import jax
import jax.numpy as jnp
from jax import lax
from jax.sharding import PartitionSpec as P

HEADS = 8


EPSILON = 1e-06


def norm_forward(values, gain_row, offset_row):
    average = jnp.mean(values, axis=-1, keepdims=True)
    centred = values - average
    inv_scale = lax.rsqrt(jnp.mean(centred * centred, axis=-1, keepdims=True) + EPSILON)
    unit_rows = centred * inv_scale
    return (unit_rows * gain_row + offset_row, unit_rows, inv_scale)


def norm_backward(grad_normed, unit_rows, inv_scale, gain_row):
    scaled = grad_normed * gain_row
    centre_term = jnp.mean(scaled, axis=-1, keepdims=True)
    unit_term = jnp.mean(scaled * unit_rows, axis=-1, keepdims=True)
    return inv_scale * (scaled - centre_term - unit_rows * unit_term)


def score_block(query_heads, key_heads, allowed, score_scale):
    raw_scores = (
        jnp.einsum("iqhd,ikhd->ihqk", query_heads, key_heads, preferred_element_type=jnp.float32)
        * score_scale
    )
    return jnp.where(allowed[:, None, None, :], raw_scores, -1e30)


def assign(route_rows, prio_rows, expert_count, capacity):
    row_count = route_rows.shape[0]
    order_key = prio_rows * row_count + jnp.arange(row_count, dtype=jnp.int32)
    order = jnp.argsort(order_key)
    inverse = jnp.argsort(order)
    ranked = route_rows[order]
    expert_iota = jnp.arange(expert_count, dtype=jnp.int32)
    first_hot = (ranked[:, 0:1] == expert_iota[None, :]).astype(jnp.int32)
    second_hot = (ranked[:, 1:2] == expert_iota[None, :]).astype(jnp.int32)
    first_rank = jnp.sum((jnp.cumsum(first_hot, axis=0) - first_hot) * first_hot, axis=1)
    second_base = jnp.cumsum(second_hot, axis=0) - second_hot + jnp.sum(first_hot, axis=0)[None, :]
    second_rank = jnp.sum(second_base * second_hot, axis=1)
    ranks = jnp.stack([first_rank, second_rank], axis=1)[inverse]
    flat_slot = route_rows * capacity + ranks
    return jnp.where(ranks < capacity, flat_slot, expert_count * capacity)


def scatter_slots(row_pairs, slot_table, slot_total):
    buffer = jnp.zeros((slot_total + 1, row_pairs.shape[2]), row_pairs.dtype)
    buffer = (
        buffer.at[slot_table[:, 0]].set(row_pairs[:, 0]).at[slot_table[:, 1]].set(row_pairs[:, 1])
    )
    return buffer[:-1]


def shards(
    inputs,
    key_mask,
    routes,
    priority,
    vectors,
    w_qkv,
    w_out,
    w_router,
    w_in,
    b_in,
    w_back,
    b_back,
    cotangent,
):
    image_count, half_len, model_width = inputs.shape
    seq_len = key_mask.shape[1]
    row_count = image_count * half_len
    head_dim = model_width // HEADS
    score_scale = head_dim ** (-0.5)
    vec_bf, qkv_w, out_w, router_w = (
        lax.all_gather(vectors.astype(jnp.bfloat16), "dp", axis=1, tiled=True),
        lax.all_gather(w_qkv.astype(jnp.bfloat16), "dp", axis=0, tiled=True),
        lax.all_gather(w_out.astype(jnp.bfloat16), "dp", axis=0, tiled=True),
        lax.all_gather(w_router.astype(jnp.bfloat16), "dp", axis=0, tiled=True),
    )
    vec_f = vec_bf.astype(jnp.float32)
    source = inputs.astype(jnp.float32).reshape(row_count, model_width)
    normed_one, unit_one, inv_one = norm_forward(source, vec_f[0], vec_f[1])
    acts_one = normed_one.astype(jnp.bfloat16)
    projected = jnp.dot(acts_one, qkv_w, preferred_element_type=jnp.float32)
    queries = (projected[:, :model_width] + vec_f[2]).astype(jnp.bfloat16)
    keys_local = projected[:, model_width : 2 * model_width].astype(jnp.bfloat16)
    values_local = (projected[:, 2 * model_width :] + vec_f[3]).astype(jnp.bfloat16)
    keys_all, values_all = (
        lax.all_gather(
            keys_local.reshape(image_count, half_len, model_width), "context", axis=1, tiled=True
        ),
        lax.all_gather(
            values_local.reshape(image_count, half_len, model_width), "context", axis=1, tiled=True
        ),
    )
    query_heads = queries.reshape(image_count, half_len, HEADS, head_dim)
    key_heads = keys_all.reshape(image_count, seq_len, HEADS, head_dim)
    value_heads = values_all.reshape(image_count, seq_len, HEADS, head_dim)
    allowed = key_mask > 0
    scores = score_block(query_heads, key_heads, allowed, score_scale)
    top_score = jnp.max(scores, axis=-1, keepdims=True)
    log_total = top_score + jnp.log(jnp.sum(jnp.exp(scores - top_score), axis=-1, keepdims=True))
    probs_bf = jnp.exp(scores - log_total).astype(jnp.bfloat16)
    mixed_bf = (
        jnp.einsum("ihqk,ikhd->iqhd", probs_bf, value_heads, preferred_element_type=jnp.float32)
        .astype(jnp.bfloat16)
        .reshape(row_count, model_width)
    )
    after_attn = source + jnp.dot(mixed_bf, out_w, preferred_element_type=jnp.float32) + vec_f[4]
    normed_two, unit_two, inv_two = norm_forward(after_attn, vec_f[5], vec_f[6])
    acts_two = normed_two.astype(jnp.bfloat16)
    logits = jnp.dot(acts_two, router_w, preferred_element_type=jnp.float32)
    router_probs = jax.nn.softmax(logits, axis=-1)
    expert_count = router_w.shape[1]
    group_size = lax.axis_size("expert")
    per_device = expert_count // group_size
    capacity = max(2, 3 * row_count // expert_count)
    slot_total = expert_count * capacity
    route_rows = routes.reshape(row_count, 2)
    slot_table = assign(route_rows, priority.reshape(row_count), expert_count, capacity)
    gate_values = jnp.take_along_axis(router_probs, route_rows, axis=1)
    acts_pairs = jnp.broadcast_to(acts_two[:, None, :], (row_count, 2, model_width))
    send_rows = scatter_slots(acts_pairs, slot_table, slot_total).reshape(
        group_size, per_device, capacity, model_width
    )
    in_w, in_b, back_w, back_b = (
        lax.all_gather(w_in.astype(jnp.bfloat16), "dp", axis=1, tiled=True),
        lax.all_gather(b_in.astype(jnp.bfloat16), "dp", axis=1, tiled=True),
        lax.all_gather(w_back.astype(jnp.bfloat16), "dp", axis=1, tiled=True),
        lax.all_gather(b_back.astype(jnp.bfloat16), "dp", axis=1, tiled=True),
    )
    received = lax.all_to_all(send_rows, "expert", split_axis=0, concat_axis=0, tiled=True)
    pre_act = (
        jnp.einsum("sjcd,jdf->sjcf", received, in_w, preferred_element_type=jnp.float32)
        + in_b.astype(jnp.float32)[None, :, None, :]
    )
    hidden = jax.nn.gelu(pre_act, approximate=False).astype(jnp.bfloat16)
    expert_rows = (
        jnp.einsum("sjcf,jfd->sjcd", hidden, back_w, preferred_element_type=jnp.float32)
        + back_b.astype(jnp.float32)[None, :, None, :]
    )
    expert_rows, pre_act, received = (expert_rows.astype(jnp.bfloat16), pre_act, received)
    returned = lax.all_to_all(expert_rows, "expert", split_axis=0, concat_axis=0, tiled=True)
    out_table = jnp.concatenate(
        [returned.reshape(slot_total, model_width), jnp.zeros((1, model_width), jnp.bfloat16)],
        axis=0,
    )
    picked = out_table[slot_table].astype(jnp.float32)
    final_rows = after_attn + jnp.sum(gate_values[:, :, None] * picked, axis=1)
    output = final_rows.astype(jnp.bfloat16).reshape(image_count, half_len, model_width)
    grad_final = cotangent.astype(jnp.float32).reshape(row_count, model_width)
    grad_gates = jnp.sum(grad_final[:, None, :] * picked, axis=2)
    slot_grads = (gate_values[:, :, None] * grad_final[:, None, :]).astype(jnp.bfloat16)
    grad_send = scatter_slots(slot_grads, slot_table, slot_total).reshape(
        group_size, per_device, capacity, model_width
    )
    grad_expert = lax.all_to_all(grad_send, "expert", split_axis=0, concat_axis=0, tiled=True)
    in_matrix, back_matrix = (
        lax.all_gather(w_in.astype(jnp.bfloat16), "dp", axis=1, tiled=True),
        lax.all_gather(w_back.astype(jnp.bfloat16), "dp", axis=1, tiled=True),
    )
    gelu_value, gelu_pullback = jax.vjp(partial(jax.nn.gelu, approximate=False), pre_act)
    hidden = gelu_value.astype(jnp.bfloat16)
    grad_b_back = jnp.sum(grad_expert.astype(jnp.float32), axis=(0, 2))
    grad_w_back = jnp.einsum(
        "sjcf,sjcd->jfd", hidden, grad_expert, preferred_element_type=jnp.float32
    )
    grad_hidden = jnp.einsum(
        "sjcd,jfd->sjcf", grad_expert, back_matrix, preferred_element_type=jnp.float32
    )
    grad_pre = gelu_pullback(grad_hidden)[0]
    grad_b_in = jnp.sum(grad_pre, axis=(0, 2))
    grad_pre_bf = grad_pre.astype(jnp.bfloat16)
    grad_w_in = jnp.einsum(
        "sjcd,sjcf->jdf", received, grad_pre_bf, preferred_element_type=jnp.float32
    )
    grad_received = jnp.einsum(
        "sjcf,jdf->sjcd", grad_pre_bf, in_matrix, preferred_element_type=jnp.float32
    ).astype(jnp.bfloat16)
    grad_returned = lax.all_to_all(grad_received, "expert", split_axis=0, concat_axis=0, tiled=True)
    share_w_in, share_b_in, share_w_back, share_b_back = (
        lax.psum_scatter(
            grad_w_in.astype(jnp.bfloat16), ("dp", "context"), scatter_dimension=1, tiled=True
        ).astype(jnp.float32),
        lax.psum_scatter(
            grad_b_in.astype(jnp.bfloat16), ("dp", "context"), scatter_dimension=1, tiled=True
        ).astype(jnp.float32),
        lax.psum_scatter(
            grad_w_back.astype(jnp.bfloat16), ("dp", "context"), scatter_dimension=1, tiled=True
        ).astype(jnp.float32),
        lax.psum_scatter(
            grad_b_back.astype(jnp.bfloat16), ("dp", "context"), scatter_dimension=1, tiled=True
        ).astype(jnp.float32),
    )
    grad_w_in, grad_b_in, grad_w_back, grad_b_back = (
        lax.all_gather(share_w_in.astype(jnp.bfloat16), "context", axis=1, tiled=True).astype(
            share_w_in.dtype
        ),
        lax.all_gather(share_b_in.astype(jnp.bfloat16), "context", axis=1, tiled=True).astype(
            share_b_in.dtype
        ),
        lax.all_gather(share_w_back.astype(jnp.bfloat16), "context", axis=1, tiled=True).astype(
            share_w_back.dtype
        ),
        lax.all_gather(share_b_back.astype(jnp.bfloat16), "context", axis=1, tiled=True).astype(
            share_b_back.dtype
        ),
    )
    back_table = jnp.concatenate(
        [grad_returned.reshape(slot_total, model_width), jnp.zeros((1, model_width), jnp.bfloat16)],
        axis=0,
    )
    grad_acts_two = jnp.sum(back_table[slot_table].astype(jnp.float32), axis=1)
    expert_iota = jnp.arange(expert_count, dtype=jnp.int32)
    one_hot = (route_rows[:, :, None] == expert_iota[None, None, :]).astype(jnp.float32)
    grad_probs = jnp.sum(one_hot * grad_gates[:, :, None], axis=1)
    grad_logits = router_probs * (
        grad_probs - jnp.sum(router_probs * grad_probs, axis=1, keepdims=True)
    )
    grad_logits_bf = grad_logits.astype(jnp.bfloat16)
    grad_router = jnp.einsum(
        "td,te->de", acts_two, grad_logits_bf, preferred_element_type=jnp.float32
    )
    grad_acts_two = grad_acts_two + jnp.einsum(
        "te,de->td", grad_logits_bf, router_w, preferred_element_type=jnp.float32
    )
    grad_gain_two = jnp.sum(grad_acts_two * unit_two, axis=0)
    grad_offset_two = jnp.sum(grad_acts_two, axis=0)
    grad_after = grad_final + norm_backward(grad_acts_two, unit_two, inv_two, vec_f[5])
    grad_bias_out = jnp.sum(grad_after, axis=0)
    grad_after_bf = grad_after.astype(jnp.bfloat16)
    grad_out = jnp.einsum("td,te->de", mixed_bf, grad_after_bf, preferred_element_type=jnp.float32)
    grad_mixed = jnp.einsum(
        "te,de->td", grad_after_bf, out_w, preferred_element_type=jnp.float32
    ).astype(jnp.bfloat16)
    grad_mixed_heads = grad_mixed.reshape(image_count, half_len, HEADS, head_dim)
    scores_again = score_block(query_heads, key_heads, allowed, score_scale)
    probs_again = jnp.exp(scores_again - log_total)
    probs_again_bf = probs_again.astype(jnp.bfloat16)
    grad_values_all = jnp.einsum(
        "ihqk,iqhd->ikhd", probs_again_bf, grad_mixed_heads, preferred_element_type=jnp.float32
    )
    grad_probs_att = jnp.einsum(
        "iqhd,ikhd->ihqk", grad_mixed_heads, value_heads, preferred_element_type=jnp.float32
    )
    row_delta = jnp.sum(probs_again * grad_probs_att, axis=-1, keepdims=True)
    grad_scores = (probs_again * (grad_probs_att - row_delta)).astype(jnp.bfloat16)
    grad_queries = (
        jnp.einsum("ihqk,ikhd->iqhd", grad_scores, key_heads, preferred_element_type=jnp.float32)
        * score_scale
    )
    grad_keys_all = (
        jnp.einsum("ihqk,iqhd->ikhd", grad_scores, query_heads, preferred_element_type=jnp.float32)
        * score_scale
    )
    grad_keys, grad_values = (
        lax.psum_scatter(
            grad_keys_all.reshape(image_count, seq_len, model_width).astype(jnp.bfloat16),
            "context",
            scatter_dimension=1,
            tiled=True,
        ).astype(jnp.float32),
        lax.psum_scatter(
            grad_values_all.reshape(image_count, seq_len, model_width).astype(jnp.bfloat16),
            "context",
            scatter_dimension=1,
            tiled=True,
        ).astype(jnp.float32),
    )
    grad_q_bf = grad_queries.reshape(row_count, model_width).astype(jnp.bfloat16)
    grad_k_bf = grad_keys.reshape(row_count, model_width).astype(jnp.bfloat16)
    grad_v_bf = grad_values.reshape(row_count, model_width).astype(jnp.bfloat16)
    grad_projected = jnp.concatenate([grad_q_bf, grad_k_bf, grad_v_bf], axis=1)
    grad_bias_query = jnp.sum(grad_q_bf.astype(jnp.float32), axis=0)
    grad_bias_value = jnp.sum(grad_v_bf.astype(jnp.float32), axis=0)
    grad_qkv = jnp.einsum("td,tc->dc", acts_one, grad_projected, preferred_element_type=jnp.float32)
    grad_acts_one = jnp.einsum(
        "tc,dc->td", grad_projected, qkv_w, preferred_element_type=jnp.float32
    )
    grad_gain_one = jnp.sum(grad_acts_one * unit_one, axis=0)
    grad_offset_one = jnp.sum(grad_acts_one, axis=0)
    grad_source = grad_after + norm_backward(grad_acts_one, unit_one, inv_one, vec_f[0])
    grad_inputs = grad_source.astype(jnp.bfloat16).reshape(image_count, half_len, model_width)
    grad_vectors = jnp.stack(
        [
            grad_gain_one,
            grad_offset_one,
            grad_bias_query,
            grad_bias_value,
            grad_bias_out,
            grad_gain_two,
            grad_offset_two,
        ],
        axis=0,
    )
    part_vectors, part_qkv, part_out, part_router = (
        lax.psum_scatter(
            grad_vectors.astype(jnp.bfloat16), "dp", scatter_dimension=1, tiled=True
        ).astype(jnp.float32),
        lax.psum_scatter(
            grad_qkv.astype(jnp.bfloat16), "dp", scatter_dimension=0, tiled=True
        ).astype(jnp.float32),
        lax.psum_scatter(
            grad_out.astype(jnp.bfloat16), "dp", scatter_dimension=0, tiled=True
        ).astype(jnp.float32),
        lax.psum_scatter(
            grad_router.astype(jnp.bfloat16), "dp", scatter_dimension=0, tiled=True
        ).astype(jnp.float32),
    )
    grad_vectors, grad_qkv, grad_out, grad_router = (
        lax.psum(part_vectors.astype(jnp.bfloat16), ("expert", "context")).astype(jnp.float32),
        lax.psum(part_qkv.astype(jnp.bfloat16), ("expert", "context")).astype(jnp.float32),
        lax.psum(part_out.astype(jnp.bfloat16), ("expert", "context")).astype(jnp.float32),
        lax.psum(part_router.astype(jnp.bfloat16), ("expert", "context")).astype(jnp.float32),
    )
    return (
        output,
        grad_inputs,
        grad_vectors,
        grad_qkv,
        grad_out,
        grad_router,
        grad_w_in,
        grad_b_in,
        grad_w_back,
        grad_b_back,
    )


def solution(mesh):
    placed = (
        P(("dp", "expert"), "context", None),
        P(("dp", "expert"), None),
        P(("dp", "expert"), "context", None, None),
        P(("dp", "expert"), "context", None),
        P(None, "dp"),
        P("dp", None),
        P("dp", None),
        P("dp", None),
        P("expert", "dp", None),
        P("expert", "dp"),
        P("expert", "dp", None),
        P("expert", "dp"),
        P(("dp", "expert"), "context", None),
    )
    return jax.shard_map(
        shards,
        mesh=mesh,
        in_specs=placed,
        out_specs=(
            P(("dp", "expert"), "context", None),
            P(("dp", "expert"), "context", None),
            P(None, "dp"),
            P("dp", None),
            P("dp", None),
            P("dp", None),
            P("expert", "dp", None),
            P("expert", "dp"),
            P("expert", "dp", None),
            P("expert", "dp"),
        ),
        check_vma=False,
    )
```

profile of v0, /device:TPU:0, one launch (start us, length us, event | category | flops | bytes accessed | tf_op | source)
XLA Modules:
  0.0 971.2 jit_solution(6886844711472974682)
XLA Ops:
  12.1 9.5 all_gather.44
  22.0 22.1 %all-gather.9.cloned.1.call-done = bf16[512,1536]{1,0:T(8,128)(2,1)} async-done(((bf16[128,1536]{1,0:T(8,128)(2,1)}), bf16[512,1536]{1,0:T(8,128)(2,1)}) %all-gather.9.cloned.1.call-update) | async-done | bytes 1572880 | tf_op jit(solution)/shard_map/all_gather | solution.py:84
  44.1 3.0 fusion.67
  50.7 3.8 fusion.46
  57.5 10.0 %all_gather.48 = bf16[512,512]{1,0:T(8,128)(2,1)S(1)} all-gather(bf16[128,512]{1,0:T(8,128)(2,1)S(1)} %convert_element_type.237), channel_id=1, replica_groups=mesh['dp'=4,'expert'=4,'context'=2] {'dp'}, dimensions={0}, use_global_device_ids=true | all-gather | bytes 655360 | tf_op jit(solution)/shard_map/all_gather | solution.py:85
  67.8 4.4 sort.31
  80.3 4.4 sort.32
  95.1 5.4 fusion.21
  100.6 4.6 exponential_reduce_fusion
  110.1 9.0 fusion.52
  121.3 4.3 reshape.278
  128.1 8.2 scatter_custom_fusion
  136.4 10.0 %scatter_custom_fusion.1 = bf16[2665,512]{1,0:T(8,128)(2,1)} fusion(bf16[2665,512]{1,0:T(8,128)(2,1)} %scatter_custom_fusion, s32[888]{0:T(1024)S(1)} %get-tuple-element.26, f32[888,512]{1,0:T(8,128)S(1)} %fusion.51, f32[512]{0:T(512)S(1)} %bitcast.281, f32[512]{0:T(512)S(1)} %bitcast.270, f32[888]{0:T(1024)S(1)} %add_rsqrt_fusion.1, ...), kind=kCustom, calls=%fused_computation.188 | custom fusion | flops 2273280 | bytes 4559872 | tf_op jit(solution)/shard_map/scatter | solution.py:57
  146.4 3.5 slice.131
  152.4 4.4 copy.114
  156.8 4.3 all-to-all-start
  163.9 7.1 all_gather.51
  171.0 8.0 all_gather.53
  179.1 41.5 %all-to-all-done = bf16[4,2,333,512]{3,1,2,0:T(2,128)(2,1)S(1)} async-done(((bf16[4,2,333,512]{3,1,2,0:T(2,128)(2,1)}), bf16[4,2,333,512]{3,1,2,0:T(2,128)(2,1)S(1)}, u32[]{:S(2)}, u32[]{:S(2)}) %all-to-all-start) | async-done | bytes 2727968 | tf_op jit(solution)/shard_map/all_to_all | solution.py:140
  220.6 57.0 %fusion.8 = (bf16[4,2,333,2048]{3,2,0,1:T(8,128)(2,1)}, f32[4,2,333,2048]{3,2,0,1:T(8,128)}, f32[2,4,333,2048]{3,2,1,0:T(8,128)}) fusion(f32[2,2048]{1,0:T(2,128)S(1)} %convert_element_type.244, bf16[2,512,2048]{2,1,0:T(8,128)(2,1)} %all-gather.15.cloned.1.call-done, bf16[4,2,333,512]{3,1,2,0:T(2,128)(2,1)S(1)} %all-to-all-done), kind=kOutput, calls=%fused_computation.25 | convolution fusion | flops 5946900480 | bytes 61497344 | tf_op jit(solution)/shard_map/sjcd,jdf->sjcf/dot_general | solution.py:142
  277.7 9.9 %fusion.35 = bf16[4,2,333,512]{3,2,0,1:T(8,128)(2,1)S(1)} fusion(f32[2,512]{1,0:T(2,128)S(1)} %convert_element_type.248, bf16[4,2,333,2048]{3,2,0,1:T(8,128)(2,1)} %get-tuple-element.38, bf16[2,2048,512]{2,1,0:T(8,128)(2,1)} %all-gather.17.cloned.1.call-done), kind=kOutput, calls=%fused_computation.64 | convolution fusion | flops 5589540864 | bytes 17838080 | tf_op jit(solution)/shard_map/sjcf,jfd->sjcd/dot_general | solution.py:147
  287.5 4.4 copy.116
  291.9 4.7 all-to-all-start.1
  302.0 7.5 all_gather.49
  311.5 17.0 %gather_fusion.4 = f32[1776]{0:T(1024)S(1)} fusion(f32[888,8]{0,1:T(8,128)S(1)} %fusion.75, s32[1776]{0:T(1024)S(1)} %reshape.330), kind=kCustom, calls=%fused_computation.4 | custom fusion | bytes 28416 | tf_op jit(solution)/shard_map/jit(take_along_axis)/gather | solution.py:129
  329.2 28.7 %all-to-all-done.1 = bf16[4,2,333,512]{3,1,2,0:T(2,128)(2,1)} async-done(((bf16[4,2,333,512]{3,1,2,0:T(2,128)(2,1)}), bf16[4,2,333,512]{3,1,2,0:T(2,128)(2,1)}, u32[]{:S(2)}, u32[]{:S(2)}) %all-to-all-start.1) | async-done | bytes 2727968 | tf_op jit(solution)/shard_map/all_to_all | solution.py:151
  364.5 6.1 gather_fusion.2
  370.6 5.3 reshape.372
  375.8 6.0 multiply_reduce_fusion.1
  381.8 6.9 scatter_custom_fusion.2
  388.8 8.1 scatter_custom_fusion.3
  404.1 63.9 %all_to_all.20 = bf16[4,2,333,512]{3,1,2,0:T(2,128)(2,1)S(1)} all-to-all(bf16[4,2,333,512]{3,1,2,0:T(2,128)(2,1)S(1)} %copy.119), channel_id=1, replica_groups=mesh['dp'=4,'expert'=4,'context'=2] {'expert'}, dimensions={0} | all-to-all | bytes 5455872 | tf_op jit(solution)/shard_map/all_to_all | solution.py:165
  467.9 12.1 %bitcast_convert_fusion = bf16[2,2048,512]{2,1,0:T(8,128)(2,1)} fusion(bf16[4,2,333,2048]{3,2,0,1:T(8,128)(2,1)} %get-tuple-element.38, bf16[4,2,333,512]{3,1,2,0:T(2,128)(2,1)S(1)} %all_to_all.20), kind=kOutput, calls=%fused_computation.46 | convolution fusion | flops 5588910080 | bytes 17833984 | tf_op jit(solution)/shard_map/sjcf,sjcd->jfd/dot_general | solution.py:173
  480.7 24.0 %fusion.89 = (bf16[2,2048]{1,0:T(2,128)(2,1)S(1)}, bf16[4,2,333,2048]{3,2,0,1:T(8,128)(2,1)}) fusion(f32[4,2,333,2048]{3,2,0,1:T(8,128)} %get-tuple-element.39, bf16[2,2048,512]{2,1,0:T(8,128)(2,1)} %all-gather.17.cloned.1.call-done, bf16[4,2,333,512]{3,1,2,0:T(2,128)(2,1)S(1)} %all_to_all.20, f32[2,4,333,2048]{3,2,1,0:T(8,128)} %get-tuple-element.55, ...), kind=kOutput, calls=%fused_computation.187 | convolution fusion | flops 5674102784 | bytes 61505536 | tf_op jit(solution)/shard_map/sjcd,jfd->sjcf/dot_general | solution.py:176
  504.7 10.3 %convert_bitcast_fusion = bf16[4,2,333,512]{3,2,0,1:T(8,128)(2,1)S(1)} fusion(bf16[2,512,2048]{2,1,0:T(8,128)(2,1)} %all-gather.15.cloned.1.call-done, bf16[4,2,333,2048]{3,2,0,1:T(8,128)(2,1)} %get-tuple-element.65), kind=kOutput, calls=%fused_computation.66 | convolution fusion | flops 5588176896 | bytes 17833984 | tf_op jit(solution)/shard_map/sjcf,jdf->sjcd/dot_general | solution.py:185
  515.0 4.4 copy.121
  519.4 4.9 all-to-all-start.3
  524.6 12.6 %bitcast_convert_fusion.1 = bf16[2,512,2048]{2,1,0:T(8,128)(2,1)} fusion(bf16[4,2,333,2048]{3,2,0,1:T(8,128)(2,1)} %get-tuple-element.65, bf16[4,2,333,512]{3,1,2,0:T(2,128)(2,1)S(1)} %copy-done.31), kind=kOutput, calls=%fused_computation.47 | convolution fusion | flops 5588910080 | bytes 17833984 | tf_op jit(solution)/shard_map/sjcd,sjcf->jdf/dot_general | solution.py:182
  537.2 48.4 %all-to-all-done.3 = bf16[4,2,333,512]{3,1,2,0:T(2,128)(2,1)} async-done(((bf16[4,2,333,512]{3,1,2,0:T(2,128)(2,1)}), bf16[4,2,333,512]{3,1,2,0:T(2,128)(2,1)}, u32[]{:S(2)}, u32[]{:S(2)}) %all-to-all-start.3) | async-done | bytes 2727968 | tf_op jit(solution)/shard_map/all_to_all | solution.py:188
  592.2 6.5 gather_fusion.3
  598.7 5.1 reshape.373
  603.8 7.7 reduce_sum.265
  623.1 16.7 %multiply_reduce_fusion = (f32[3,8,296]{2,1,0:T(8,128)S(1)}, f32[3,8,296,592]{3,2,1,0:T(8,128)}) fusion(f32[3,8,296,592]{3,2,1,0:T(8,128)} %copy-done, f32[3,8,296]{2,1,0:T(8,128)S(1)} %copy-done.38, pred[3,592]{1,0:T(4,128)(4,1)S(1)} %copy-done.41, bf16[3,296,8,64]{1,3,2,0:T(8,128)(2,1)S(1)} %copy.126, bf16[3,592,8,64]{1,3,2,0:T(8,128)(2,1)S(1)} %bitcast.253), kind=kOutput, calls=%fused_computation.40 | convolution fusion | flops 559333440 | bytes 36431088 | tf_op jit(solution)/shard_map/iqhd,ikhd->ihqk/dot_general | solution.py:251
  639.9 13.2 %multiply_convert_fusion = bf16[3,8,296,592]{3,2,1,0:T(8,128)(2,1)S(1)} fusion(f32[3,8,296,592]{3,2,1,0:T(8,128)} %get-tuple-element.60, f32[3,8,296,592]{3,2,1,0:T(8,128)} %copy-done, f32[3,8,296]{2,1,0:T(8,128)S(1)} %get-tuple-element.59, f32[3,8,296]{2,1,0:T(8,128)S(1)} %copy-done.38, pred[3,592]{1,0:T(4,128)(4,1)S(1)} %copy-done.41), kind=kLoop, calls=%fused_computation.39 | loop fusion | flops 25233408 | bytes 42114288 | tf_op jit(solution)/shard_map/convert_element_type | solution.py:255
  653.1 3.6 multiply_convert_fusion.1
  657.2 4.4 copy.141
  663.5 10.9 %convolution_convert_fusion.1 = bf16[3,8,64,592]{3,2,1,0:T(8,128)(2,1)} fusion(bf16[3,296,8,64]{1,3,2,0:T(8,128)(2,1)} %copy-done.25, f32[3,8,296,592]{3,2,1,0:T(8,128)} %copy-done, f32[3,8,296]{2,1,0:T(8,128)S(1)} %copy-done.38, pred[3,592]{1,0:T(4,128)(4,1)S(1)} %copy-done.41), kind=kOutput, calls=%fused_computation.72 | convolution fusion | flops 556044288 | bytes 19580400 | tf_op jit(solution)/shard_map/ihqk,iqhd->ikhd/dot_general | solution.py:248
  674.5 4.4 copy.143
  681.9 4.1 reduce_sum.282
  691.2 7.1 fusion.88
  701.0 3.1 reshape.382
  707.5 3.1 reshape.384
  714.2 5.3 convolution_convert_fusion
  720.4 31.7 %reduce-scatter.41.cloned.1.call-done = bf16[64,2]{1,0:T(8,128)(2,1)} async-done(((bf16[512,2]{1,0:T(8,128)(2,1)}), bf16[64,2]{1,0:T(8,128)(2,1)}) %reduce-scatter.41.cloned.1.call-update) | async-done | bytes 272
  755.3 33.9 %reduce-scatter.39.cloned.1.call-done = bf16[256,2]{1,0:T(8,128)(2,1)} async-done(((bf16[2048,2]{1,0:T(8,128)(2,1)}), bf16[256,2]{1,0:T(8,128)(2,1)}) %reduce-scatter.39.cloned.1.call-update) | async-done | bytes 1040
  792.6 7.3 all-gather.21.cloned.1.call-done
  802.7 8.9 all-gather.19.cloned.1.call-done
  814.5 5.5 fusion.83
  821.5 19.5 %reduce-scatter.25.cloned.1.call-done = bf16[128,512]{1,0:T(8,128)(2,1)} async-done(((bf16[512,512]{1,0:T(8,128)(2,1)}), bf16[128,512]{1,0:T(8,128)(2,1)}) %reduce-scatter.25.cloned.1.call-update) | async-done | bytes 131088 | tf_op jit(solution)/shard_map/reduce_scatter | solution.py:311
  841.0 33.8 %reduce-scatter.23.cloned.1.call-done = bf16[128,1536]{1,0:T(8,128)(2,1)} async-done(((bf16[512,1536]{1,0:T(8,128)(2,1)}), bf16[128,1536]{1,0:T(8,128)(2,1)}) %reduce-scatter.23.cloned.1.call-update) | async-done | bytes 393232 | tf_op jit(solution)/shard_map/reduce_scatter | solution.py:308
  874.8 3.1 add_convert_fusion.1
  877.9 23.9 %reduce-scatter.35.cloned.1.call-done = bf16[128,7]{1,0:T(8,128)(2,1)} async-done(((bf16[512,7]{1,0:T(8,128)(2,1)}), bf16[128,7]{1,0:T(8,128)(2,1)}) %reduce-scatter.35.cloned.1.call-update) | async-done | bytes 1808
  902.7 16.1 %all-reduce.4 = (bf16[7,128]{1,0:T(8,128)(2,1)S(1)}, bf16[128,8]{0,1:T(8,128)(2,1)S(1)}) all-reduce(bf16[7,128]{1,0:T(8,128)(2,1)S(1)} %copy.146, bf16[128,8]{0,1:T(8,128)(2,1)S(1)} %copy.148), channel_id=1, replica_groups=mesh['dp'=4,'expert'=4,'context'=2] {'expert','context'}, use_global_device_ids=true, to_apply=%region_41.42 | all-reduce | flops 1920 | bytes 7680 | tf_op jit(solution)/shard_map/psum | solution.py:319
  919.9 40.6 %all-reduce.8.cloned.1.call-done = (bf16[128,1536]{1,0:T(8,128)(2,1)}, bf16[128,512]{1,0:T(8,128)(2,1)}) async-done(((bf16[128,1536]{1,0:T(8,128)(2,1)}, bf16[128,512]{1,0:T(8,128)(2,1)}), (bf16[128,1536]{1,0:T(8,128)(2,1)}, bf16[128,512]{1,0:T(8,128)(2,1)})) %all-reduce.8.cloned.1.call-update) | async-done | bytes 524304 | tf_op jit(solution)/shard_map/psum | solution.py:320
  (338 shorter events, 126.5 us)
Async XLA Ops:
  7.2 37.0 %all-gather.9.cloned.1.call-start = ((), (), s32[]{:S(2)}) async-start(), calls=%async_computation.14 | async-start | bytes 1966080 | tf_op jit(solution)/shard_map/all_gather | solution.py:84
  9.2 83.1 %all-gather.13.cloned.1.call-start = ((), (), s32[]{:S(2)}) async-start(), calls=%async_computation.16 | async-start | bytes 2727936 | tf_op jit(solution)/shard_map/all_gather | solution.py:97
  11.5 35.7 %copy-start.57 = (f32[888]{0:T(1024)}, f32[888]{0:T(1024)S(1)}, u32[]{:S(2)}) copy-start(f32[888]{0:T(1024)S(1)} %div.35) | copy-start | bytes 10660
  12.1 35.0 %copy-start.59 = (f32[888]{0:T(1024)}, f32[888]{0:T(1024)S(1)}, u32[]{:S(2)}) copy-start(f32[888]{0:T(1024)S(1)} %rsqrt.20) | copy-start | bytes 10660
  21.7 25.5 %copy-start.61 = (f32[1,512]{1,0:T(1,128)}, f32[1,512]{1,0:T(1,128)S(1)}, u32[]{:S(2)}) copy-start(f32[1,512]{1,0:T(1,128)S(1)} %get-tuple-element.51) | copy-start | bytes 6148
  21.7 25.5 %copy-start.65 = (f32[1,512]{1,0:T(1,128)}, f32[1,512]{1,0:T(1,128)S(1)}, u32[]{:S(2)}) copy-start(f32[1,512]{1,0:T(1,128)S(1)} %get-tuple-element.52) | copy-start | bytes 6148
  21.7 114.7 %copy-start.52 = (f32[1,512]{1,0:T(1,128)}, f32[1,512]{1,0:T(1,128)S(1)}, u32[]{:S(2)}) copy-start(f32[1,512]{1,0:T(1,128)S(1)} %get-tuple-element.46) | copy-start | bytes 6148
  21.7 114.7 %copy-start.63 = (f32[1,512]{1,0:T(1,128)}, f32[1,512]{1,0:T(1,128)S(1)}, u32[]{:S(2)}) copy-start(f32[1,512]{1,0:T(1,128)S(1)} %get-tuple-element.47) | copy-start | bytes 6148
  22.0 25.2 %copy-start.17 = (f32[888,512]{1,0:T(8,128)}, f32[888,512]{1,0:T(8,128)S(1)}, u32[]{:S(2)}) copy-start(f32[888,512]{1,0:T(8,128)S(1)} %fusion.50) | copy-start | bytes 5455876
  50.6 56.7 %all-gather.11.cloned.1.call-start = ((), (), s32[]{:S(2)}) async-start(), calls=%async_computation.15 | async-start | bytes 2727936 | tf_op jit(solution)/shard_map/all_gather | solution.py:100
  54.5 13.0 %copy-start.70 = (s32[1,1,888,2]{2,3,1,0:T(2,128)S(1)}, s32[1,1,888,2]{2,3,1,0:T(2,128)}, u32[]{:S(2)}) copy-start(s32[1,1,888,2]{2,3,1,0:T(2,128)} %param.15) | copy-start | bytes 21316
  54.5 13.2 %copy-start.75 = (s32[1,1,888]{2,1,0:T(1,128)S(1)}, s32[1,1,888]{2,1,0:T(1,128)}, u32[]{:S(2)}) copy-start(s32[1,1,888]{2,1,0:T(1,128)} %param.16) | copy-start | bytes 10660
  54.5 124.6 %all-gather.15.cloned.1.call-start = ((), (), s32[]{:S(2)}) async-start(), calls=%async_computation.17 | async-start | bytes 5242880 | tf_op jit(solution)/shard_map/all_gather | solution.py:135
  57.5 52.6 %copy-start.40 = (pred[3,592]{1,0:T(4,128)(4,1)}, pred[3,592]{1,0:T(4,128)(4,1)S(1)}, u32[]{:S(2)}) copy-start(pred[3,592]{1,0:T(4,128)(4,1)S(1)} %broadcast_compare_fusion) | copy-start | bytes 5332
  67.5 58.1 %copy-start.32 = (bf16[512,512]{1,0:T(8,128)(2,1)}, bf16[512,512]{1,0:T(8,128)(2,1)S(1)}, u32[]{:S(2)}) copy-start(bf16[512,512]{1,0:T(8,128)(2,1)S(1)} %all_gather.48) | copy-start | bytes 1572868
  67.7 18.9 %copy-start.5 = (s32[1,1,888,2]{3,2,1,0:T(8,128)}, s32[1,1,888,2]{3,2,1,0:T(8,128)S(1)}, u32[]{:S(2)}) copy-start(s32[1,1,888,2]{3,2,1,0:T(8,128)S(1)} %copy.106) | copy-start | bytes 21316
  87.4 40.7 %copy-start.72 = (s32[888]{0:T(1024)}, s32[888]{0:T(1024)S(1)}, u32[]{:S(2)}) copy-start(s32[888]{0:T(1024)S(1)} %get-tuple-element.27) | copy-start | bytes 10660
  87.4 48.9 %copy-start.71 = (s32[888]{0:T(1024)}, s32[888]{0:T(1024)S(1)}, u32[]{:S(2)}) copy-start(s32[888]{0:T(1024)S(1)} %get-tuple-element.26) | copy-start | bytes 10660
  100.6 6.7 copy-start
  107.3 11.8 %copy-start.37 = (f32[3,8,296]{2,1,0:T(8,128)}, f32[3,8,296]{2,1,0:T(8,128)S(1)}, u32[]{:S(2)}) copy-start(f32[3,8,296]{2,1,0:T(8,128)S(1)} %log_add_fusion) | copy-start | bytes 85252
  110.1 9.0 copy-start.21
  127.4 8.9 copy-start.2
  127.7 8.7 copy-start.42
  128.1 18.3 %copy-start.45 = (f32[888]{0:T(1024)}, f32[888]{0:T(1024)S(1)}, u32[]{:S(2)}) copy-start(f32[888]{0:T(1024)S(1)} %add_rsqrt_fusion.1) | copy-start | bytes 10660
  156.8 63.8 %all-to-all-start = ((bf16[4,2,333,512]{3,1,2,0:T(2,128)(2,1)}), bf16[4,2,333,512]{3,1,2,0:T(2,128)(2,1)S(1)}, u32[]{:S(2)}, u32[]{:S(2)}) async-start(bf16[4,2,333,512]{3,1,2,0:T(2,128)(2,1)} %copy.114), calls=%async_computation | async-start | bytes 5455872 | tf_op jit(solution)/shard_map/all_to_all | solution.py:140
  161.1 10.0 %copy-start.76 = (f32[2,128]{1,0:T(2,128)S(1)}, f32[2,128]{1,0:T(2,128)}, u32[]{:S(2)}) copy-start(f32[2,128]{1,0:T(2,128)} %param.24) | copy-start | bytes 3076
  161.1 116.6 %all-gather.17.cloned.1.call-start = ((), (), s32[]{:S(2)}) async-start(), calls=%async_computation.18 | async-start | bytes 5242880 | tf_op jit(solution)/shard_map/all_gather | solution.py:137
  171.0 106.6 %copy-start.67 = (f32[2,2048]{1,0:T(2,128)}, f32[2,2048]{1,0:T(2,128)S(1)}, u32[]{:S(2)}) copy-start(f32[2,2048]{1,0:T(2,128)S(1)} %convert_element_type.244) | copy-start | bytes 49156
  220.6 57.0 %copy-start.30 = (bf16[4,2,333,512]{3,1,2,0:T(2,128)(2,1)}, bf16[4,2,333,512]{3,1,2,0:T(2,128)(2,1)S(1)}, u32[]{:S(2)}) copy-start(bf16[4,2,333,512]{3,1,2,0:T(2,128)(2,1)S(1)} %all-to-all-done) | copy-start | bytes 8183812
  291.9 66.0 %all-to-all-start.1 = ((bf16[4,2,333,512]{3,1,2,0:T(2,128)(2,1)}), bf16[4,2,333,512]{3,1,2,0:T(2,128)(2,1)}, u32[]{:S(2)}, u32[]{:S(2)}) async-start(bf16[4,2,333,512]{3,1,2,0:T(2,128)(2,1)} %copy.116), calls=%async_computation.1 | async-start | bytes 5455872 | tf_op jit(solution)/shard_map/all_to_all | solution.py:151
  296.6 391.4 %reduce-scatter.29.cloned.1.call-start = ((), (), s32[]{:S(2)}) async-start(), calls=%async_computation.23 | async-start | bytes 4718592 | tf_op jit(solution)/shard_map/reduce_scatter | solution.py:196
  296.7 12.8 %copy-start.3 = (f32[888,512]{1,0:T(8,128)S(1)}, f32[888,512]{1,0:T(8,128)}, u32[]{:S(2)}) copy-start(f32[888,512]{1,0:T(8,128)} %copy-done.2) | copy-start | bytes 5455876
  296.7 12.8 %copy-start.43 = (f32[888]{0:T(1024)S(1)}, f32[888]{0:T(1024)}, u32[]{:S(2)}) copy-start(f32[888]{0:T(1024)} %copy-done.42) | copy-start | bytes 10660
  296.7 12.8 %copy-start.46 = (f32[888]{0:T(1024)S(1)}, f32[888]{0:T(1024)}, u32[]{:S(2)}) copy-start(f32[888]{0:T(1024)} %copy-done.45) | copy-start | bytes 10660
  296.8 12.8 %copy-start.53 = (f32[1,512]{1,0:T(1,128)S(1)}, f32[1,512]{1,0:T(1,128)}, u32[]{:S(2)}) copy-start(f32[1,512]{1,0:T(1,128)} %copy-done.52) | copy-start | bytes 6148
  296.8 12.8 %copy-start.64 = (f32[1,512]{1,0:T(1,128)S(1)}, f32[1,512]{1,0:T(1,128)}, u32[]{:S(2)}) copy-start(f32[1,512]{1,0:T(1,128)} %copy-done.63) | copy-start | bytes 6148
  309.5 19.0 %copy-start.50 = (bf16[512,8]{0,1:T(8,128)(2,1)}, bf16[512,8]{0,1:T(8,128)(2,1)S(1)}, u32[]{:S(2)}) copy-start(bf16[512,8]{0,1:T(8,128)(2,1)S(1)} %all_gather.49) | copy-start | bytes 24580
  467.9 12.1 %copy-start.13 = (bf16[4,2,333,512]{3,1,2,0:T(2,128)(2,1)}, bf16[4,2,333,512]{3,1,2,0:T(2,128)(2,1)S(1)}, u32[]{:S(2)}) copy-start(bf16[4,2,333,512]{3,1,2,0:T(2,128)(2,1)S(1)} %all_to_all.20) | copy-start | bytes 8183812
  519.4 66.3 %all-to-all-start.3 = ((bf16[4,2,333,512]{3,1,2,0:T(2,128)(2,1)}), bf16[4,2,333,512]{3,1,2,0:T(2,128)(2,1)}, u32[]{:S(2)}, u32[]{:S(2)}) async-start(bf16[4,2,333,512]{3,1,2,0:T(2,128)(2,1)} %copy.121), calls=%async_computation.3 | async-start | bytes 5455872 | tf_op jit(solution)/shard_map/all_to_all | solution.py:188
  524.2 164.6 %reduce-scatter.27.cloned.1.call-start = ((), (), s32[]{:S(2)}) async-start(), calls=%async_computation.21 | async-start | bytes 4718592 | tf_op jit(solution)/shard_map/reduce_scatter | solution.py:190
  537.2 163.8 %reduce-scatter.31.cloned.1.call-start = ((), (), s32[]{:S(2)}) async-start(), calls=%async_computation.25 | async-start | bytes 2727936
  603.8 7.7 copy-start.4
  603.8 7.7 copy-start.44
  603.8 7.7 copy-start.47
  603.8 7.7 copy-start.51
  603.8 7.7 copy-start.54
  623.1 16.7 %copy-start.25 = (bf16[3,296,8,64]{1,3,2,0:T(8,128)(2,1)}, bf16[3,296,8,64]{1,3,2,0:T(8,128)(2,1)S(1)}, u32[]{:S(2)}) copy-start(bf16[3,296,8,64]{1,3,2,0:T(8,128)(2,1)S(1)} %copy.126) | copy-start | bytes 2727940
  639.9 13.2 %copy-start.16 = (bf16[3,296,8,64]{1,3,2,0:T(8,128)(2,1)S(1)}, bf16[3,296,8,64]{1,3,2,0:T(8,128)(2,1)}, u32[]{:S(2)}) copy-start(bf16[3,296,8,64]{1,3,2,0:T(8,128)(2,1)} %copy.104) | copy-start | bytes 2727940
  663.5 44.0 %reduce-scatter.33.cloned.1.call-start = ((), (), s32[]{:S(2)}) async-start(), calls=%async_computation.26 | async-start | bytes 2727936
  680.8 38.8 %reduce-scatter.37.cloned.1.call-start = ((), (), s32[]{:S(2)}) async-start(), calls=%async_computation.28 | async-start | bytes 163840
  681.0 8.3 copy-start.8
  681.0 8.3 copy-start.28
  681.9 70.2 %reduce-scatter.41.cloned.1.call-start = ((), (), s32[]{:S(2)}) async-start(), calls=%async_computation.30 | async-start | bytes 147456
  686.8 102.3 %reduce-scatter.39.cloned.1.call-start = ((), (), s32[]{:S(2)}) async-start(), calls=%async_computation.29 | async-start | bytes 589824
  688.0 111.8 %all-gather.21.cloned.1.call-start = ((), (), s32[]{:S(2)}) async-start(), calls=%async_computation.24 | async-start | bytes 1572864 | tf_op jit(solution)/shard_map/all_gather | solution.py:210
  688.8 122.8 %all-gather.19.cloned.1.call-start = ((), (), s32[]{:S(2)}) async-start(), calls=%async_computation.22 | async-start | bytes 1572864 | tf_op jit(solution)/shard_map/all_gather | solution.py:204
  689.3 151.7 %reduce-scatter.25.cloned.1.call-start = ((), (), s32[]{:S(2)}) async-start(), calls=%async_computation.20 | async-start | bytes 655360 | tf_op jit(solution)/shard_map/reduce_scatter | solution.py:311
  690.9 183.9 %reduce-scatter.23.cloned.1.call-start = ((), (), s32[]{:S(2)}) async-start(), calls=%async_computation.19 | async-start | bytes 1966080 | tf_op jit(solution)/shard_map/reduce_scatter | solution.py:308
  710.6 8.8 copy-start.14
  719.5 182.3 %reduce-scatter.35.cloned.1.call-start = ((), (), s32[]{:S(2)}) async-start(), calls=%async_computation.27 | async-start | bytes 163840
  792.5 21.9 %copy-start.12 = (bf16[3,296,512]{2,1,0:T(8,128)(2,1)S(1)}, bf16[3,296,512]{2,1,0:T(8,128)(2,1)}, u32[]{:S(2)}) copy-start(bf16[3,296,512]{2,1,0:T(8,128)(2,1)} %param.13) | copy-start | bytes 2727940
  792.6 21.9 %copy-start.58 = (f32[888]{0:T(1024)S(1)}, f32[888]{0:T(1024)}, u32[]{:S(2)}) copy-start(f32[888]{0:T(1024)} %copy-done.57) | copy-start | bytes 10660
  792.6 21.9 %copy-start.60 = (f32[888]{0:T(1024)S(1)}, f32[888]{0:T(1024)}, u32[]{:S(2)}) copy-start(f32[888]{0:T(1024)} %copy-done.59) | copy-start | bytes 10660
  821.5 139.1 %all-reduce.8.cloned.1.call-start = ((), (), s32[]{:S(2)}) async-start(), calls=%async_computation.31 | async-start | bytes 1048576 | tf_op jit(solution)/shard_map/psum | solution.py:320
  (34 other events, 121.5 us)
Sparse Core Ops, SparseCore 0:
  10.4 33.6 all-gather.8
  50.8 10.1 all-gather.12
  63.1 12.1 all-gather.10
  76.9 54.5 all-gather.14
  164.0 53.1 all-gather.16
  480.1 49.5 reduce-scatter.28
  537.3 52.0 reduce-scatter.26
  663.6 7.3 reduce-scatter.30
  680.9 6.3 reduce-scatter.32
  690.4 24.9 reduce-scatter.36
  718.7 33.3 reduce-scatter.40
  755.0 34.1 reduce-scatter.38
  790.8 9.0 all-gather.20
  801.3 10.1 all-gather.18
  815.0 25.9 reduce-scatter.24
  843.8 30.9 reduce-scatter.22
  878.0 23.8 reduce-scatter.34
  904.2 56.2 all-reduce.7
where the time goes:
time: 977 us; the launch traced here: 971 us
  waiting for transfers between devices  342 us (35%)
  matrix products  200 us (20%)
  local copies, waits for them, and re-layouts  170 us (17%)
  blocking collectives  126 us (13%)
  other arithmetic  104 us (11%)
  between operations  15.9 us (2%)
  starting transfers between devices  14.8 us (2%)
    unnamed x24, waiting for transfers between devices  90.9 us
    all_to_all x1, blocking collectives, shards(): lax.all_to_all(grad_send, 'expert', split_axis=0, concat_axis=0, tiled=True)  63.9 us
    dot_general x1, matrix products, shards(): jnp.einsum('sjcd,jdf->sjcf', received, in_w, preferred_element_type=jnp.f...  57 us
    all_to_all x1, waiting for transfers between devices, shards(): lax.all_to_all(grad_received, 'expert', split_axis=0, concat_axis=0, tile...  48.4 us
    all_to_all x1, waiting for transfers between devices, shards(): lax.all_to_all(send_rows, 'expert', split_axis=0, concat_axis=0, tiled=True)  41.5 us
    psum x1, waiting for transfers between devices, shards(): lax.psum(part_qkv.astype(jnp.bfloat16), ('expert', 'context'))  40.6 us
    unnamed x171, local copies, waits for them, and re-layouts  36.9 us
    reduce_scatter x1, waiting for transfers between devices, shards(): lax.psum_scatter(grad_qkv.astype(jnp.bfloat16), 'dp', scatter_dimension=0...  33.8 us
  transfers between devices with their start and end apart: 21, of which 12 were waited for; matrix products, arithmetic and copies ran while one was open for 39% of the time, Pallas kernels for 0%

commit v1 on v0

v1 whole, which is shorter than its diff:
```python
from functools import partial

import jax
import jax.numpy as jnp
from jax import lax
from jax.experimental import pallas as pl
from jax.experimental.pallas import tpu as pltpu
from jax.sharding import PartitionSpec as P

HEADS = 8
EPSILON = 1e-06
LANES = 128
BF = jnp.bfloat16
F32 = jnp.float32
I32 = jnp.int32
MIB = 1 << 20


def up(size, unit):
    return -(-size // unit) * unit


def nn(a, b):
    return jnp.dot(a, b, preferred_element_type=F32)


def nt(a, b):
    return lax.dot_general(a, b, (((1,), (1,)), ((), ())), preferred_element_type=F32)


def tn(a, b):
    return lax.dot_general(a, b, (((0,), (0,)), ((), ())), preferred_element_type=F32)


def iota(shape, dim):
    return lax.broadcasted_iota(I32, shape, dim)


def call(body, name, grid, ins, outs, scratch=(), flops=0, moved=0, vmem=56, aliases=None):
    in_specs = [pl.BlockSpec(*spec) if spec else pl.BlockSpec(memory_space=pltpu.VMEM) for spec in ins]
    out_specs = [pl.BlockSpec(*spec) if spec else pl.BlockSpec(memory_space=pltpu.VMEM) for spec, _ in outs]
    return pl.pallas_call(
        body,
        name=name,
        grid=grid,
        in_specs=in_specs,
        out_specs=out_specs,
        out_shape=[jax.ShapeDtypeStruct(*shape) for _, shape in outs],
        scratch_shapes=list(scratch),
        input_output_aliases=aliases or {},
        cost_estimate=pl.CostEstimate(flops=int(flops), bytes_accessed=int(moved), transcendentals=0),
        compiler_params=pltpu.CompilerParams(vmem_limit_bytes=vmem * MIB),
    )


def normed(values):
    average = jnp.mean(values, axis=-1, keepdims=True)
    centred = values - average
    inv_scale = lax.rsqrt(jnp.mean(centred * centred, axis=-1, keepdims=True) + EPSILON)
    return centred * inv_scale, inv_scale


def norm_backward(grad, unit, inv_scale, gain):
    scaled = grad * gain
    centre = jnp.mean(scaled, axis=-1, keepdims=True)
    along = jnp.mean(scaled * unit, axis=-1, keepdims=True)
    return inv_scale * (scaled - centre - unit * along)


def split3(value):
    high = value.astype(BF).astype(F32)
    rest = value - high
    mid = rest.astype(BF).astype(F32)
    return high, mid, rest - mid


def pick(slots, first, rows):
    own = iota((rows, slots.shape[1]), 0) + first
    hit = (own == slots[0:1, :]) | (own == slots[1:2, :])
    return jnp.where(hit, 1.0, 0.0).astype(BF)


def plan_kernel(experts, cap, cap_pad, routes, key_col, key_row, grad, slots, send):
    expert = pl.program_id(0)

    @pl.when(expert == 0)
    def _():
        ids = iota((experts, routes.shape[1]), 0)
        before = jnp.where(key_col[...] < key_row[...], 1.0, 0.0).astype(BF)
        first = jnp.where(routes[0:1, :] == ids, 1.0, 0.0)
        second = jnp.where(routes[1:2, :] == ids, 1.0, 0.0)
        count = jnp.sum(first, axis=1, keepdims=True)
        rank_first = jnp.sum(nn(first.astype(BF), before) * first, axis=0, keepdims=True)
        rank_second = jnp.sum((nn(second.astype(BF), before) + count) * second, axis=0, keepdims=True)
        ranks = jnp.concatenate([rank_first, rank_second], axis=0).astype(I32)
        owned = jnp.where(ranks < cap, routes[...] * cap_pad + ranks, -1)
        slots[...] = jnp.concatenate([owned, jnp.full((6, owned.shape[1]), -1, I32)], axis=0)

    one_hot = pick(slots[...], expert * cap_pad, cap_pad)
    send[0] = nn(one_hot, grad[...]).astype(BF)


def dispatch_kernel(experts, cap, cap_pad, acts, router, routes, slots, send, gates):
    expert = pl.program_id(0)
    tokens, width = acts.shape
    lanes = up(cap_pad, LANES)

    @pl.when(expert == 0)
    def _():
        logits = nt(router[...], acts[...])
        logits = jnp.exp(logits - jnp.max(logits, axis=0, keepdims=True))
        probs = logits / jnp.sum(logits, axis=0, keepdims=True)
        ids = iota((experts, tokens), 0)
        for choice in range(2):
            gate = jnp.sum(jnp.where(routes[choice : choice + 1, :] == ids, probs, 0.0), axis=0, keepdims=True)
            high, mid, low = split3(gate)
            gates[choice] = jnp.concatenate([high, mid, low, jnp.zeros((5, tokens), F32)], axis=0)

    own = iota((lanes, tokens), 0) + expert * cap_pad
    hit_first = own == slots[0:1, :]
    hit_second = own == slots[1:2, :]
    one_first = jnp.where(hit_first, 1.0, 0.0).astype(BF)
    one_second = jnp.where(hit_second, 1.0, 0.0).astype(BF)
    rows = nn((one_first + one_second)[:cap_pad], acts[...])
    gate = nt(gates[0].astype(BF), one_first) + nt(gates[1].astype(BF), one_second)
    gate = jnp.concatenate([gate, jnp.zeros((8, width - lanes), F32)], axis=1)
    at = iota((cap_pad, 1), 0) - cap
    for part in range(3):
        rows = jnp.where(at == part, gate[part : part + 1, :], rows)
    send[0] = rows.astype(BF)


def gelu_parts(z):
    share = 0.5 * (1.0 + lax.erf(z * 0.7071067811865476))
    slope = share + z * (0.3989422804014327 * jnp.exp(-0.5 * z * z))
    return z * share, slope


def expert_kernel(
    cap, chunk, got, got_grad, w_in, b_in, w_back, b_back,
    out_rows, out_back, grad_in, grad_b_in, grad_back, grad_b_back,
    acts, hidden, slope, delta, grad_pre,
):
    groups, cap_pad, width = got.shape
    ff = w_in.shape[1]
    lanes = up(cap_pad, LANES)
    at = iota((cap_pad, 1), 0)
    same = at == iota((1, lanes), 1)
    for src in range(groups):
        rows = pl.ds(src * cap_pad, cap_pad)
        block = got[src]
        acts[rows, :] = jnp.where(at < cap, block.astype(F32), 0.0).astype(BF)
        wide = block.astype(F32)
        gate = wide[cap : cap + 1, :lanes] + wide[cap + 1 : cap + 2, :lanes] + wide[cap + 2 : cap + 3, :lanes]
        gate = jnp.sum(jnp.where(same, gate, 0.0), axis=1, keepdims=True)
        delta[rows, :] = (gate * got_grad[src].astype(F32)).astype(BF)
        for lo in range(0, ff, chunk):
            cols = pl.ds(lo, chunk)
            z = nn(acts[rows, :], w_in[:, cols]) + b_in[:, cols]
            value, rise = gelu_parts(z)
            hidden[rows, cols] = value.astype(BF)
            slope[rows, cols] = rise.astype(BF)
        made = (nn(hidden[rows, :], w_back[...]) + b_back[...]).astype(BF).astype(F32)
        out_rows[src] = (gate * made).astype(BF)
        dot = jnp.sum(made * got_grad[src].astype(F32), axis=1, keepdims=True)
        dot = jnp.sum(jnp.where(same, dot, 0.0), axis=0, keepdims=True)
        parts = split3(jnp.concatenate([dot, jnp.zeros((1, width - lanes), F32)], axis=1))
        for lo in range(0, ff, chunk):
            cols = pl.ds(lo, chunk)
            dz = nt(delta[rows, :], w_back[cols, :]) * slope[rows, cols].astype(F32)
            total = jnp.sum(dz, axis=0, keepdims=True)
            grad_b_in[:, cols] = total if src == 0 else grad_b_in[:, cols] + total
            grad_pre[rows, cols] = dz.astype(BF)
        back = nt(grad_pre[rows, :], w_in[...])
        for part in range(3):
            back = jnp.where(at == cap + part, parts[part], back)
        out_back[src] = back.astype(BF)
    grad_b_back[...] = jnp.sum(delta[...].astype(F32), axis=0, keepdims=True)
    for lo in range(0, ff, chunk):
        cols = pl.ds(lo, chunk)
        grad_back[cols, :] = tn(hidden[:, cols], delta[...]).astype(BF)
        grad_in[:, cols] = tn(acts[...], grad_pre[:, cols]).astype(BF)


def forward_kernel(half, x_own, x_other, bias, vec, w_qkv, w_out, q_ref, k_ref, v_ref, p_ref, o_ref, h_ref, a_ref):
    width = x_own.shape[1]
    half_pad = up(half, 16)
    head_dim = width // HEADS
    scale = head_dim ** (-0.5)
    gain, offset, bias_q, bias_v = (vec[row : row + 1, :] for row in range(4))
    own = x_own[...].astype(F32)
    unit, _ = normed(own)
    acts = (unit * gain + offset).astype(BF)
    unit, _ = normed(x_other[...].astype(F32))
    other = (unit * gain + offset).astype(BF)
    q_ref[...] = ((nn(acts, w_qkv[:, :width]) + bias_q).astype(BF).astype(F32) * scale).astype(BF)
    pad = jnp.zeros((half_pad - half, width), BF)
    for part, rows in enumerate((acts, other)):
        start = part * half_pad
        k_ref[0, pl.ds(start, half), :] = nn(rows, w_qkv[:, width : 2 * width]).astype(BF)
        v_ref[0, pl.ds(start, half), :] = (nn(rows, w_qkv[:, 2 * width :]) + bias_v).astype(BF)
        if half_pad > half:
            k_ref[0, pl.ds(start + half, half_pad - half), :] = pad
            v_ref[0, pl.ds(start + half, half_pad - half), :] = pad
    low = iota((1, LANES), 1) < head_dim
    zero = jnp.zeros((), BF)
    for pair in range(width // LANES):
        cols = pl.ds(pair * LANES, LANES)
        q_pair, k_pair, v_pair = q_ref[:, cols], k_ref[0, :, cols], v_ref[0, :, cols]
        mixed = []
        for sub in range(2):
            mask = low if sub == 0 else jnp.logical_not(low)
            scores = nt(jnp.where(mask, q_pair, zero), k_pair) + bias[0]
            raised = jnp.exp(scores - jnp.max(scores, axis=1, keepdims=True))
            probs = (raised * (1.0 / jnp.sum(raised, axis=1, keepdims=True))).astype(BF)
            p_ref[0, 2 * pair + sub] = probs
            mixed.append(nn(probs, v_pair))
        o_ref[:, cols] = jnp.where(low, mixed[0], mixed[1]).astype(BF)
    after = own + nn(o_ref[...], w_out[...]) + vec[4:5, :]
    h_ref[...] = after
    unit, _ = normed(after)
    a_ref[...] = (unit * vec[5:6, :] + vec[6:7, :]).astype(BF)


def backward_kernel(
    experts, cap, cap_pad, grad, table, slots, h_ref, o_ref, a_ref, router, vec, w_out, q_ref, k_ref, v_ref, p_ref,
    dh_ref, dq_ref, dk_ref, dv_ref, g_out, g_router, g_vec, hits,
):
    image = pl.program_id(0)
    half, width = grad.shape
    head_dim = width // HEADS
    half_pad = up(half, 16)
    lanes = up(cap_pad, LANES)
    lane = iota((1, LANES), 1)
    acts = a_ref[...]
    logits = jnp.where(lane < experts, nn(acts, router[...]), -1e30)
    logits = jnp.exp(logits - jnp.max(logits, axis=1, keepdims=True))
    probs = logits / jnp.sum(logits, axis=1, keepdims=True)
    grad_probs = jnp.zeros((half, LANES), F32)
    first, second = slots[:, 0:1], slots[:, 1:2]
    back = jnp.zeros((half, width), F32)
    for expert in range(experts):
        own = iota((half, lanes), 1)
        own = jnp.where(own < cap_pad, own + expert * cap_pad, -2)
        hit = (own == first) | (own == second)
        one_hot = jnp.where(hit, 1.0, 0.0)
        start = expert * cap_pad
        tail = table[pl.ds(start + cap_pad - 16, 16), :].astype(F32)
        at = cap - (cap_pad - 16)
        dots = tail[at : at + 1, :lanes] + tail[at + 1 : at + 2, :lanes] + tail[at + 2 : at + 3, :lanes]
        dots = jnp.sum(jnp.where(hit, dots, 0.0), axis=1, keepdims=True)
        grad_probs = jnp.where(lane == expert, dots, grad_probs)
        back = back + nn(one_hot[:, :cap_pad].astype(BF), table[pl.ds(start, cap_pad), :])
    inner = jnp.sum(probs * grad_probs, axis=1, keepdims=True)
    grad_logits = (probs * (grad_probs - inner)).astype(BF)
    part_router = tn(acts, grad_logits)
    back = back + nt(grad_logits, router[...])
    unit, inv_scale = normed(h_ref[...])
    out_grad = grad[...].astype(F32)
    dh = out_grad + norm_backward(back, unit, inv_scale, vec[5:6, :])
    dh_ref[...] = dh
    dh_low = dh.astype(BF)
    part_out = tn(o_ref[...], dh_low)
    rows = [
        jnp.sum(dh, axis=0, keepdims=True),
        jnp.sum(back * unit, axis=0, keepdims=True),
        jnp.sum(back, axis=0, keepdims=True),
    ]
    part_vec = jnp.concatenate(rows + [jnp.zeros((5, width), F32)], axis=0)

    @pl.when(image == 0)
    def _():
        g_out[...] = part_out
        g_router[...] = part_router
        g_vec[...] = part_vec

    @pl.when(image > 0)
    def _():
        g_out[...] += part_out
        g_router[...] += part_router
        g_vec[...] += part_vec

    do = nt(dh_low, w_out[...]).astype(BF)
    low = lane < head_dim
    zero = jnp.zeros((), BF)
    scale = head_dim ** (-0.5)
    for pair in range(width // LANES):
        cols = slice(pair * LANES, (pair + 1) * LANES)
        do_pair = do[:, cols]
        q_pair, k_pair, v_pair = q_ref[:, cols], k_ref[0, :, cols], v_ref[0, :, cols]
        dq, dk, dv = [], [], []
        for sub in range(2):
            mask = low if sub == 0 else jnp.logical_not(low)
            p_low = p_ref[0, 2 * pair + sub]
            p = p_low.astype(F32)
            dp = nt(jnp.where(mask, do_pair, zero), v_pair)
            inner = jnp.sum(p * dp, axis=1, keepdims=True)
            ds = (p * (dp - inner)).astype(BF)
            dv.append(tn(p_low, do_pair))
            dk.append(tn(ds, q_pair))
            dq.append(nn(ds, k_pair))
        dq_ref[:, cols] = (jnp.where(low, dq[0], dq[1]) * scale).astype(BF)
        dk_pair = jnp.where(low, dk[0], dk[1]).astype(BF)
        dv_pair = jnp.where(low, dv[0], dv[1]).astype(BF)
        for part in range(2):
            dk_ref[part, :, cols] = dk_pair[part * half_pad : part * half_pad + half]
            dv_ref[part, :, cols] = dv_pair[part * half_pad : part * half_pad + half]


def input_kernel(x_ref, dh_ref, dq_ref, dk_own, dk_got, dv_own, dv_got, vec, w_qkv, dx_ref, g_qkv, g_vec):
    image = pl.program_id(0)
    width = x_ref.shape[1]
    unit, inv_scale = normed(x_ref[...].astype(F32))
    acts = (unit * vec[0:1, :] + vec[1:2, :]).astype(BF)
    dq = dq_ref[...]
    dk = (dk_own[0].astype(F32) + dk_got[...].astype(F32)).astype(BF)
    dv = (dv_own[0].astype(F32) + dv_got[...].astype(F32)).astype(BF)
    da = jnp.zeros(unit.shape, F32)
    parts = []
    for at, piece in enumerate((dq, dk, dv)):
        parts.append(tn(acts, piece))
        da = da + nt(piece, w_qkv[:, at * width : (at + 1) * width])
    dx_ref[...] = (dh_ref[...] + norm_backward(da, unit, inv_scale, vec[0:1, :])).astype(BF)
    rows = [
        jnp.sum(da * unit, axis=0, keepdims=True),
        jnp.sum(da, axis=0, keepdims=True),
        jnp.sum(dq.astype(F32), axis=0, keepdims=True),
        jnp.sum(dv.astype(F32), axis=0, keepdims=True),
    ]
    part_vec = jnp.concatenate(rows + [jnp.zeros((4, width), F32)], axis=0)

    @pl.when(image == 0)
    def _():
        g_vec[...] = part_vec
        for at in range(3):
            g_qkv[:, at * width : (at + 1) * width] = parts[at]

    @pl.when(image > 0)
    def _():
        g_vec[...] += part_vec
        for at in range(3):
            g_qkv[:, at * width : (at + 1) * width] += parts[at]


def combine_kernel(slots, table, h_ref, out_ref):
    half = slots.shape[0]
    total = table.shape[0]
    own = iota((half, total), 1)
    hit = (own == slots[:, 0:1]) | (own == slots[:, 1:2])
    out_ref[...] = (h_ref[...] + nn(jnp.where(hit, 1.0, 0.0).astype(BF), table[...])).astype(BF)


def shards(
    inputs, key_mask, routes, priority, vectors, w_qkv, w_out, w_router, w_in, b_in, w_back, b_back, cotangent
):
    images, half, width = inputs.shape
    tokens = images * half
    groups = lax.axis_size("expert")
    dps = lax.axis_size("dp")
    per_device = w_in.shape[0]
    experts = groups * per_device
    ff = w_in.shape[2]
    cap = max(2, 3 * tokens // experts)
    cap_pad = up(cap + 3, 16)
    half_pad = up(half, 16)
    total = experts * cap_pad
    context = lax.axis_index("context")
    swap = [(0, 1), (1, 0)]

    x = inputs.reshape(tokens, width)
    grad = cotangent.reshape(tokens, width)
    x_other = lax.ppermute(x, "context", swap)

    dense = jnp.concatenate([w_qkv, w_out, w_router, vectors.T], axis=1).astype(BF)
    dense = lax.all_gather(dense, "dp", axis=0, tiled=True)
    qkv_all, out_all = dense[:, : 3 * width], dense[:, 3 * width : 4 * width]
    router_all = dense[:, 4 * width : 4 * width + experts]
    vec = dense[:, 4 * width + experts :].astype(F32).T
    vec = jnp.concatenate([vec, jnp.zeros((1, width), F32)], axis=0)
    router_pad = jnp.concatenate([router_all, jnp.zeros((width, LANES - experts), BF)], axis=1)

    in_w = lax.all_gather(w_in.astype(BF), "dp", axis=1, tiled=True)
    back_w = lax.all_gather(w_back.astype(BF), "dp", axis=1, tiled=True)
    in_b = lax.all_gather(b_in.astype(BF), "dp", axis=1, tiled=True).astype(F32)
    back_b = lax.all_gather(b_back.astype(BF), "dp", axis=1, tiled=True).astype(F32)

    route_rows = routes.reshape(tokens, 2).T
    keys = priority.reshape(tokens) * tokens + jnp.arange(tokens, dtype=I32)
    block = ((1, cap_pad, width), lambda e: (e, 0, 0))
    slots, send_grad = call(
        partial(plan_kernel, experts, cap, cap_pad),
        "plan",
        (experts,),
        [None] * 4,
        [(((8, tokens), lambda e: (0, 0)), ((8, tokens), I32)), (block, ((experts, cap_pad, width), BF))],
        flops=2 * total * tokens * width,
        moved=4 * total * width,
    )(route_rows, keys[:, None], keys[None, :], grad)
    slot_cols = slots.T

    def exchange(rows):
        return lax.all_to_all(rows, "expert", split_axis=0, concat_axis=0, tiled=True)

    def by_expert(rows, which):
        return rows.reshape(groups, per_device, cap_pad, width)[:, which]

    got_grad = [exchange(by_expert(send_grad, which)) for which in range(per_device)]

    mask = jnp.where(key_mask > 0, 0.0, -1e30).astype(F32)
    first, second = mask[:, :half], mask[:, half:]
    own = jnp.where(context == 0, first, second)
    other = jnp.where(context == 0, second, first)
    off = jnp.full((images, half_pad - half), -1e30, F32)
    bias = jnp.concatenate([own, off, other, off], axis=1)[:, None, :]
    keys_pad = 2 * half_pad
    row = ((half, width), lambda i: (i, 0))
    cube = ((1, keys_pad, width), lambda i: (i, 0, 0))
    prob = ((1, HEADS, half, keys_pad), lambda i: (i, 0, 0, 0))
    q, k, v, p, o, after, acts = call(
        partial(forward_kernel, half),
        "forward",
        (images,),
        [row, row, ((1, 1, keys_pad), lambda i: (i, 0, 0)), None, None, None],
        [
            (row, ((tokens, width), BF)),
            (cube, ((images, keys_pad, width), BF)),
            (cube, ((images, keys_pad, width), BF)),
            (prob, ((images, HEADS, half, keys_pad), BF)),
            (row, ((tokens, width), BF)),
            (row, ((tokens, width), F32)),
            (row, ((tokens, width), BF)),
        ],
        flops=2 * tokens * width * (6 * width + 4 * keys_pad),
        moved=20 * tokens * width,
    )(x, x_other, bias, vec, qkv_all, out_all)

    (send_rows,) = call(
        partial(dispatch_kernel, experts, cap, cap_pad),
        "dispatch",
        (experts,),
        [None] * 4,
        [(block, ((experts, cap_pad, width), BF))],
        scratch=[pltpu.VMEM((2, 8, tokens), F32)],
        flops=2 * total * tokens * width,
        moved=4 * total * width,
    )(acts, router_all.T, route_rows, slots)
    got = [exchange(by_expert(send_rows, which)) for which in range(per_device)]

    out_rows, back_rows, g_in, g_b_in, g_back, g_b_back = [], [], [], [], [], []
    slab = (groups, cap_pad, width)
    rows_all = groups * cap_pad
    for which in range(per_device):
        made = call(
            partial(expert_kernel, cap, 512),
            "expert",
            (),
            [None] * 6,
            [
                (None, (slab, BF)),
                (None, (slab, BF)),
                (None, ((width, ff), BF)),
                (None, ((1, ff), F32)),
                (None, ((ff, width), BF)),
                (None, ((1, width), F32)),
            ],
            scratch=[
                pltpu.VMEM((rows_all, width), BF),
                pltpu.VMEM((rows_all, ff), BF),
                pltpu.VMEM((rows_all, ff), BF),
                pltpu.VMEM((rows_all, width), BF),
                pltpu.VMEM((rows_all, ff), BF),
            ],
            flops=12 * rows_all * width * ff,
            moved=8 * rows_all * width + 8 * width * ff,
        )(
            got[which], got_grad[which], in_w[which], in_b[which][None], back_w[which], back_b[which][None]
        )
        for kept, piece in zip((out_rows, back_rows, g_in, g_b_in, g_back, g_b_back), made):
            kept.append(piece)

    def returned(parts):
        moved = [exchange(part) for part in parts]
        return jnp.stack(moved, axis=1).reshape(total, width)

    back_table = returned(back_rows)
    out_table = returned(out_rows)

    def expert_sum(parts):
        share = lax.psum_scatter(jnp.stack(parts), ("dp", "context"), scatter_dimension=1, tiled=True)
        return lax.all_gather(share, "context", axis=1, tiled=True).astype(F32)

    grad_w_in = expert_sum(g_in)
    grad_w_back = expert_sum(g_back)

    halves = ((2, half, width), lambda i: (0, i, 0))
    fixed = lambda i: (0, 0)
    dh, dq, dk, dv, g_out, g_router, g_vec_two = call(
        partial(backward_kernel, experts, cap, cap_pad),
        "backward",
        (images,),
        [row, None, ((half, 8), lambda i: (i, 0)), row, row, row, None, None, None, row, cube, cube, prob],
        [
            (row, ((tokens, width), F32)),
            (row, ((tokens, width), BF)),
            (halves, ((2, tokens, width), BF)),
            (halves, ((2, tokens, width), BF)),
            (((width, width), fixed), ((width, width), F32)),
            (((width, LANES), fixed), ((width, LANES), F32)),
            (((8, width), fixed), ((8, width), F32)),
        ],
        scratch=[pltpu.VMEM((8, LANES), F32)],
        flops=2 * tokens * width * (total + 2 * width + 8 * keys_pad),
        moved=30 * tokens * width,
    )(grad, back_table, slot_cols, after, o, acts, router_pad, vec, out_all, q, k, v, p)

    dk_got = lax.ppermute(dk[1], "context", swap)
    dv_got = lax.ppermute(dv[1], "context", swap)
    own_half = ((1, half, width), lambda i: (0, i, 0))
    dx, g_qkv, g_vec_one = call(
        input_kernel,
        "input",
        (images,),
        [row, row, row, own_half, row, own_half, row, None, None],
        [
            (row, ((tokens, width), BF)),
            (((width, 3 * width), fixed), ((width, 3 * width), F32)),
            (((8, width), fixed), ((8, width), F32)),
        ],
        flops=12 * tokens * width * width,
        moved=20 * tokens * width,
    )(x, dh, dq, dk, dk_got, dv, dv_got, vec, qkv_all)

    (output,) = call(
        combine_kernel,
        "combine",
        (images,),
        [((half, 8), lambda i: (i, 0)), None, row],
        [(row, ((tokens, width), BF))],
        flops=2 * tokens * width * total,
        moved=10 * tokens * width,
    )(slot_cols, out_table, after)

    mine = (jnp.arange(groups) == lax.axis_index("expert")).astype(F32)
    wide_b = jnp.concatenate(g_b_in, axis=0).reshape(per_device, dps, ff // dps)
    wide_b = wide_b.transpose(1, 0, 2).reshape(width, -1)
    b_cols = wide_b.shape[1]
    wide_b = (mine[None, :, None] * wide_b[:, None, :]).reshape(width, groups * b_cols)
    slim_b = jnp.concatenate(g_b_back, axis=0).T
    slim_b = (mine[None, :, None] * slim_b[:, None, :]).reshape(width, experts)
    vec_cols = jnp.concatenate([g_vec_one[:4], g_vec_two[:3]], axis=0).T
    pack = jnp.concatenate([g_qkv, g_out, g_router[:, :experts], vec_cols, wide_b, slim_b], axis=1).astype(BF)
    pack = lax.psum_scatter(pack, "dp", scatter_dimension=0, tiled=True)
    pack = lax.psum(pack, ("expert", "context")).astype(F32)
    cuts = [3 * width, width, experts, 7, groups * b_cols, experts]
    pieces, at = [], 0
    for size in cuts:
        pieces.append(pack[:, at : at + size])
        at += size
    grad_qkv, grad_out, grad_router, grad_vec, wide_b, slim_b = pieces
    group = lax.axis_index("expert")
    wide_b = lax.dynamic_slice_in_dim(wide_b, group * b_cols, b_cols, axis=1)
    grad_b_in = wide_b.reshape(per_device, ff // dps)
    slim_b = lax.dynamic_slice_in_dim(slim_b, group * per_device, per_device, axis=1)
    return (
        output.reshape(images, half, width),
        dx.reshape(images, half, width),
        grad_vec.T,
        grad_qkv,
        grad_out,
        grad_router,
        grad_w_in,
        grad_b_in,
        grad_w_back,
        slim_b.T,
    )


def solution(mesh):
    tokens = P(("dp", "expert"), "context", None)
    by_rows = P("dp", None)
    experts = P("expert", "dp", None)
    expert_bias = P("expert", "dp")
    return jax.shard_map(
        shards,
        mesh=mesh,
        in_specs=(
            tokens,
            P(("dp", "expert"), None),
            P(("dp", "expert"), "context", None, None),
            tokens,
            P(None, "dp"),
            by_rows,
            by_rows,
            by_rows,
            experts,
            expert_bias,
            experts,
            expert_bias,
            tokens,
        ),
        out_specs=(
            tokens,
            tokens,
            P(None, "dp"),
            by_rows,
            by_rows,
            by_rows,
            experts,
            expert_bias,
            experts,
            expert_bias,
        ),
        check_vma=False,
    )
```

time: 977 us -> 493 us (0.50)
  matrix products: 200 us -> 0 us
  Pallas kernels: 0 us -> 136 us
  waiting for transfers between devices: 342 us -> 209 us
  local copies, waits for them, and re-layouts: 170 us -> 49.9 us
  blocking collectives: 126 us -> 16 us
  other arithmetic: 104 us -> 25.3 us
  starting transfers between devices: 14.8 us -> 34.7 us
    dot_general x21 -> x0, matrix products: 200 us -> none  [the longest x1 57 us: shards(): jnp.einsum('sjcd,jdf->sjcf', received, in_w, preferred_element_type=jnp.f...]
    pallas_call x0 -> x8, Pallas kernels: none -> 136 us  [the longest x2 50.2 us: shards(): call(partial(expert_kernel, cap, 512), 'expert', (), [None] * 6, [(None,...]
    unnamed x24 -> x9, waiting for transfers between devices: 90.9 us -> 2.09 us
    all_to_all x1 -> x0, blocking collectives: 63.9 us -> none  [shards(): lax.all_to_all(grad_send, 'expert', split_axis=0, concat_axis=0, tiled=True)]
    reduce_scatter x4 -> x3, waiting for transfers between devices: 53.3 us -> 0.05 us  [the longest x2 0.03 us: expert_sum(): lax.psum_scatter(jnp.stack(parts), ('dp', 'context'), scatter_dimension=1...]
    all_to_all x3 -> x8, waiting for transfers between devices: 119 us -> 165 us  [exchange(): lax.all_to_all(rows, 'expert', split_axis=0, concat_axis=0, tiled=True)]
    gather x7 -> x0, local copies, waits for them, and re-layouts: 35.3 us -> none  [the longest x3 18.7 us: shards(): gate_values = jnp.take_along_axis(router_probs, route_rows, axis=1)]
    unnamed x171 -> x45, local copies, waits for them, and re-layouts: 36.9 us -> 3.51 us
  transfers between devices with their start and end apart: 21 -> 20, of which waited for: 12 -> 9; matrix products, arithmetic and copies ran while one was open for 39% -> 12% of each run, Pallas kernels for 0% -> 23%
where the time goes in v1:
time: 493 us; the launch traced here: 485 us
  waiting for transfers between devices  209 us (42%)
  Pallas kernels  136 us (28%)
  local copies, waits for them, and re-layouts  49.9 us (10%)
  starting transfers between devices  34.7 us (7%)
  other arithmetic  25.3 us (5%)
  blocking collectives  16 us (3%)
  between operations  14.8 us (3%)
    all_to_all x8, waiting for transfers between devices, exchange(): lax.all_to_all(rows, 'expert', split_axis=0, concat_axis=0, tiled=True)  165 us
    pallas_call x2, Pallas kernels, shards(): call(partial(expert_kernel, cap, 512), 'expert', (), [None] * 6, [(None,...  50.2 us
    pallas_call x1, Pallas kernels, shards(): call(partial(backward_kernel, experts, cap, cap_pad), 'backward', (images...  33.9 us
    all_to_all x8, starting transfers between devices, exchange(): lax.all_to_all(rows, 'expert', split_axis=0, concat_axis=0, tiled=True)  33.8 us
    psum x1, waiting for transfers between devices, shards(): pack = lax.psum(pack, ('expert', 'context')).astype(F32)  28.7 us
    pallas_call x1, Pallas kernels, shards(): call(partial(forward_kernel, half), 'forward', (images,), [row, row, ((1,...  16.9 us
    all_gather x1, waiting for transfers between devices, shards(): back_w = lax.all_gather(w_back.astype(BF), 'dp', axis=1, tiled=True)  12.2 us
    pallas_call x1, Pallas kernels, shards(): call(input_kernel, 'input', (images,), [row, row, row, own_half, row, own...  11.3 us
  transfers between devices with their start and end apart: 20, of which 9 were waited for; matrix products, arithmetic and copies ran while one was open for 12% of the time, Pallas kernels for 23%

profile of v1, /device:TPU:0, one launch (start us, length us, event | category | flops | bytes accessed | tf_op | source)
XLA Modules:
  0.0 484.9 jit_solution(17958352545830367079)
XLA Ops:
  7.2 1.3 convert.42
  8.5 1.0 convert.43
  9.5 0.7 convert.44
  10.3 0.7 convert.45
  11.2 0.9 concatenate.30
  12.2 1.1 convert_element_type.37
  14.2 0.8 iota_add_fusion.key_col
  15.0 7.7 %plan.1 = (s32[8,888]{1,0:T(8,128)}, bf16[8,336,512]{2,1,0:T(8,128)(2,1)}) custom-call(s32[2,888]{1,0:T(2,128)} %bitcast.94, s32[888,1]{1,0:T(8,128)} %iota_add_fusion.key_col, s32[1,888]{1,0:T(1,128)} %bitcast_add_fusion.key_row, bf16[888,512]{1,0:T(8,128)(2,1)} %bitcast.91), custom_call_target="tpu_custom_call" | custom-call | flops 2444230656 | bytes 5505024 | tf_op jit(solution)/shard_map/plan/pallas_call | solution.py:390
  22.6 3.6 slice_bitcast_fusion.6
  26.3 6.3 %all-to-all-start.4 = ((bf16[4,336,512]{2,1,0:T(8,128)(2,1)}), bf16[4,336,512]{2,1,0:T(8,128)(2,1)S(1)}, u32[]{:S(2)}, u32[]{:S(2)}) async-start(bf16[4,336,512]{2,1,0:T(8,128)(2,1)} %get-tuple-element.107), calls=%async_computation.4 | async-start | bytes 2752512 | tf_op jit(solution)/shard_map/all_to_all | solution.py:402
  32.5 1.1 convert_element_type.40
  33.8 31.5 %all-to-all-done.4.got_grad = bf16[4,336,512]{2,1,0:T(8,128)(2,1)S(1)} async-done(((bf16[4,336,512]{2,1,0:T(8,128)(2,1)}), bf16[4,336,512]{2,1,0:T(8,128)(2,1)S(1)}, u32[]{:S(2)}, u32[]{:S(2)}) %all-to-all-start.4) | async-done | bytes 1376288 | tf_op jit(solution)/shard_map/all_to_all | solution.py:402
  65.3 3.5 all-to-all-start.1
  69.6 1.0 slice_bitcast_fusion.10
  70.7 0.7 copy.63.vec
  71.4 1.6 fusion
  73.7 2.7 slice.122.w_qkv
  76.3 1.9 slice.123.w_out
  78.2 16.9 %forward.1 = (bf16[888,512]{1,0:T(8,128)(2,1)}, bf16[3,608,512]{2,1,0:T(8,128)(2,1)}, bf16[3,608,512]{2,1,0:T(8,128)(2,1)}, bf16[3,8,296,608]{3,2,1,0:T(8,128)(2...) custom-call(bf16[888,512]{1,0:T(8,128)(2,1)} %bitcast.85, ...), custom_call_target="tpu_custom_call" | custom-call | flops 5004853248 | bytes 9093120 | tf_op jit(solution)/shard_map/forward/pallas_call | solution.py:419
  95.1 9.3 %dispatch.1 = bf16[8,336,512]{2,1,0:T(8,128)(2,1)} custom-call(bf16[888,512]{1,0:T(8,128)(2,1)} %get-tuple-element.42.acts.a_ref, bf16[8,512]{1,0:T(8,128)(2,1)} %copy.64.router, s32[2,888]{1,0:T(2,128)} %bitcast.95, s32[8,888]{1,0:T(8,128)} %get-tuple-element.41.slots), custom_call_target="tpu_custom_call" | custom-call | flops 2444230656 | bytes 5505024 | tf_op jit(solution)/shard_map/dispatch/pallas_call | solution.py:437
  104.4 3.5 slice_bitcast_fusion.7
  107.9 5.1 %all-to-all-start.3 = ((bf16[4,336,512]{2,1,0:T(8,128)(2,1)}), bf16[4,336,512]{2,1,0:T(8,128)(2,1)S(1)}, u32[]{:S(2)}, u32[]{:S(2)}) async-start(bf16[4,336,512]{2,1,0:T(8,128)(2,1)} %get-tuple-element.109), calls=%async_computation.3 | async-start | bytes 2752512 | tf_op jit(solution)/shard_map/all_to_all | solution.py:402
  112.9 7.9 %all_gather.25 = bf16[2,512]{1,0:T(2,128)(2,1)S(1)} all-gather(bf16[2,128]{1,0:T(2,128)(2,1)S(1)} %convert_element_type.41), channel_id=1, replica_groups=mesh['dp'=4,'expert'=4,'context'=2] {'dp'}, dimensions={1}, use_global_device_ids=true | all-gather | bytes 2560 | tf_op jit(solution)/shard_map/all_gather | solution.py:385
  120.9 8.0 %all_gather.23 = bf16[2,2048]{1,0:T(2,128)(2,1)S(1)} all-gather(bf16[2,512]{1,0:T(2,128)(2,1)S(1)} %convert_element_type.38), channel_id=1, replica_groups=mesh['dp'=4,'expert'=4,'context'=2] {'dp'}, dimensions={1}, use_global_device_ids=true | all-gather | bytes 10240 | tf_op jit(solution)/shard_map/all_gather | solution.py:384
  130.1 4.8 slice_bitcast_fusion.3
  134.9 9.7 %all-to-all-done.3.got = bf16[4,336,512]{2,1,0:T(8,128)(2,1)S(1)} async-done(((bf16[4,336,512]{2,1,0:T(8,128)(2,1)}), bf16[4,336,512]{2,1,0:T(8,128)(2,1)S(1)}, u32[]{:S(2)}, u32[]{:S(2)}) %all-to-all-start.3) | async-done | bytes 1376288 | tf_op jit(solution)/shard_map/all_to_all | solution.py:402
  144.6 3.5 all-to-all-start
  148.4 12.2 %all-gather.10.cloned.1.call-done = bf16[2,2048,512]{2,1,0:T(8,128)(2,1)} async-done(((bf16[2,512,512]{2,1,0:T(8,128)(2,1)}), bf16[2,2048,512]{2,1,0:T(8,128)(2,1)}) %all-gather.10.cloned.1.call-update) | async-done | bytes 4194320 | tf_op jit(solution)/shard_map/all_gather | solution.py:383
  160.7 4.5 slice_bitcast_fusion.2
  165.2 25.2 %expert.3 = (bf16[4,336,512]{2,1,0:T(8,128)(2,1)}, bf16[4,336,512]{2,1,0:T(8,128)(2,1)}, bf16[512,2048]{1,0:T(8,128)(2,1)}, f32[1,2048]{1,0:T(1,128)}, bf16[2048,512]{1,0:T(8,128)(2,1)}, /*index=5*/f32[1,512]{1,0:T(1,128)}) custom-call(bf16[4,336,512]{2,1,0:T(8,128)(2,1)} %copy-done.8, bf16[4,336,512]{2,1,0:T(8,128)(2,1)} %copy-done.6, ...), custom_call_target="tpu_custom_call" | custom-call | flops 16911433728 | bytes 13893632 | tf_op jit(solution)/shard_map/expert/pallas_call | solution.py:453
  190.4 1.2 copy-done.9
  191.6 25.0 %expert.2 = (bf16[4,336,512]{2,1,0:T(8,128)(2,1)}, bf16[4,336,512]{2,1,0:T(8,128)(2,1)}, bf16[512,2048]{1,0:T(8,128)(2,1)}, f32[1,2048]{1,0:T(1,128)}, bf16[2048,512]{1,0:T(8,128)(2,1)}, /*index=5*/f32[1,512]{1,0:T(1,128)}) custom-call(bf16[4,336,512]{2,1,0:T(8,128)(2,1)} %copy-done.9, bf16[4,336,512]{2,1,0:T(8,128)(2,1)} %copy-done.7, ...), custom_call_target="tpu_custom_call" | custom-call | flops 16911433728 | bytes 13893632 | tf_op jit(solution)/shard_map/expert/pallas_call | solution.py:453
  216.6 4.0 pad_maximum_fusion
  220.7 4.8 all-to-all-start.7
  225.5 4.3 pad_maximum_fusion.1
  229.8 28.4 %all-to-all-done.7 = bf16[4,336,512]{2,1,0:T(8,128)(2,1)S(1)} async-done(((bf16[4,336,512]{2,1,0:T(8,128)(2,1)}), bf16[4,336,512]{2,1,0:T(8,128)(2,1)S(1)}, u32[]{:S(2)}, u32[]{:S(2)}) %all-to-all-start.7) | async-done | bytes 1376288 | tf_op jit(solution)/shard_map/all_to_all | solution.py:402
  258.2 3.5 all-to-all-start.6
  261.8 1.0 copy.60
  263.2 0.7 concatenate.33.router
  263.8 30.1 %all-to-all-done.6 = bf16[4,336,512]{2,1,0:T(8,128)(2,1)S(1)} async-done(((bf16[4,336,512]{2,1,0:T(8,128)(2,1)}), bf16[4,336,512]{2,1,0:T(8,128)(2,1)S(1)}, u32[]{:S(2)}, u32[]{:S(2)}) %all-to-all-start.6) | async-done | bytes 1376288 | tf_op jit(solution)/shard_map/all_to_all | solution.py:402
  294.2 1.8 copy.70
  296.1 33.9 %backward.1 = (f32[888,512]{1,0:T(8,128)}, bf16[888,512]{1,0:T(8,128)(2,1)}, bf16[2,888,512]{2,1,0:T(8,128)(2,1)}, bf16[2,888,512]{2,1,0:T(8,128)(2,1)}, f32[512...) custom-call(bf16[888,512]{1,0:T(8,128)(2,1)} %bitcast.92, bf16[2688,512]{1,0:T(8,128)(2,1)} %bitcast.76, ...), custom_call_target="tpu_custom_call" | custom-call | flops 7798259712 | bytes 13639680 | tf_op jit(solution)/shard_map/backward/pallas_call | solution.py:497
  330.1 1.4 slice_bitcast_fusion.9
  331.8 1.0 slice_bitcast_fusion.8
  333.8 1.0 slice.166
  334.8 0.7 slice.167
  335.6 11.3 %input.1 = (bf16[888,512]{1,0:T(8,128)(2,1)}, f32[512,1536]{1,0:T(8,128)}, f32[8,512]{1,0:T(8,128)}) custom-call(bf16[888,512]{1,0:T(8,128)(2,1)} %bitcast.86, f32[888,512]{1,0:T(8,128)} %get-tuple-element.54.dh_ref, bf16[888,512]{1,0:T(8,128)(2,1)} %get-tuple-element.55.dq_ref, bf16[2,888,512]{2,1,0:T(8,128)(2,1)} %get-tuple-element.56.dk_own, ...), custom_call_target="tpu_custom_call" | custom-call | flops 2793406464 | bytes 9093120 | tf_op jit(solution)/shard_map/input/pallas_call | solution.py:519
  346.9 2.1 convert.46
  349.0 0.7 slice.168
  349.9 3.4 concatenate.37
  353.3 3.6 all-to-all-start.5
  357.7 32.6 %all-to-all-done.5 = bf16[4,336,512]{2,1,0:T(8,128)(2,1)S(1)} async-done(((bf16[4,336,512]{2,1,0:T(8,128)(2,1)}), bf16[4,336,512]{2,1,0:T(8,128)(2,1)S(1)}, u32[]{:S(2)}, u32[]{:S(2)}) %all-to-all-start.5) | async-done | bytes 1376288 | tf_op jit(solution)/shard_map/all_to_all | solution.py:402
  390.2 3.5 all-to-all-start.2
  395.3 33.1 %all-to-all-done.2 = bf16[4,336,512]{2,1,0:T(8,128)(2,1)S(1)} async-done(((bf16[4,336,512]{2,1,0:T(8,128)(2,1)}), bf16[4,336,512]{2,1,0:T(8,128)(2,1)S(1)}, u32[]{:S(2)}, u32[]{:S(2)}) %all-to-all-start.2) | async-done | bytes 1376288 | tf_op jit(solution)/shard_map/all_to_all | solution.py:402
  428.6 1.8 copy.69
  430.5 6.4 %combine.1 = bf16[888,512]{1,0:T(8,128)(2,1)} custom-call(s32[888,8]{1,0:T(8,128)} %bitcast.88, bf16[2688,512]{1,0:T(8,128)(2,1)} %bitcast.79, f32[888,512]{1,0:T(8,128)} %get-tuple-element.46.h_ref), custom_call_target="tpu_custom_call" | custom-call | flops 2444230656 | bytes 4546560 | tf_op jit(solution)/shard_map/combine/pallas_call | solution.py:533
  436.8 2.8 convert_element_type.45
  439.6 2.8 convert_element_type.46
  442.5 28.7 %all-reduce.4.cloned.1.call-done = bf16[128,2103]{1,0:T(8,128)(2,1)} async-done(((bf16[128,2103]{1,0:T(8,128)(2,1)}), bf16[128,2103]{1,0:T(8,128)(2,1)}) %all-reduce.4.cloned.1.call-update) | async-done | bytes 538384 | tf_op jit(solution)/shard_map/psum | solution.py:553
  471.1 1.2 convert_element_type.44
  473.1 0.9 fusion.1
  474.8 0.7 reshape.117
  476.3 1.0 slice.141
  477.2 0.7 slice.142
  (118 shorter events, 11.3 us)
Async XLA Ops:
  7.2 5.0 %copy-start.2 = (f32[2,128,2048]{2,1,0:T(8,128)S(1)}, f32[2,128,2048]{2,1,0:T(8,128)}, u32[]{:S(2)}) copy-start(f32[2,128,2048]{2,1,0:T(8,128)} %param.21) | copy-start | bytes 6291460
  7.2 62.4 %all-gather.6.cloned.1.call-start = ((), (), s32[]{:S(2)}) async-start(), calls=%async_computation.11 | async-start | bytes 2785280 | tf_op jit(solution)/shard_map/all_gather | solution.py:375
  12.1 1.2 copy-start.13
  12.1 118.0 %all-gather.8.cloned.1.call-start = ((), (), s32[]{:S(2)}) async-start(), calls=%async_computation.12 | async-start | bytes 5242880 | tf_op jit(solution)/shard_map/all_gather | solution.py:382
  26.3 6.3 %copy-start.3 = (f32[2,512,512]{2,1,0:T(8,128)S(1)}, f32[2,512,512]{2,1,0:T(8,128)}, u32[]{:S(2)}) copy-start(f32[2,512,512]{2,1,0:T(8,128)} %param.23) | copy-start | bytes 6291460
  26.3 39.0 %all-to-all-start.4 = ((bf16[4,336,512]{2,1,0:T(8,128)(2,1)}), bf16[4,336,512]{2,1,0:T(8,128)(2,1)S(1)}, u32[]{:S(2)}, u32[]{:S(2)}) async-start(bf16[4,336,512]{2,1,0:T(8,128)(2,1)} %get-tuple-element.107), calls=%async_computation.4 | async-start | bytes 2752512 | tf_op jit(solution)/shard_map/all_to_all | solution.py:402
  32.5 128.1 %all-gather.10.cloned.1.call-start = ((), (), s32[]{:S(2)}) async-start(), calls=%async_computation.13 | async-start | bytes 5242880 | tf_op jit(solution)/shard_map/all_gather | solution.py:383
  33.6 35.2 %copy-start.14 = (s32[3,592]{1,0:T(4,128)S(1)}, s32[3,592]{1,0:T(4,128)}, u32[]{:S(2)}) copy-start(s32[3,592]{1,0:T(4,128)} %param.14) | copy-start | bytes 21316
  33.7 44.5 %collective-permute-start = (bf16[888,512]{1,0:T(8,128)(2,1)}, bf16[888,512]{1,0:T(8,128)(2,1)}, u32[]{:S(2)}, u32[]{:S(2)}) collective-permute-start(bf16[888,512]{1,0:T(8,128)(2,1)} %bitcast.84), channel_id=1, source_target_pairs={{0,1},{1,0},{2,3},{3,2},{4,5},{5,4},{6,7},{7,6},{8,9},{9,8},{10,11... | collective-permute-start | bytes 2727944 | tf_op jit(solution)/shard_map/ppermute | solution.py:372
  65.3 8.4 %copy-start.6 = (bf16[4,336,512]{2,1,0:T(8,128)(2,1)}, bf16[4,336,512]{2,1,0:T(8,128)(2,1)S(1)}, u32[]{:S(2)}) copy-start(bf16[4,336,512]{2,1,0:T(8,128)(2,1)S(1)} %all-to-all-done.4.got_grad) | copy-start | bytes 4128772
  65.3 42.6 %all-to-all-start.1 = ((bf16[4,336,512]{2,1,0:T(8,128)(2,1)}), bf16[4,336,512]{2,1,0:T(8,128)(2,1)S(1)}, u32[]{:S(2)}, u32[]{:S(2)}) async-start(bf16[4,336,512]{2,1,0:T(8,128)(2,1)} %get-tuple-element.106), calls=%async_computation.1 | async-start | bytes 2752512 | tf_op jit(solution)/shard_map/all_to_all | solution.py:402
  107.8 5.1 %copy-start.17 = (f32[2,512]{1,0:T(2,128)S(1)}, f32[2,512]{1,0:T(2,128)}, u32[]{:S(2)}) copy-start(f32[2,512]{1,0:T(2,128)} %param.22) | copy-start | bytes 12292
  107.8 5.1 %copy-start.20 = (f32[2,128]{1,0:T(2,128)S(1)}, f32[2,128]{1,0:T(2,128)}, u32[]{:S(2)}) copy-start(f32[2,128]{1,0:T(2,128)} %param.24) | copy-start | bytes 3076
  107.8 27.1 %copy-start.7 = (bf16[4,336,512]{2,1,0:T(8,128)(2,1)}, bf16[4,336,512]{2,1,0:T(8,128)(2,1)S(1)}, u32[]{:S(2)}) copy-start(bf16[4,336,512]{2,1,0:T(8,128)(2,1)S(1)} %all-to-all-done.1.got_grad) | copy-start | bytes 4128772
  107.9 36.8 %all-to-all-start.3 = ((bf16[4,336,512]{2,1,0:T(8,128)(2,1)}), bf16[4,336,512]{2,1,0:T(8,128)(2,1)S(1)}, u32[]{:S(2)}, u32[]{:S(2)}) async-start(bf16[4,336,512]{2,1,0:T(8,128)(2,1)} %get-tuple-element.109), calls=%async_computation.3 | async-start | bytes 2752512 | tf_op jit(solution)/shard_map/all_to_all | solution.py:402
  144.6 20.6 %copy-start.8 = (bf16[4,336,512]{2,1,0:T(8,128)(2,1)}, bf16[4,336,512]{2,1,0:T(8,128)(2,1)S(1)}, u32[]{:S(2)}) copy-start(bf16[4,336,512]{2,1,0:T(8,128)(2,1)S(1)} %all-to-all-done.3.got) | copy-start | bytes 4128772
  144.6 45.8 %all-to-all-start = ((bf16[4,336,512]{2,1,0:T(8,128)(2,1)}), bf16[4,336,512]{2,1,0:T(8,128)(2,1)S(1)}, u32[]{:S(2)}, u32[]{:S(2)}) async-start(bf16[4,336,512]{2,1,0:T(8,128)(2,1)} %get-tuple-element.108), calls=%async_computation | async-start | bytes 2752512 | tf_op jit(solution)/shard_map/all_to_all | solution.py:402
  148.2 208.8 %reduce-scatter.6.cloned.1.call-start = ((), (), s32[]{:S(2)}) async-start(), calls=%async_computation.16 | async-start | bytes 4718592 | tf_op jit(solution)/shard_map/reduce_scatter | solution.py:489
  190.4 1.2 copy-start.9
  191.6 25.0 %copy-start.5 = (bf16[512,2048]{1,0:T(8,128)(2,1)S(1)}, bf16[512,2048]{1,0:T(8,128)(2,1)}, u32[]{:S(2)}) copy-start(bf16[512,2048]{1,0:T(8,128)(2,1)} %get-tuple-element.69) | copy-start | bytes 6291460
  220.7 4.8 copy-start.4
  220.7 37.5 %all-to-all-start.7 = ((bf16[4,336,512]{2,1,0:T(8,128)(2,1)}), bf16[4,336,512]{2,1,0:T(8,128)(2,1)S(1)}, u32[]{:S(2)}, u32[]{:S(2)}) async-start(bf16[4,336,512]{2,1,0:T(8,128)(2,1)} %get-tuple-element.48), calls=%async_computation.7 | async-start | bytes 2752512 | tf_op jit(solution)/shard_map/all_to_all | solution.py:402
  225.5 168.4 %reduce-scatter.8.cloned.1.call-start = ((), (), s32[]{:S(2)}) async-start(), calls=%async_computation.18 | async-start | bytes 4718592 | tf_op jit(solution)/shard_map/reduce_scatter | solution.py:489
  229.8 32.0 %copy-start.12 = (s32[8,888]{1,0:T(8,128)S(1)}, s32[8,888]{1,0:T(8,128)}, u32[]{:S(2)}) copy-start(s32[8,888]{1,0:T(8,128)} %get-tuple-element.41.slots) | copy-start | bytes 85252
  229.8 33.3 %copy-start.11 = (bf16[512,8]{1,0:T(8,128)(2,1)S(1)}, bf16[512,8]{1,0:T(8,128)(2,1)}, u32[]{:S(2)}) copy-start(bf16[512,8]{1,0:T(8,128)(2,1)} %get-tuple-element.110) | copy-start | bytes 24580
  258.2 35.8 %all-to-all-start.6 = ((bf16[4,336,512]{2,1,0:T(8,128)(2,1)}), bf16[4,336,512]{2,1,0:T(8,128)(2,1)S(1)}, u32[]{:S(2)}, u32[]{:S(2)}) async-start(bf16[4,336,512]{2,1,0:T(8,128)(2,1)} %get-tuple-element.47), calls=%async_computation.6 | async-start | bytes 2752512 | tf_op jit(solution)/shard_map/all_to_all | solution.py:402
  261.8 132.8 %reduce-scatter.4.cloned.1.call-start = ((), (), s32[]{:S(2)}) async-start(), calls=%async_computation.14 | async-start | bytes 2785280 | tf_op jit(solution)/shard_map/reduce_scatter | solution.py:552
  330.0 1.8 copy-start.1
  330.0 3.0 copy-start.15
  330.1 3.0 copy-start.16
  330.1 3.4 copy-start.18
  330.1 3.4 copy-start.19
  331.4 2.3 copy-start.10
  331.5 4.0 collective-permute-start.1
  332.8 2.9 collective-permute-start.2
  353.3 36.9 %all-to-all-start.5 = ((bf16[4,336,512]{2,1,0:T(8,128)(2,1)}), bf16[4,336,512]{2,1,0:T(8,128)(2,1)S(1)}, u32[]{:S(2)}, u32[]{:S(2)}) async-start(bf16[4,336,512]{2,1,0:T(8,128)(2,1)} %get-tuple-element.45), calls=%async_computation.5 | async-start | bytes 2752512 | tf_op jit(solution)/shard_map/all_to_all | solution.py:402
  356.9 79.9 %all-gather.12.cloned.1.call-start = ((), (), s32[]{:S(2)}) async-start(), calls=%async_computation.17 | async-start | bytes 1572864 | tf_op jit(solution)/shard_map/all_gather | solution.py:490
  390.2 38.1 %all-to-all-start.2 = ((bf16[4,336,512]{2,1,0:T(8,128)(2,1)}), bf16[4,336,512]{2,1,0:T(8,128)(2,1)S(1)}, u32[]{:S(2)}, u32[]{:S(2)}) async-start(bf16[4,336,512]{2,1,0:T(8,128)(2,1)} %get-tuple-element.44), calls=%async_computation.2 | async-start | bytes 2752512 | tf_op jit(solution)/shard_map/all_to_all | solution.py:402
  393.8 45.8 %all-gather.14.cloned.1.call-start = ((), (), s32[]{:S(2)}) async-start(), calls=%async_computation.19 | async-start | bytes 1572864 | tf_op jit(solution)/shard_map/all_gather | solution.py:490
  394.6 76.6 %all-reduce.4.cloned.1.call-start = ((), (), s32[]{:S(2)}) async-start(), calls=%async_computation.15 | async-start | bytes 1114112 | tf_op jit(solution)/shard_map/psum | solution.py:553
  471.1 3.5 copy-start
Sparse Core Ops, SparseCore 0:
  12.3 39.1 all-gather.5
  53.3 52.7 all-gather.7
  107.9 52.7 all-gather.9
  220.8 51.3 reduce-scatter.5
  275.8 51.3 reduce-scatter.7
  353.5 33.8 reduce-scatter.3
  388.9 9.0 all-gather.11
  399.5 10.1 all-gather.13
  412.1 58.9 all-reduce.3

commit v2 on v1

--- a/solution.py
+++ b/solution.py
@@ -156,7 +156,7 @@
         delta[rows, :] = (gate * got_grad[src].astype(F32)).astype(BF)
         for lo in range(0, ff, chunk):
             cols = pl.ds(lo, chunk)
-            z = nn(acts[rows, :], w_in[:, cols]) + b_in[:, cols]
+            z = nn(acts[rows, :], w_in[:, cols]) + b_in[lo // chunk].astype(F32)
             value, rise = gelu_parts(z)
             hidden[rows, cols] = value.astype(BF)
             slope[rows, cols] = rise.astype(BF)
@@ -350,6 +350,186 @@
     out_ref[...] = (h_ref[...] + nn(jnp.where(hit, 1.0, 0.0).astype(BF), table[...])).astype(BF)
 
 
+MESH = pl.DeviceIdType.MESH
+
+
+def send(src, dst, sems, slot, device):
+    copy = pltpu.make_async_remote_copy(
+        src_ref=src, dst_ref=dst, send_sem=sems[0].at[slot], recv_sem=sems[1].at[slot],
+        device_id=device, device_id_type=MESH,
+    )
+    copy.start()
+    return copy
+
+
+def greet(devices):
+    barrier = pltpu.get_barrier_semaphore()
+    for device in devices:
+        pl.semaphore_signal(barrier, inc=1, device_id=device, device_id_type=MESH)
+    pl.semaphore_wait(barrier, len(devices))
+
+
+def comm_call(body, name, number, ins, outs, scratch, flops=0, moved=0, vmem=56):
+    return pl.pallas_call(
+        body,
+        name=name,
+        in_specs=[pl.BlockSpec(memory_space=space) for space in ins],
+        out_specs=[pl.BlockSpec(memory_space=space) for _, _, space in outs],
+        out_shape=[jax.ShapeDtypeStruct(shape, dtype) for shape, dtype, _ in outs],
+        scratch_shapes=list(scratch),
+        cost_estimate=pl.CostEstimate(flops=int(flops), bytes_accessed=int(moved), transcendentals=0),
+        compiler_params=pltpu.CompilerParams(
+            vmem_limit_bytes=vmem * MIB, collective_id=number, has_side_effects=True
+        ),
+    )
+
+
+def start_kernel(
+    dps, x, w_qkv, w_out, w_router, vectors, b_in, b_back,
+    qkv_all, out_all, router_all, b_in_all, vec, bias_back, x_other,
+    vec_all, back_all, far_send, far_recv, near_send, near_recv,
+):
+    dp, group, core = lax.axis_index("dp"), lax.axis_index("expert"), lax.axis_index("context")
+    rows = w_qkv.shape[0]
+    half = rows // 2
+    near = (dp, group, 1 - core)
+    peers = [(lax.rem(dp + step, dps), group, core) for step in range(1, dps)]
+    greet(peers + [near])
+    far, close = (far_send, far_recv), (near_send, near_recv)
+    waits = [send(x, x_other, close, 0, near)]
+    qkv_all[dp] = w_qkv[...].astype(BF)
+    own = pl.ds(pl.multiple_of(core * half, half), half)
+    copies = []
+    for step, peer in enumerate(peers):
+        copies.append(send(qkv_all.at[dp, own], qkv_all.at[dp, own], far, step * 6, peer))
+    out_all[dp] = w_out[...].astype(BF)
+    spare = router_all.shape[2] - w_router.shape[1]
+    router_all[dp] = jnp.concatenate([w_router[...], jnp.zeros((rows, spare), F32)], axis=1).astype(BF)
+    vec_all[dp] = jnp.concatenate([vectors[...], jnp.zeros((1, rows), F32)], axis=0).astype(BF)
+    b_in_all[dp] = b_in[...].astype(BF)
+    back_all[dp] = b_back[...].astype(BF)
+    for step, peer in enumerate(peers):
+        copies.append(send(out_all.at[dp, own], out_all.at[dp, own], far, step * 6 + 1, peer))
+    for step, peer in enumerate(peers):
+        for at, ref in enumerate((router_all, vec_all, b_in_all, back_all)):
+            waits.append(send(ref.at[dp], ref.at[dp], far, step * 6 + 2 + at, peer))
+    for at, copy in enumerate(copies):
+        step, ref = at % len(peers), (qkv_all, out_all)[at // len(peers)]
+        copy.wait()
+        source = lax.rem(dp - step - 1 + dps, dps)
+        waits.append(send(ref.at[source, own], ref.at[source, own], close, 1 + at, near))
+    for copy in waits:
+        copy.wait()
+    vec[...] = jnp.concatenate([vec_all[at].astype(F32) for at in range(dps)], axis=1)
+    bias_back[...] = jnp.concatenate([back_all[at].astype(F32) for at in range(dps)], axis=1)
+
+
+def reduce_kernel(
+    dps, groups, g_qkv, g_out, g_router, g_one, g_two, b_in, b_back,
+    o_qkv, o_out, o_router, o_vec, o_in, o_back,
+    near_out, near_in, far_out, far_in, deep_out, deep_in, total,
+    small_near, small_far, small_got, small_deep, bin_near, bin_far, bin_got,
+    near_s, near_r, far_s, far_r, deep_s, deep_r, last_s, last_r,
+):
+    dp, group, core = lax.axis_index("dp"), lax.axis_index("expert"), lax.axis_index("context")
+    width = g_out.shape[0]
+    rows = width // dps
+    half = rows // 2
+    near = (dp, group, 1 - core)
+    peers = [(lax.rem(dp + step, dps), group, core) for step in range(1, dps)]
+    others = [(dp, lax.rem(group + step, groups), core) for step in range(1, groups)]
+    greet(peers + others + [near])
+    near_sems, far_sems, deep_sems, last_sems = (near_s, near_r), (far_s, far_r), (deep_s, deep_r), (last_s, last_r)
+    chunk = g_router.shape[1]
+    sources = [(g_qkv, at) for at in range(0, g_qkv.shape[1], width)] + [(g_out, 0), (g_router, 0)]
+    sizes = [width] * (len(sources) - 1) + [chunk]
+    starts = [width * at for at in range(len(sources))]
+
+    small = jnp.concatenate([g_one[0:4], g_two[0:3], jnp.zeros((1, width), F32), b_back[...]], axis=0)
+    small = jnp.concatenate([small, jnp.zeros((16 - small.shape[0], width), F32)], axis=0)
+    for at in range(dps):
+        small_near[0, at] = small[:, at * rows : (at + 1) * rows]
+        bin_near[0, at] = b_in[:, at * bin_near.shape[3] : (at + 1) * bin_near.shape[3]]
+    first = [
+        send(small_near.at[0], small_near.at[1], near_sems, 0, near),
+        send(bin_near.at[0], bin_near.at[1], near_sems, 1, near),
+    ]
+    theirs = pl.multiple_of((1 - core) * half, half)
+    ours = pl.multiple_of(core * half, half)
+    for at, (ref, lane) in enumerate(sources):
+        cols = pl.ds(starts[at], sizes[at])
+        for block in range(dps):
+            near_out[block, :, cols] = ref[pl.ds(block * rows + theirs, half), lane : lane + sizes[at]].astype(BF)
+        first.append(send(near_out.at[:, :, cols], near_in.at[:, :, cols], near_sems, 2 + at, near))
+    second = []
+    for copy in first[:2]:
+        copy.wait()
+    small_far[...] = small_near[0] + small_near[1]
+    bin_far[...] = bin_near[0] + bin_near[1]
+    smalls = []
+    for step, peer in enumerate(peers):
+        target = lax.rem(dp + step + 1, dps)
+        smalls.append(send(small_far.at[target], small_got.at[step], far_sems, step, peer))
+        smalls.append(send(bin_far.at[target], bin_got.at[step], far_sems, dps + step, peer))
+    for at, (ref, lane) in enumerate(sources):
+        cols = pl.ds(starts[at], sizes[at])
+        first[2 + at].wait()
+        for step, peer in enumerate(peers):
+            target = lax.rem(dp + step + 1, dps)
+            block = ref[pl.ds(pl.multiple_of(target * rows, rows) + ours, half), lane : lane + sizes[at]]
+            far_out[step, :, cols] = (block + near_in[target, :, cols].astype(F32)).astype(BF)
+            second.append(
+                send(far_out.at[step, :, cols], far_in.at[step, :, cols], far_sems, (2 + at) * dps + step, peer)
+            )
+    for copy in smalls:
+        copy.wait()
+    lone = small_far[dp]
+    lone_in = bin_far[dp]
+    for step in range(dps - 1):
+        lone = lone + small_got[step]
+        lone_in = lone_in + bin_got[step]
+    o_in[...] = lone_in
+    o_back[...] = lone[8 : 8 + o_back.shape[0]]
+    small_deep[group] = lone
+    third = []
+    for step, peer in enumerate(others):
+        third.append(send(small_deep.at[group], small_deep.at[group], deep_sems, step, peer))
+    for at, (ref, lane) in enumerate(sources):
+        cols = pl.ds(starts[at], sizes[at])
+        mine = ref[pl.ds(pl.multiple_of(dp * rows, rows) + ours, half), lane : lane + sizes[at]]
+        mine = mine + near_in[dp, :, cols].astype(F32)
+        for step in range(dps - 1):
+            second[at * (dps - 1) + step].wait()
+            mine = mine + far_in[step, :, cols].astype(F32)
+        deep_in[group, :, cols] = mine.astype(BF)
+        for step, peer in enumerate(others):
+            third.append(
+                send(deep_in.at[group, :, cols], deep_in.at[group, :, cols], deep_sems, (1 + at) * groups + step, peer)
+            )
+    for copy in third[: groups - 1]:
+        copy.wait()
+    lone = small_deep[0]
+    for at in range(1, groups):
+        lone = lone + small_deep[at]
+    o_vec[...] = lone[0:7]
+    last = []
+    here = pl.ds(ours, half)
+    for at in range(len(sources)):
+        cols = pl.ds(starts[at], sizes[at])
+        for step in range(groups - 1):
+            third[(1 + at) * (groups - 1) + step].wait()
+        done = deep_in[0, :, cols].astype(F32)
+        for source in range(1, groups):
+            done = done + deep_in[source, :, cols].astype(F32)
+        total[here, cols] = done
+        last.append(send(total.at[here, cols], total.at[here, cols], last_sems, at, near))
+    for at in range(len(sources)):
+        last[at].wait()
+    o_qkv[...] = total[:, : 3 * width]
+    o_out[...] = total[:, 3 * width : 4 * width]
+    o_router[...] = total[:, 4 * width : 4 * width + o_router.shape[1]]
+
+
 def shards(
     inputs, key_mask, routes, priority, vectors, w_qkv, w_out, w_router, w_in, b_in, w_back, b_back, cotangent
 ):
@@ -369,20 +549,40 @@
 
     x = inputs.reshape(tokens, width)
     grad = cotangent.reshape(tokens, width)
-    x_other = lax.ppermute(x, "context", swap)
-
-    dense = jnp.concatenate([w_qkv, w_out, w_router, vectors.T], axis=1).astype(BF)
-    dense = lax.all_gather(dense, "dp", axis=0, tiled=True)
-    qkv_all, out_all = dense[:, : 3 * width], dense[:, 3 * width : 4 * width]
-    router_all = dense[:, 4 * width : 4 * width + experts]
-    vec = dense[:, 4 * width + experts :].astype(F32).T
-    vec = jnp.concatenate([vec, jnp.zeros((1, width), F32)], axis=0)
-    router_pad = jnp.concatenate([router_all, jnp.zeros((width, LANES - experts), BF)], axis=1)
-
-    in_w = lax.all_gather(w_in.astype(BF), "dp", axis=1, tiled=True)
-    back_w = lax.all_gather(w_back.astype(BF), "dp", axis=1, tiled=True)
-    in_b = lax.all_gather(b_in.astype(BF), "dp", axis=1, tiled=True).astype(F32)
-    back_b = lax.all_gather(b_back.astype(BF), "dp", axis=1, tiled=True).astype(F32)
+    V, A = pltpu.VMEM, pl.ANY
+    rows = w_qkv.shape[0]
+    qkv_all, out_all, router_all, in_b, vec, back_b, x_other = comm_call(
+        partial(start_kernel, dps),
+        "start",
+        0,
+        [V] * 7,
+        [
+            ((dps, rows, 3 * width), BF, V),
+            ((dps, rows, width), BF, V),
+            ((dps, rows, LANES), BF, V),
+            ((dps, per_device, ff // dps), BF, V),
+            ((8, width), F32, V),
+            ((per_device, width), F32, V),
+            ((tokens, width), BF, V),
+        ],
+        [
+            pltpu.VMEM((dps, 8, rows), BF),
+            pltpu.VMEM((dps, per_device, width // dps), BF),
+            pltpu.SemaphoreType.DMA((6 * (dps - 1),)),
+            pltpu.SemaphoreType.DMA((6 * (dps - 1),)),
+            pltpu.SemaphoreType.DMA((1 + 2 * (dps - 1),)),
+            pltpu.SemaphoreType.DMA((1 + 2 * (dps - 1),)),
+        ],
+        moved=8 * width * width * 4,
+    )(x, w_qkv, w_out, w_router, vectors, b_in, b_back)
+    qkv_all = qkv_all.reshape(width, 3 * width)
+    out_all = out_all.reshape(width, width)
+    router_pad = router_all.reshape(width, LANES)
+    router_rows = router_pad[:, :experts].T
+
+    in_w, back_w, x_other = lax.optimization_barrier((w_in.astype(BF), w_back.astype(BF), x_other))
+    in_w = lax.all_gather(in_w, "dp", axis=1, tiled=True)
+    back_w = lax.all_gather(back_w, "dp", axis=1, tiled=True)
 
     route_rows = routes.reshape(tokens, 2).T
     keys = priority.reshape(tokens) * tokens + jnp.arange(tokens, dtype=I32)
@@ -443,7 +643,7 @@
         scratch=[pltpu.VMEM((2, 8, tokens), F32)],
         flops=2 * total * tokens * width,
         moved=4 * total * width,
-    )(acts, router_all.T, route_rows, slots)
+    )(acts, router_rows, route_rows, slots)
     got = [exchange(by_expert(send_rows, which)) for which in range(per_device)]
 
     out_rows, back_rows, g_in, g_b_in, g_back, g_b_back = [], [], [], [], [], []
@@ -451,7 +651,7 @@
     rows_all = groups * cap_pad
     for which in range(per_device):
         made = call(
-            partial(expert_kernel, cap, 512),
+            partial(expert_kernel, cap, ff // dps),
             "expert",
             (),
             [None] * 6,
@@ -473,7 +673,7 @@
             flops=12 * rows_all * width * ff,
             moved=8 * rows_all * width + 8 * width * ff,
         )(
-            got[which], got_grad[which], in_w[which], in_b[which][None], back_w[which], back_b[which][None]
+            got[which], got_grad[which], in_w[which], in_b[:, which][:, None], back_w[which], back_b[which][None]
         )
         for kept, piece in zip((out_rows, back_rows, g_in, g_b_in, g_back, g_b_back), made):
             kept.append(piece)
@@ -540,38 +740,56 @@
         moved=10 * tokens * width,
     )(slot_cols, out_table, after)
 
-    mine = (jnp.arange(groups) == lax.axis_index("expert")).astype(F32)
-    wide_b = jnp.concatenate(g_b_in, axis=0).reshape(per_device, dps, ff // dps)
-    wide_b = wide_b.transpose(1, 0, 2).reshape(width, -1)
-    b_cols = wide_b.shape[1]
-    wide_b = (mine[None, :, None] * wide_b[:, None, :]).reshape(width, groups * b_cols)
-    slim_b = jnp.concatenate(g_b_back, axis=0).T
-    slim_b = (mine[None, :, None] * slim_b[:, None, :]).reshape(width, experts)
-    vec_cols = jnp.concatenate([g_vec_one[:4], g_vec_two[:3]], axis=0).T
-    pack = jnp.concatenate([g_qkv, g_out, g_router[:, :experts], vec_cols, wide_b, slim_b], axis=1).astype(BF)
-    pack = lax.psum_scatter(pack, "dp", scatter_dimension=0, tiled=True)
-    pack = lax.psum(pack, ("expert", "context")).astype(F32)
-    cuts = [3 * width, width, experts, 7, groups * b_cols, experts]
-    pieces, at = [], 0
-    for size in cuts:
-        pieces.append(pack[:, at : at + size])
-        at += size
-    grad_qkv, grad_out, grad_router, grad_vec, wide_b, slim_b = pieces
-    group = lax.axis_index("expert")
-    wide_b = lax.dynamic_slice_in_dim(wide_b, group * b_cols, b_cols, axis=1)
-    grad_b_in = wide_b.reshape(per_device, ff // dps)
-    slim_b = lax.dynamic_slice_in_dim(slim_b, group * per_device, per_device, axis=1)
+    wide = 4 * width + LANES
+    dma = pltpu.SemaphoreType.DMA
+    halves_of = rows // 2
+    grad_qkv, grad_out, grad_router, grad_vec, grad_b_in, grad_b_back = comm_call(
+        partial(reduce_kernel, dps, groups),
+        "reduce",
+        1,
+        [V] * 7,
+        [
+            ((rows, 3 * width), F32, V),
+            ((rows, width), F32, V),
+            ((rows, experts), F32, V),
+            ((7, rows), F32, V),
+            ((per_device, ff // dps), F32, V),
+            ((per_device, rows), F32, V),
+        ],
+        [
+            pltpu.VMEM((dps, halves_of, wide), BF),
+            pltpu.VMEM((dps, halves_of, wide), BF),
+            pltpu.VMEM((dps - 1, halves_of, wide), BF),
+            pltpu.VMEM((dps - 1, halves_of, wide), BF),
+            pltpu.VMEM((8, LANES), BF),
+            pltpu.VMEM((groups, halves_of, wide), BF),
+            pltpu.VMEM((rows, wide), F32),
+            pltpu.VMEM((2, dps, 16, rows), F32),
+            pltpu.VMEM((dps, 16, rows), F32),
+            pltpu.VMEM((dps - 1, 16, rows), F32),
+            pltpu.VMEM((groups, 16, rows), F32),
+            pltpu.VMEM((2, dps, per_device, ff // dps), F32),
+            pltpu.VMEM((dps, per_device, ff // dps), F32),
+            pltpu.VMEM((dps - 1, per_device, ff // dps), F32),
+            dma((7,)), dma((7,)), dma((7 * dps,)), dma((7 * dps,)),
+            dma((6 * groups,)), dma((6 * groups,)), dma((5,)), dma((5,)),
+        ],
+        moved=20 * width * wide,
+    )(
+        g_qkv, g_out, g_router, g_vec_one, g_vec_two,
+        jnp.concatenate(g_b_in, axis=0), jnp.concatenate(g_b_back, axis=0),
+    )
     return (
         output.reshape(images, half, width),
         dx.reshape(images, half, width),
-        grad_vec.T,
+        grad_vec,
         grad_qkv,
         grad_out,
         grad_router,
         grad_w_in,
         grad_b_in,
         grad_w_back,
-        slim_b.T,
+        grad_b_back,
     )
 
 

time: 493 us -> 492 us (level)
  waiting for transfers between devices: 209 us -> 86.9 us
  blocking collectives: 16 us -> 107 us
  Pallas kernels: 136 us -> 198 us
  local copies, waits for them, and re-layouts: 49.9 us -> 33.9 us
  starting transfers between devices: 34.7 us -> 20.3 us
    all_to_all x0 -> x3, blocking collectives: none -> 107 us  [exchange(): lax.all_to_all(rows, 'expert', split_axis=0, concat_axis=0, tiled=True)]
    all_to_all x8 -> x5, waiting for transfers between devices: 165 us -> 86 us  [exchange(): lax.all_to_all(rows, 'expert', split_axis=0, concat_axis=0, tiled=True)]
    pallas_call x2 -> x4, Pallas kernels: 50.2 us -> 113 us  [the longest x2 50.2 us: shards(): call(partial(expert_kernel, cap, ff // dps), 'expert', (), [None] * 6, [(...]
    psum x1 -> x0, waiting for transfers between devices: 28.7 us -> none  [shards(): pack = lax.psum(pack, ('expert', 'context')).astype(F32)]
    all_gather x2 -> x0, blocking collectives: 16 us -> none  [the longest x1 8.04 us: shards(): in_b = lax.all_gather(b_in.astype(BF), 'dp', axis=1, tiled=True).astype(F32)]
    all_to_all x8 -> x5, starting transfers between devices: 33.8 us -> 19.1 us  [exchange(): lax.all_to_all(rows, 'expert', split_axis=0, concat_axis=0, tiled=True)]
    all_gather x3 -> x2, waiting for transfers between devices: 12.3 us -> 0.02 us  [the longest x1 0.02 us: shards(): in_w = lax.all_gather(in_w, 'dp', axis=1, tiled=True)]
    slice x11 -> x1, local copies, waits for them, and re-layouts: 11.8 us -> 0.61 us  [shards(): in_b[:, which][:, None]]
  transfers between devices with their start and end apart: 20 -> 13, of which waited for: 9 -> 4; matrix products, arithmetic and copies ran while one was open for 12% -> 8% of each run, Pallas kernels for 23% -> 31%
where the time goes in v2:
time: 492 us; the launch traced here: 484 us
  Pallas kernels  198 us (40%)
  blocking collectives  107 us (22%)
  waiting for transfers between devices  86.9 us (18%)
  local copies, waits for them, and re-layouts  33.9 us (7%)
  other arithmetic  22.9 us (5%)
  starting transfers between devices  20.3 us (4%)
  between operations  14.8 us (3%)
    all_to_all x3, blocking collectives, exchange(): lax.all_to_all(rows, 'expert', split_axis=0, concat_axis=0, tiled=True)  107 us
    all_to_all x5, waiting for transfers between devices, exchange(): lax.all_to_all(rows, 'expert', split_axis=0, concat_axis=0, tiled=True)  86 us
    pallas_call x2, Pallas kernels, shards(): call(partial(expert_kernel, cap, ff // dps), 'expert', (), [None] * 6, [(...  50.2 us
    pallas_call x1, Pallas kernels, shards(): comm_call(partial(reduce_kernel, dps, groups), 'reduce', 1, [V] * 7, [((r...  41.4 us
    pallas_call x1, Pallas kernels, shards(): call(partial(backward_kernel, experts, cap, cap_pad), 'backward', (images...  33 us
    pallas_call x1, Pallas kernels, shards(): comm_call(partial(start_kernel, dps), 'start', 0, [V] * 7, [((dps, rows,...  21.6 us
    all_to_all x5, starting transfers between devices, exchange(): lax.all_to_all(rows, 'expert', split_axis=0, concat_axis=0, tiled=True)  19.1 us
    pallas_call x1, Pallas kernels, shards(): call(partial(forward_kernel, half), 'forward', (images,), [row, row, ((1,...  16.9 us
  transfers between devices with their start and end apart: 13, of which 4 were waited for; matrix products, arithmetic and copies ran while one was open for 8% of the time, Pallas kernels for 31%

profile of v2, /device:TPU:0, one launch (start us, length us, event | category | flops | bytes accessed | tf_op | source)
XLA Modules:
  0.0 483.9 jit_solution(6796577452899470366)
XLA Ops:
  7.2 1.6 copy.31.w_router
  8.8 2.8 convert_element_type.12
  11.5 1.1 convert_element_type.13
  12.7 21.6 %start.1 = (bf16[4,128,1536]{2,1,0:T(8,128)(2,1)}, bf16[4,128,512]{2,1,0:T(8,128)(2,1)}, bf16[4,128,128]{2,1,0:T(8,128)(2,1)}, bf16[4,2,512]{2,1,0:T(2,128)(2,1)...) custom-call(bf16[888,512]{1,0:T(8,128)(2,1)} %bitcast.61, f32[128,1536]{1,0:T(8,128)} %w_qkv.1, ...), custom_call_target="tpu_custom_call" | custom-call | bytes 8388608 | tf_op jit(solution)/shard_map/start/pallas_call | solution.py:554
  34.3 0.0 all-gather.5.cloned.1.call-start
  34.3 0.7 all-gather.5.cloned.1.call-update
  35.0 0.6 bitcast_add_fusion.key_row
  35.6 0.1 slice_select_fusion.1
  35.7 0.1 pad_maximum_fusion.5
  35.8 0.6 broadcast_in_dim.15.bias
  36.4 0.7 copy.32.router
  37.1 0.2 copy.29
  37.3 0.8 iota_add_fusion.key_col
  38.1 7.6 %plan.1 = (s32[8,888]{1,0:T(8,128)}, bf16[8,336,512]{2,1,0:T(8,128)(2,1)}) custom-call(s32[2,888]{1,0:T(2,128)} %bitcast.83, s32[888,1]{1,0:T(8,128)} %iota_add_fusion.key_col, s32[1,888]{1,0:T(1,128)} %bitcast_add_fusion.key_row, bf16[888,512]{1,0:T(8,128)(2,1)} %bitcast.78), custom_call_target="tpu_custom_call" | custom-call | flops 2444230656 | bytes 5505024 | tf_op jit(solution)/shard_map/plan/pallas_call | solution.py:590
  45.8 16.9 %forward.1 = (bf16[888,512]{1,0:T(8,128)(2,1)}, bf16[3,608,512]{2,1,0:T(8,128)(2,1)}, bf16[3,608,512]{2,1,0:T(8,128)(2,1)}, bf16[3,8,296,608]{3,2,1,0:T(8,128)(2...) custom-call(bf16[888,512]{1,0:T(8,128)(2,1)} %bitcast.62, ...), custom_call_target="tpu_custom_call" | custom-call | flops 5004853248 | bytes 9093120 | tf_op jit(solution)/shard_map/forward/pallas_call | solution.py:619
  62.7 9.5 %dispatch.1 = bf16[8,336,512]{2,1,0:T(8,128)(2,1)} custom-call(bf16[888,512]{1,0:T(8,128)(2,1)} %get-tuple-element.63.acts.a_ref, bf16[8,512]{1,0:T(8,128)(2,1)} %copy.32.router, s32[2,888]{1,0:T(2,128)} %bitcast.84, s32[8,888]{1,0:T(8,128)} %get-tuple-element.57.slots), custom_call_target="tpu_custom_call" | custom-call | flops 2444230656 | bytes 5505024 | tf_op jit(solution)/shard_map/dispatch/pallas_call | solution.py:637
  72.2 3.5 slice_bitcast_fusion.7
  75.6 4.8 all-to-all-start
  80.4 3.1 slice_bitcast_fusion.6
  83.5 30.3 %all-to-all-done.got = bf16[4,336,512]{2,1,0:T(8,128)(2,1)S(1)} async-done(((bf16[4,336,512]{2,1,0:T(8,128)(2,1)}), bf16[4,336,512]{2,1,0:T(8,128)(2,1)S(1)}, u32[]{:S(2)}, u32[]{:S(2)}) %all-to-all-start) | async-done | bytes 1376288 | tf_op jit(solution)/shard_map/all_to_all | solution.py:602
  113.8 35.8 %all_to_all.40.got_grad = bf16[4,336,512]{2,1,0:T(8,128)(2,1)} all-to-all(bf16[4,336,512]{2,1,0:T(8,128)(2,1)S(1)} %get-tuple-element.128), channel_id=1, replica_groups=mesh['dp'=4,'expert'=4,'context'=2] {'expert'}, dimensions={0} | all-to-all | bytes 2752512 | tf_op jit(solution)/shard_map/all_to_all | solution.py:602
  149.6 3.5 all-to-all-start.3
  153.2 0.6 fusion.1
  153.8 0.6 fusion
  154.4 4.5 slice_bitcast_fusion.2
  158.9 26.2 %all-to-all-done.3.got = bf16[4,336,512]{2,1,0:T(8,128)(2,1)S(1)} async-done(((bf16[4,336,512]{2,1,0:T(8,128)(2,1)}), bf16[4,336,512]{2,1,0:T(8,128)(2,1)S(1)}, u32[]{:S(2)}, u32[]{:S(2)}) %all-to-all-start.3) | async-done | bytes 1376288 | tf_op jit(solution)/shard_map/all_to_all | solution.py:602
  185.2 3.5 all-to-all-start.4
  188.7 0.3 reduce-scatter.5.cloned.1.call-start
  189.0 4.8 slice_bitcast_fusion.3
  193.8 25.1 %expert.2 = (bf16[4,336,512]{2,1,0:T(8,128)(2,1)}, bf16[4,336,512]{2,1,0:T(8,128)(2,1)}, bf16[512,2048]{1,0:T(8,128)(2,1)}, f32[1,2048]{1,0:T(1,128)}, bf16[2048,512]{1,0:T(8,128)(2,1)}, /*index=5*/f32[1,512]{1,0:T(1,128)}) custom-call(bf16[4,336,512]{2,1,0:T(8,128)(2,1)} %copy-done.7, bf16[4,336,512]{2,1,0:T(8,128)(2,1)} %all_to_all.40.got_grad, ...), custom_call_target="tpu_custom_call" | custom-call | flops 16911433728 | bytes 13893632 | tf_op jit(solution)/shard_map/expert/pallas_call | solution.py:653
  218.9 2.0 all-to-all-done.4.got_grad
  220.9 1.1 copy-done.8
  222.0 25.1 %expert.3 = (bf16[4,336,512]{2,1,0:T(8,128)(2,1)}, bf16[4,336,512]{2,1,0:T(8,128)(2,1)}, bf16[512,2048]{1,0:T(8,128)(2,1)}, f32[1,2048]{1,0:T(1,128)}, bf16[2048,512]{1,0:T(8,128)(2,1)}, /*index=5*/f32[1,512]{1,0:T(1,128)}) custom-call(bf16[4,336,512]{2,1,0:T(8,128)(2,1)} %copy-done.5, bf16[4,336,512]{2,1,0:T(8,128)(2,1)} %copy-done.8, ...), custom_call_target="tpu_custom_call" | custom-call | flops 16911433728 | bytes 13893632 | tf_op jit(solution)/shard_map/expert/pallas_call | solution.py:653
  247.1 3.9 pad_maximum_fusion.1
  251.0 3.7 all-to-all-start.6
  254.7 0.3 reduce-scatter.3.cloned.1.call-start
  255.0 4.4 pad_maximum_fusion
  259.4 27.5 %all-to-all-done.6 = bf16[4,336,512]{2,1,0:T(8,128)(2,1)S(1)} async-done(((bf16[4,336,512]{2,1,0:T(8,128)(2,1)}), bf16[4,336,512]{2,1,0:T(8,128)(2,1)S(1)}, u32[]{:S(2)}, u32[]{:S(2)}) %all-to-all-start.6) | async-done | bytes 1376288 | tf_op jit(solution)/shard_map/all_to_all | solution.py:602
  286.9 36.6 %all_to_all.41 = bf16[4,336,512]{2,1,0:T(8,128)(2,1)} all-to-all(bf16[4,336,512]{2,1,0:T(8,128)(2,1)} %get-tuple-element.74), channel_id=1, replica_groups=mesh['dp'=4,'expert'=4,'context'=2] {'expert'}, dimensions={0} | all-to-all | bytes 2752512 | tf_op jit(solution)/shard_map/all_to_all | solution.py:602
  323.5 34.6 %all_to_all.42 = bf16[4,336,512]{2,1,0:T(8,128)(2,1)S(1)} all-to-all(bf16[4,336,512]{2,1,0:T(8,128)(2,1)S(1)} %copy-done.6), channel_id=1, replica_groups=mesh['dp'=4,'expert'=4,'context'=2] {'expert'}, dimensions={0} | all-to-all | bytes 2752512 | tf_op jit(solution)/shard_map/all_to_all | solution.py:602
  358.2 3.5 all-to-all-start.5
  361.7 0.0 all-gather.11.cloned.1.call-start
  361.8 1.0 copy.30
  362.8 2.0 pad_maximum_fusion.3
  364.8 1.8 copy.38
  366.6 33.0 %backward.1 = (f32[888,512]{1,0:T(8,128)}, bf16[888,512]{1,0:T(8,128)(2,1)}, bf16[2,888,512]{2,1,0:T(8,128)(2,1)}, bf16[2,888,512]{2,1,0:T(8,128)(2,1)}, f32[512...) custom-call(bf16[888,512]{1,0:T(8,128)(2,1)} %bitcast.79, bf16[2688,512]{1,0:T(8,128)(2,1)} %bitcast.64, ...), custom_call_target="tpu_custom_call" | custom-call | flops 7798259712 | bytes 13639680 | tf_op jit(solution)/shard_map/backward/pallas_call | solution.py:697
  399.7 2.3 slice_bitcast_fusion.9
  402.0 1.0 slice_bitcast_fusion.8
  403.0 0.5 collective-permute-start.1
  403.6 0.6 pad_maximum_fusion.6.b_back
  404.2 0.6 pad_maximum_fusion.4.b_in
  404.8 0.3 pad_maximum_fusion.2
  405.0 1.8 copy.37
  406.8 6.4 %combine.1 = bf16[888,512]{1,0:T(8,128)(2,1)} custom-call(s32[888,8]{1,0:T(8,128)} %bitcast.75, bf16[2688,512]{1,0:T(8,128)(2,1)} %bitcast.67, f32[888,512]{1,0:T(8,128)} %get-tuple-element.72.h_ref), custom_call_target="tpu_custom_call" | custom-call | flops 2444230656 | bytes 4546560 | tf_op jit(solution)/shard_map/combine/pallas_call | solution.py:733
  413.2 11.5 %input.1 = (bf16[888,512]{1,0:T(8,128)(2,1)}, f32[512,1536]{1,0:T(8,128)}, f32[8,512]{1,0:T(8,128)}) custom-call(bf16[888,512]{1,0:T(8,128)(2,1)} %bitcast.63, f32[888,512]{1,0:T(8,128)} %get-tuple-element.80.dh_ref, bf16[888,512]{1,0:T(8,128)(2,1)} %get-tuple-element.81.dq_ref, bf16[2,888,512]{2,1,0:T(8,128)(2,1)} %get-tuple-element.82.dk_own, ...), custom_call_target="tpu_custom_call" | custom-call | flops 2793406464 | bytes 9093120 | tf_op jit(solution)/shard_map/input/pallas_call | solution.py:719
  424.7 41.4 %reduce.1 = (f32[128,1536]{1,0:T(8,128)}, f32[128,512]{1,0:T(8,128)}, f32[128,8]{1,0:T(8,128)}, f32[7,128]{1,0:T(8,128)}, f32[2,512]{1,0:T(2,128)}, /*index=5*/f32[2,128]{1,0:T(2,128)}) custom-call(f32[512,1536]{1,0:T(8,128)} %get-tuple-element.85.g_qkv, f32[512,512]{1,0:T(8,128)} %get-tuple-element.86.g_out, f32[512,128]{1,0:T(8,128)} %get-tuple-element.87.g_router, ...), custom_call_target="tpu_custom_call" | custom-call | bytes 22282240 | tf_op jit(solution)/shard_map/reduce/pallas_call | solution.py:746
  466.1 1.5 copy.39
  467.6 2.8 convert_element_type.15
  470.4 2.9 convert_element_type.14
  473.3 0.6 copy.49
  473.9 0.9 copy.50
  474.8 0.7 copy.51
  475.5 0.6 copy.52
  476.1 0.6 copy.53
  (68 shorter events, 0.3 us)
Async XLA Ops:
  7.2 4.4 copy-start.2
  7.2 147.2 %all-gather.7.cloned.1.call-start = ((), (), s32[]{:S(2)}) async-start(), calls=%async_computation.11 | async-start | bytes 5242880 | tf_op jit(solution)/shard_map/all_gather | solution.py:585
  12.7 22.4 %copy-start.14 = (s32[1,1,888]{2,1,0:T(1,128)S(1)}, s32[1,1,888]{2,1,0:T(1,128)}, u32[]{:S(2)}) copy-start(s32[1,1,888]{2,1,0:T(1,128)} %param.16) | copy-start | bytes 10660
  12.7 23.0 %copy-start.15 = (s32[3,592]{1,0:T(4,128)S(1)}, s32[3,592]{1,0:T(4,128)}, u32[]{:S(2)}) copy-start(s32[3,592]{1,0:T(4,128)} %param.14) | copy-start | bytes 21316
  34.2 2.2 copy-start.11
  34.3 154.7 %all-gather.5.cloned.1.call-start = ((), (), s32[]{:S(2)}) async-start(), calls=%async_computation.10 | async-start | bytes 5242880 | tf_op jit(solution)/shard_map/all_gather | solution.py:584
  75.6 38.2 %all-to-all-start = ((bf16[4,336,512]{2,1,0:T(8,128)(2,1)}), bf16[4,336,512]{2,1,0:T(8,128)(2,1)S(1)}, u32[]{:S(2)}, u32[]{:S(2)}) async-start(bf16[4,336,512]{2,1,0:T(8,128)(2,1)} %get-tuple-element.130), calls=%async_computation | async-start | bytes 2752512 | tf_op jit(solution)/shard_map/all_to_all | solution.py:602
  113.8 35.8 %copy-start.7 = (bf16[4,336,512]{2,1,0:T(8,128)(2,1)}, bf16[4,336,512]{2,1,0:T(8,128)(2,1)S(1)}, u32[]{:S(2)}) copy-start(bf16[4,336,512]{2,1,0:T(8,128)(2,1)S(1)} %all-to-all-done.got) | copy-start | bytes 4128772
  113.8 39.4 %copy-start.18 = (f32[2,512]{1,0:T(2,128)S(1)}, f32[2,512]{1,0:T(2,128)}, u32[]{:S(2)}) copy-start(f32[2,512]{1,0:T(2,128)} %get-tuple-element.69) | copy-start | bytes 12292
  113.8 40.0 %copy-start.12 = (bf16[4,2,512]{2,1,0:T(2,128)(2,1)S(1)}, bf16[4,2,512]{2,1,0:T(2,128)(2,1)}, u32[]{:S(2)}) copy-start(bf16[4,2,512]{2,1,0:T(2,128)(2,1)} %get-tuple-element.67) | copy-start | bytes 24580
  149.6 35.5 %all-to-all-start.3 = ((bf16[4,336,512]{2,1,0:T(8,128)(2,1)}), bf16[4,336,512]{2,1,0:T(8,128)(2,1)S(1)}, u32[]{:S(2)}, u32[]{:S(2)}) async-start(bf16[4,336,512]{2,1,0:T(8,128)(2,1)} %get-tuple-element.131), calls=%async_computation.3 | async-start | bytes 2752512 | tf_op jit(solution)/shard_map/all_to_all | solution.py:602
  185.1 8.7 %copy-start.5 = (bf16[4,336,512]{2,1,0:T(8,128)(2,1)}, bf16[4,336,512]{2,1,0:T(8,128)(2,1)S(1)}, u32[]{:S(2)}) copy-start(bf16[4,336,512]{2,1,0:T(8,128)(2,1)S(1)} %all-to-all-done.3.got) | copy-start | bytes 4128772
  185.2 35.8 %all-to-all-start.4 = ((bf16[4,336,512]{2,1,0:T(8,128)(2,1)}), bf16[4,336,512]{2,1,0:T(8,128)(2,1)S(1)}, u32[]{:S(2)}, u32[]{:S(2)}) async-start(bf16[4,336,512]{2,1,0:T(8,128)(2,1)} %get-tuple-element.129), calls=%async_computation.4 | async-start | bytes 2752512 | tf_op jit(solution)/shard_map/all_to_all | solution.py:602
  188.7 177.9 %reduce-scatter.5.cloned.1.call-start = ((), (), s32[]{:S(2)}) async-start(), calls=%async_computation.14 | async-start | bytes 4718592 | tf_op jit(solution)/shard_map/reduce_scatter | solution.py:689
  220.9 1.1 copy-start.8
  222.0 25.1 %copy-start.4 = (bf16[2048,512]{1,0:T(8,128)(2,1)S(1)}, bf16[2048,512]{1,0:T(8,128)(2,1)}, u32[]{:S(2)}) copy-start(bf16[2048,512]{1,0:T(8,128)(2,1)} %get-tuple-element.101) | copy-start | bytes 6291460
  251.0 4.0 copy-start.3
  251.0 35.9 %all-to-all-start.6 = ((bf16[4,336,512]{2,1,0:T(8,128)(2,1)}), bf16[4,336,512]{2,1,0:T(8,128)(2,1)S(1)}, u32[]{:S(2)}, u32[]{:S(2)}) async-start(bf16[4,336,512]{2,1,0:T(8,128)(2,1)} %get-tuple-element.73), calls=%async_computation.6 | async-start | bytes 2752512 | tf_op jit(solution)/shard_map/all_to_all | solution.py:602
  254.7 148.8 %reduce-scatter.3.cloned.1.call-start = ((), (), s32[]{:S(2)}) async-start(), calls=%async_computation.12 | async-start | bytes 4718592 | tf_op jit(solution)/shard_map/reduce_scatter | solution.py:689
  259.4 64.2 %copy-start.6 = (bf16[4,336,512]{2,1,0:T(8,128)(2,1)S(1)}, bf16[4,336,512]{2,1,0:T(8,128)(2,1)}, u32[]{:S(2)}) copy-start(bf16[4,336,512]{2,1,0:T(8,128)(2,1)} %get-tuple-element.70) | copy-start | bytes 4128772
  286.9 36.6 %copy-start = (bf16[4,336,512]{2,1,0:T(8,128)(2,1)}, bf16[4,336,512]{2,1,0:T(8,128)(2,1)S(1)}, u32[]{:S(2)}) copy-start(bf16[4,336,512]{2,1,0:T(8,128)(2,1)S(1)} %all-to-all-done.6) | copy-start | bytes 4128772
  323.5 38.2 %copy-start.13 = (s32[8,888]{1,0:T(8,128)S(1)}, s32[8,888]{1,0:T(8,128)}, u32[]{:S(2)}) copy-start(s32[8,888]{1,0:T(8,128)} %get-tuple-element.57.slots) | copy-start | bytes 85252
  358.2 46.6 %all-to-all-start.5 = ((bf16[4,336,512]{2,1,0:T(8,128)(2,1)}), bf16[4,336,512]{2,1,0:T(8,128)(2,1)S(1)}, u32[]{:S(2)}, u32[]{:S(2)}) async-start(bf16[4,336,512]{2,1,0:T(8,128)(2,1)} %get-tuple-element.71), calls=%async_computation.5 | async-start | bytes 2752512 | tf_op jit(solution)/shard_map/all_to_all | solution.py:602
  361.7 105.8 %all-gather.11.cloned.1.call-start = ((), (), s32[]{:S(2)}) async-start(), calls=%async_computation.15 | async-start | bytes 1572864 | tf_op jit(solution)/shard_map/all_gather | solution.py:690
  366.6 103.9 %all-gather.9.cloned.1.call-start = ((), (), s32[]{:S(2)}) async-start(), calls=%async_computation.13 | async-start | bytes 1572864 | tf_op jit(solution)/shard_map/all_gather | solution.py:690
  399.7 2.3 copy-start.1
  399.7 3.8 copy-start.21
  399.7 3.8 copy-start.22
  399.7 4.4 copy-start.16
  399.7 4.4 copy-start.17
  402.0 11.2 %collective-permute-start = (bf16[888,512]{1,0:T(8,128)(2,1)}, bf16[888,512]{1,0:T(8,128)(2,1)}, u32[]{:S(2)}, u32[]{:S(2)}) collective-permute-start(bf16[888,512]{1,0:T(8,128)(2,1)} %slice_bitcast_fusion.9), channel_id=1, source_target_pairs={{0,1},{1,0},{2,3},{3,2},{4,5},{5,4},{6,7},{7,6},{8,9},{9,8},{10,11... | collective-permute-start | bytes 2727944 | tf_op jit(solution)/shard_map/ppermute | solution.py:716
  403.0 10.2 %collective-permute-start.1 = (bf16[888,512]{1,0:T(8,128)(2,1)}, bf16[888,512]{1,0:T(8,128)(2,1)}, u32[]{:S(2)}, u32[]{:S(2)}) collective-permute-start(bf16[888,512]{1,0:T(8,128)(2,1)} %slice_bitcast_fusion.8), channel_id=1, source_target_pairs={{0,1},{1,0},{2,3},{3,2},{4,5},{5,4},{6,7},{7,6},{8,9},{9,8},{10,11... | collective-permute-start | bytes 2727944 | tf_op jit(solution)/shard_map/ppermute | solution.py:717
  470.4 2.9 copy-start.20
  470.4 3.5 copy-start.9
  470.4 4.4 copy-start.10
  470.4 5.1 %copy-start.19 = (f32[2,512]{1,0:T(2,128)S(1)}, f32[2,512]{1,0:T(2,128)}, u32[]{:S(2)}) copy-start(f32[2,512]{1,0:T(2,128)} %get-tuple-element.155) | copy-start | bytes 12292
  470.4 5.7 %copy-start.23 = (f32[2,128]{1,0:T(2,128)S(1)}, f32[2,128]{1,0:T(2,128)}, u32[]{:S(2)}) copy-start(f32[2,128]{1,0:T(2,128)} %get-tuple-element.157) | copy-start | bytes 3076
Sparse Core Ops, SparseCore 0:
  34.4 53.9 all-gather.6
  90.2 52.6 all-gather.4
  251.1 50.6 reduce-scatter.4
  305.4 51.3 reduce-scatter.2
  366.7 10.3 all-gather.10
  403.7 10.3 all-gather.8

commit v3 on v2

--- a/solution.py
+++ b/solution.py
@@ -100,86 +100,195 @@
     send[0] = nn(one_hot, grad[...]).astype(BF)
 
 
-def dispatch_kernel(experts, cap, cap_pad, acts, router, routes, slots, send, gates):
-    expert = pl.program_id(0)
-    tokens, width = acts.shape
-    lanes = up(cap_pad, LANES)
-
-    @pl.when(expert == 0)
-    def _():
-        logits = nt(router[...], acts[...])
-        logits = jnp.exp(logits - jnp.max(logits, axis=0, keepdims=True))
-        probs = logits / jnp.sum(logits, axis=0, keepdims=True)
-        ids = iota((experts, tokens), 0)
-        for choice in range(2):
-            gate = jnp.sum(jnp.where(routes[choice : choice + 1, :] == ids, probs, 0.0), axis=0, keepdims=True)
-            high, mid, low = split3(gate)
-            gates[choice] = jnp.concatenate([high, mid, low, jnp.zeros((5, tokens), F32)], axis=0)
-
-    own = iota((lanes, tokens), 0) + expert * cap_pad
-    hit_first = own == slots[0:1, :]
-    hit_second = own == slots[1:2, :]
-    one_first = jnp.where(hit_first, 1.0, 0.0).astype(BF)
-    one_second = jnp.where(hit_second, 1.0, 0.0).astype(BF)
-    rows = nn((one_first + one_second)[:cap_pad], acts[...])
-    gate = nt(gates[0].astype(BF), one_first) + nt(gates[1].astype(BF), one_second)
-    gate = jnp.concatenate([gate, jnp.zeros((8, width - lanes), F32)], axis=1)
-    at = iota((cap_pad, 1), 0) - cap
-    for part in range(3):
-        rows = jnp.where(at == part, gate[part : part + 1, :], rows)
-    send[0] = rows.astype(BF)
-
-
 def gelu_parts(z):
     share = 0.5 * (1.0 + lax.erf(z * 0.7071067811865476))
     slope = share + z * (0.3989422804014327 * jnp.exp(-0.5 * z * z))
     return z * share, slope
 
 
-def expert_kernel(
-    cap, chunk, got, got_grad, w_in, b_in, w_back, b_back,
-    out_rows, out_back, grad_in, grad_b_in, grad_back, grad_b_back,
-    acts, hidden, slope, delta, grad_pre,
+def experts_kernel(
+    groups, cap, acts, router, routes, slots, send_grad, w_in, b_in, w_back, b_back,
+    table, out_rows, g_in, g_b_in, g_back, g_b_back,
+    gates, a_send, a_recv, g_recv, d_send, w_in_v, w_back_v, rows_v, hidden, grad_pre, delta, slope, g_in_v, g_back_v,
+    a_s, a_r, g_s, g_r, d_s, d_r, w_sem, out_sem,
 ):
-    groups, cap_pad, width = got.shape
-    ff = w_in.shape[1]
+    dp, group, core = lax.axis_index("dp"), lax.axis_index("expert"), lax.axis_index("context")
+    own, _, cap_pad, width = a_send.shape
+    tokens = acts.shape[0]
+    experts = groups * own
+    ff = w_in_v.shape[1]
+    chunk = b_in.shape[3]
     lanes = up(cap_pad, LANES)
     at = iota((cap_pad, 1), 0)
     same = at == iota((1, lanes), 1)
-    for src in range(groups):
-        rows = pl.ds(src * cap_pad, cap_pad)
-        block = got[src]
-        acts[rows, :] = jnp.where(at < cap, block.astype(F32), 0.0).astype(BF)
-        wide = block.astype(F32)
-        gate = wide[cap : cap + 1, :lanes] + wide[cap + 1 : cap + 2, :lanes] + wide[cap + 2 : cap + 3, :lanes]
-        gate = jnp.sum(jnp.where(same, gate, 0.0), axis=1, keepdims=True)
-        delta[rows, :] = (gate * got_grad[src].astype(F32)).astype(BF)
-        for lo in range(0, ff, chunk):
-            cols = pl.ds(lo, chunk)
-            z = nn(acts[rows, :], w_in[:, cols]) + b_in[lo // chunk].astype(F32)
-            value, rise = gelu_parts(z)
-            hidden[rows, cols] = value.astype(BF)
-            slope[rows, cols] = rise.astype(BF)
-        made = (nn(hidden[rows, :], w_back[...]) + b_back[...]).astype(BF).astype(F32)
-        out_rows[src] = (gate * made).astype(BF)
-        dot = jnp.sum(made * got_grad[src].astype(F32), axis=1, keepdims=True)
-        dot = jnp.sum(jnp.where(same, dot, 0.0), axis=0, keepdims=True)
-        parts = split3(jnp.concatenate([dot, jnp.zeros((1, width - lanes), F32)], axis=1))
-        for lo in range(0, ff, chunk):
-            cols = pl.ds(lo, chunk)
-            dz = nt(delta[rows, :], w_back[cols, :]) * slope[rows, cols].astype(F32)
-            total = jnp.sum(dz, axis=0, keepdims=True)
-            grad_b_in[:, cols] = total if src == 0 else grad_b_in[:, cols] + total
-            grad_pre[rows, cols] = dz.astype(BF)
-        back = nt(grad_pre[rows, :], w_in[...])
+
+    def device(step):
+        return (dp, lax.rem(group + step, groups), core)
+
+    def remote(src, dst, sems, slot, target):
+        return pltpu.make_async_remote_copy(
+            src_ref=src, dst_ref=dst, send_sem=sems[0].at[slot], recv_sem=sems[1].at[slot],
+            device_id=target, device_id_type=MESH,
+        )
+
+    def rows_out(which, step):
+        return remote(a_send.at[which, step], a_recv.at[which, step], (a_s, a_r), which * groups + step, device(step))
+
+    def grad_out(which, step):
+        expert = lax.rem(group + step, groups) * own + which
+        return remote(send_grad.at[expert], g_recv.at[which, step], (g_s, g_r), which * groups + step, device(step))
+
+    def back_out(which, step):
+        target = (dp, lax.rem(group - step + groups, groups), core)
+        place = table.at[group * own + which]
+        return remote(d_send.at[which, step], place, (d_s, d_r), which * groups + step, target)
+
+    def load(which):
+        return (
+            pltpu.make_async_copy(w_in.at[which], w_in_v, w_sem.at[0]),
+            pltpu.make_async_copy(w_back.at[which], w_back_v, w_sem.at[1]),
+        )
+
+    def store(which):
+        return (
+            pltpu.make_async_copy(g_in_v, g_in.at[which], out_sem.at[0]),
+            pltpu.make_async_copy(g_back_v, g_back.at[which], out_sem.at[1]),
+        )
+
+    greet([device(step) for step in range(1, groups)])
+    for copy in load(0):
+        copy.start()
+    logits = nt(router[...], acts[...])
+    logits = jnp.exp(logits - jnp.max(logits, axis=0, keepdims=True))
+    probs = logits / jnp.sum(logits, axis=0, keepdims=True)
+    ids = iota((experts, tokens), 0)
+    for choice in range(2):
+        gate = jnp.sum(jnp.where(routes[choice : choice + 1, :] == ids, probs, 0.0), axis=0, keepdims=True)
+        gates[choice] = jnp.concatenate(list(split3(gate)) + [jnp.zeros((5, tokens), F32)], axis=0)
+
+    def dispatch(turn, _):
+        which = turn // groups
+        step = lax.rem(turn + 1, groups)
+        expert = lax.rem(group + step, groups) * own + which
+        ids = iota((lanes, tokens), 0) + expert * cap_pad
+        first = jnp.where(ids == slots[0:1, :], 1.0, 0.0).astype(BF)
+        second = jnp.where(ids == slots[1:2, :], 1.0, 0.0).astype(BF)
+        rows = nn((first + second)[:cap_pad], acts[...])
+        gate = nt(gates[0].astype(BF), first) + nt(gates[1].astype(BF), second)
+        gate = jnp.concatenate([gate, jnp.zeros((8, width - lanes), F32)], axis=1)
         for part in range(3):
-            back = jnp.where(at == cap + part, parts[part], back)
-        out_back[src] = back.astype(BF)
-    grad_b_back[...] = jnp.sum(delta[...].astype(F32), axis=0, keepdims=True)
-    for lo in range(0, ff, chunk):
-        cols = pl.ds(lo, chunk)
-        grad_back[cols, :] = tn(hidden[:, cols], delta[...]).astype(BF)
-        grad_in[:, cols] = tn(acts[...], grad_pre[:, cols]).astype(BF)
+            rows = jnp.where(at == cap + part, gate[part : part + 1, :], rows)
+        rows = rows.astype(BF)
+
+        @pl.when(step > 0)
+        def _():
+            a_send[which, step] = rows
+            rows_out(which, step).start()
+            grad_out(which, step).start()
+
+        @pl.when(step == 0)
+        def _():
+            a_recv[which, 0] = rows
+            g_recv[which, 0] = send_grad[expert]
+
+        return 0
+
+    lax.fori_loop(0, own * groups, dispatch, 0)
+
+    def expert(which, _):
+        for copy in load(which):
+            copy.wait()
+
+        def block(step, _):
+            @pl.when(step > 0)
+            def _():
+                rows_out(which, step).wait_recv()
+
+            src = lax.rem(group - step + groups, groups)
+            rows = pl.ds(pl.multiple_of(step * cap_pad, 16), cap_pad)
+            got = a_recv[which, step].astype(F32)
+            acts_in = jnp.where(at < cap, got, 0.0).astype(BF)
+            rows_v[rows, :] = acts_in
+            gate = got[cap : cap + 1, :lanes] + got[cap + 1 : cap + 2, :lanes] + got[cap + 2 : cap + 3, :lanes]
+            gate = jnp.sum(jnp.where(same, gate, 0.0), axis=1, keepdims=True)
+            for part in range(ff // chunk):
+                cols = slice(part * chunk, (part + 1) * chunk)
+                z = nn(acts_in, w_in_v[:, cols]) + b_in[part, which].astype(F32)
+                value, rise = gelu_parts(z)
+                hidden[rows, cols] = value.astype(BF)
+                slope[:, cols] = rise.astype(BF)
+            made = (nn(hidden[rows, :], w_back_v[...]) + b_back[which]).astype(BF).astype(F32)
+            out_rows[src, which] = (gate * made).astype(BF)
+
+            @pl.when(step > 0)
+            def _():
+                grad_out(which, step).wait_recv()
+
+            got_grad = g_recv[which, step].astype(F32)
+            low = (gate * got_grad).astype(BF)
+            delta[rows, :] = low
+            dot = jnp.sum(made * got_grad, axis=1, keepdims=True)
+            dot = jnp.sum(jnp.where(same, dot, 0.0), axis=0, keepdims=True)
+            parts = split3(jnp.concatenate([dot, jnp.zeros((1, width - lanes), F32)], axis=1))
+            for part in range(ff // chunk):
+                cols = slice(part * chunk, (part + 1) * chunk)
+                dz = nt(low, w_back_v[cols, :]) * slope[:, cols].astype(F32)
+                so_far = jnp.where(step > 0, g_b_in[which, :, cols], 0.0)
+                g_b_in[which, :, cols] = so_far + jnp.sum(dz, axis=0, keepdims=True)
+                grad_pre[rows, cols] = dz.astype(BF)
+            back = nt(grad_pre[rows, :], w_in_v[...])
+            for part in range(3):
+                back = jnp.where(at == cap + part, parts[part], back)
+            back = back.astype(BF)
+
+            @pl.when(step > 0)
+            def _():
+                d_send[which, step] = back
+                back_out(which, step).start()
+
+            @pl.when(step == 0)
+            def _():
+                table[group * own + which] = back
+
+            return 0
+
+        lax.fori_loop(0, groups, block, 0)
+
+        @pl.when(which + 1 < own)
+        def _():
+            for copy in load(which + 1):
+                copy.start()
+
+        @pl.when(which > 0)
+        def _():
+            for copy in store(which - 1):
+                copy.wait()
+
+        g_b_back[which] = jnp.sum(delta[...].astype(F32), axis=0, keepdims=True)
+
+        def weights(part, _):
+            cols = pl.ds(pl.multiple_of(part * chunk, LANES), chunk)
+            g_back_v[cols, :] = tn(hidden[:, cols], delta[...]).astype(BF)
+            g_in_v[:, cols] = tn(rows_v[...], grad_pre[:, cols]).astype(BF)
+            return 0
+
+        lax.fori_loop(0, ff // chunk, weights, 0)
+        for copy in store(which):
+            copy.start()
+        return 0
+
+    lax.fori_loop(0, own, expert, 0)
+    for copy in store(own - 1):
+        copy.wait()
+
+    def finish(turn, _):
+        which, step = turn // (groups - 1), 1 + lax.rem(turn, groups - 1)
+        rows_out(which, step).wait_send()
+        grad_out(which, step).wait_send()
+        back_out(which, step).wait()
+        return 0
+
+    lax.fori_loop(0, own * (groups - 1), finish, 0)
 
 
 def forward_kernel(half, x_own, x_other, bias, vec, w_qkv, w_out, q_ref, k_ref, v_ref, p_ref, o_ref, h_ref, a_ref):
@@ -598,14 +707,6 @@
     )(route_rows, keys[:, None], keys[None, :], grad)
     slot_cols = slots.T
 
-    def exchange(rows):
-        return lax.all_to_all(rows, "expert", split_axis=0, concat_axis=0, tiled=True)
-
-    def by_expert(rows, which):
-        return rows.reshape(groups, per_device, cap_pad, width)[:, which]
-
-    got_grad = [exchange(by_expert(send_grad, which)) for which in range(per_device)]
-
     mask = jnp.where(key_mask > 0, 0.0, -1e30).astype(F32)
     first, second = mask[:, :half], mask[:, half:]
     own = jnp.where(context == 0, first, second)
@@ -634,59 +735,49 @@
         moved=20 * tokens * width,
     )(x, x_other, bias, vec, qkv_all, out_all)
 
-    (send_rows,) = call(
-        partial(dispatch_kernel, experts, cap, cap_pad),
-        "dispatch",
-        (experts,),
-        [None] * 4,
-        [(block, ((experts, cap_pad, width), BF))],
-        scratch=[pltpu.VMEM((2, 8, tokens), F32)],
-        flops=2 * total * tokens * width,
-        moved=4 * total * width,
-    )(acts, router_rows, route_rows, slots)
-    got = [exchange(by_expert(send_rows, which)) for which in range(per_device)]
-
-    out_rows, back_rows, g_in, g_b_in, g_back, g_b_back = [], [], [], [], [], []
-    slab = (groups, cap_pad, width)
     rows_all = groups * cap_pad
-    for which in range(per_device):
-        made = call(
-            partial(expert_kernel, cap, ff // dps),
-            "expert",
-            (),
-            [None] * 6,
-            [
-                (None, (slab, BF)),
-                (None, (slab, BF)),
-                (None, ((width, ff), BF)),
-                (None, ((1, ff), F32)),
-                (None, ((ff, width), BF)),
-                (None, ((1, width), F32)),
-            ],
-            scratch=[
-                pltpu.VMEM((rows_all, width), BF),
-                pltpu.VMEM((rows_all, ff), BF),
-                pltpu.VMEM((rows_all, ff), BF),
-                pltpu.VMEM((rows_all, width), BF),
-                pltpu.VMEM((rows_all, ff), BF),
-            ],
-            flops=12 * rows_all * width * ff,
-            moved=8 * rows_all * width + 8 * width * ff,
-        )(
-            got[which], got_grad[which], in_w[which], in_b[:, which][:, None], back_w[which], back_b[which][None]
-        )
-        for kept, piece in zip((out_rows, back_rows, g_in, g_b_in, g_back, g_b_back), made):
-            kept.append(piece)
-
-    def returned(parts):
-        moved = [exchange(part) for part in parts]
-        return jnp.stack(moved, axis=1).reshape(total, width)
-
-    back_table = returned(back_rows)
-    out_table = returned(out_rows)
+    dma = pltpu.SemaphoreType.DMA
+    turns = per_device * groups
+    back_table, out_rows, g_in, g_b_in, g_back, g_b_back = comm_call(
+        partial(experts_kernel, groups, cap),
+        "experts",
+        2,
+        [V, V, V, V, V, A, V, A, V],
+        [
+            ((experts, cap_pad, width), BF, V),
+            ((groups, per_device, cap_pad, width), BF, V),
+            ((per_device, width, ff), BF, A),
+            ((per_device, 1, ff), F32, V),
+            ((per_device, ff, width), BF, A),
+            ((per_device, 1, width), F32, V),
+        ],
+        [
+            pltpu.VMEM((2, 8, tokens), F32),
+            pltpu.VMEM((per_device, groups, cap_pad, width), BF),
+            pltpu.VMEM((per_device, groups, cap_pad, width), BF),
+            pltpu.VMEM((per_device, groups, cap_pad, width), BF),
+            pltpu.VMEM((per_device, groups, cap_pad, width), BF),
+            pltpu.VMEM((width, ff), BF),
+            pltpu.VMEM((ff, width), BF),
+            pltpu.VMEM((rows_all, width), BF),
+            pltpu.VMEM((rows_all, ff), BF),
+            pltpu.VMEM((rows_all, ff), BF),
+            pltpu.VMEM((rows_all, width), BF),
+            pltpu.VMEM((cap_pad, ff), BF),
+            pltpu.VMEM((width, ff), BF),
+            pltpu.VMEM((ff, width), BF),
+        ]
+        + [dma((turns,))] * 6
+        + [dma((2,))] * 2,
+        flops=12 * per_device * rows_all * width * ff,
+        moved=8 * per_device * rows_all * width + 8 * per_device * width * ff,
+    )(acts, router_rows, route_rows, slots, send_grad, in_w, in_b[:, :, None], back_w, back_b[:, None])
+    back_table = back_table.reshape(total, width)
+    out_rows = out_rows.reshape(groups, per_device * cap_pad, width)
+    out_table = lax.all_to_all(out_rows, "expert", split_axis=0, concat_axis=0, tiled=True).reshape(total, width)
 
     def expert_sum(parts):
-        share = lax.psum_scatter(jnp.stack(parts), ("dp", "context"), scatter_dimension=1, tiled=True)
+        share = lax.psum_scatter(parts, ("dp", "context"), scatter_dimension=1, tiled=True)
         return lax.all_gather(share, "context", axis=1, tiled=True).astype(F32)
 
     grad_w_in = expert_sum(g_in)
@@ -741,7 +832,6 @@
     )(slot_cols, out_table, after)
 
     wide = 4 * width + LANES
-    dma = pltpu.SemaphoreType.DMA
     halves_of = rows // 2
     grad_qkv, grad_out, grad_router, grad_vec, grad_b_in, grad_b_back = comm_call(
         partial(reduce_kernel, dps, groups),
@@ -777,7 +867,7 @@
         moved=20 * width * wide,
     )(
         g_qkv, g_out, g_router, g_vec_one, g_vec_two,
-        jnp.concatenate(g_b_in, axis=0), jnp.concatenate(g_b_back, axis=0),
+        g_b_in[:, 0], g_b_back[:, 0],
     )
     return (
         output.reshape(images, half, width),

time: 492 us -> 514 us (1.045); the launches traced: 484 us -> 513 us
  Pallas kernels: 198 us -> 325 us
  blocking collectives: 107 us -> 0 us
  waiting for transfers between devices: 86.9 us -> 143 us
  local copies, waits for them, and re-layouts: 33.9 us -> 14 us
  starting transfers between devices: 20.3 us -> 5.37 us
  other arithmetic: 22.9 us -> 11.1 us
    pallas_call x3 -> x1, Pallas kernels: 59.7 us -> 188 us  [shards(): comm_call(partial(experts_kernel, groups, cap), 'experts', 2, [V, V, V, V...]
    all_to_all x3 -> x0, blocking collectives: 107 us -> none  [exchange(): lax.all_to_all(rows, 'expert', split_axis=0, concat_axis=0, tiled=True)]
    all_to_all x5 -> x1, waiting for transfers between devices: 86 us -> 0.01 us  [shards(): lax.all_to_all(out_rows, 'expert', split_axis=0, concat_axis=0, tiled=True)]
    reduce_scatter x2, waiting for transfers between devices: 0.01 us -> 62.9 us  [expert_sum(): lax.psum_scatter(parts, ('dp', 'context'), scatter_dimension=1, tiled=True)]
    all_gather x1, waiting for transfers between devices: 0.01 us -> 54.6 us  [shards(): back_w = lax.all_gather(back_w, 'dp', axis=1, tiled=True)]
    all_gather x1, waiting for transfers between devices: 0.02 us -> 24.3 us  [shards(): in_w = lax.all_gather(in_w, 'dp', axis=1, tiled=True)]
    squeeze x4 -> x0, local copies, waits for them, and re-layouts: 15.9 us -> none  [the longest x2 6.54 us: by_expert(): return rows.reshape(groups, per_device, cap_pad, width)[:, which]]
    all_to_all x5 -> x1, starting transfers between devices: 19.1 us -> 4.61 us  [shards(): lax.all_to_all(out_rows, 'expert', split_axis=0, concat_axis=0, tiled=True)]
  transfers between devices with their start and end apart: 13 -> 9, of which waited for: 4 -> 4; matrix products, arithmetic and copies ran while one was open for 8% -> 2% of each run, Pallas kernels for 31% -> 23%
where the time goes in v3:
time: 514 us; the launch traced here: 513 us
  Pallas kernels  325 us (63%)
  waiting for transfers between devices  143 us (28%)
  between operations  14.3 us (3%)
  local copies, waits for them, and re-layouts  14 us (3%)
  other arithmetic  11.1 us (2%)
  starting transfers between devices  5.37 us (1%)
    pallas_call x1, Pallas kernels, shards(): comm_call(partial(experts_kernel, groups, cap), 'experts', 2, [V, V, V, V...  188 us
    reduce_scatter x2, waiting for transfers between devices, expert_sum(): lax.psum_scatter(parts, ('dp', 'context'), scatter_dimension=1, tiled=True)  62.9 us
    all_gather x1, waiting for transfers between devices, shards(): back_w = lax.all_gather(back_w, 'dp', axis=1, tiled=True)  54.6 us
    pallas_call x1, Pallas kernels, shards(): comm_call(partial(reduce_kernel, dps, groups), 'reduce', 1, [V] * 7, [((r...  40.8 us
    pallas_call x1, Pallas kernels, shards(): call(partial(backward_kernel, experts, cap, cap_pad), 'backward', (images...  33.1 us
    all_gather x1, waiting for transfers between devices, shards(): in_w = lax.all_gather(in_w, 'dp', axis=1, tiled=True)  24.3 us
    pallas_call x1, Pallas kernels, shards(): comm_call(partial(start_kernel, dps), 'start', 0, [V] * 7, [((dps, rows,...  21.6 us
    pallas_call x1, Pallas kernels, shards(): call(partial(forward_kernel, half), 'forward', (images,), [row, row, ((1,...  16.9 us
  transfers between devices with their start and end apart: 9, of which 4 were waited for; matrix products, arithmetic and copies ran while one was open for 2% of the time, Pallas kernels for 23%

profile of v3, /device:TPU:0, one launch (start us, length us, event | category | flops | bytes accessed | tf_op | source)
XLA Modules:
  0.0 513.1 jit_solution(16927732266227954915)
XLA Ops:
  7.2 0.0 copy-start.1
  7.2 0.0 all-gather.5.cloned.1.call-start
  7.2 1.6 copy.29.w_router
  8.8 2.7 convert_element_type.12
  11.5 0.0 copy-done.1
  11.5 1.1 convert_element_type.13
  12.6 21.6 %start.1 = (bf16[4,128,1536]{2,1,0:T(8,128)(2,1)}, bf16[4,128,512]{2,1,0:T(8,128)(2,1)}, bf16[4,128,128]{2,1,0:T(8,128)(2,1)}, bf16[4,2,512]{2,1,0:T(2,128)(2,1)...) custom-call(bf16[888,512]{1,0:T(8,128)(2,1)} %bitcast.31, f32[128,1536]{1,0:T(8,128)} %w_qkv.1, ...), custom_call_target="tpu_custom_call" | custom-call | bytes 8388608 | tf_op jit(solution)/shard_map/start/pallas_call | solution.py:663
  34.2 0.0 copy-start.5
  34.2 0.0 copy-start.10
  34.2 0.0 all-gather.5.cloned.1.call-update
  34.3 0.0 all-gather.7.cloned.1.call-start
  34.3 0.7 all-gather.7.cloned.1.call-update
  35.0 0.0 reduce-scatter.3.cloned.1.call-start
  35.1 0.1 slice_select_fusion.1
  35.2 0.1 pad_maximum_fusion
  35.2 0.6 broadcast_in_dim.21.bias
  35.9 0.7 copy.30.router
  36.5 0.6 copy.31.b_in
  37.2 0.6 broadcast_in_dim.23.b_back
  37.8 0.2 copy.27
  38.0 0.6 bitcast_add_fusion.key_row
  38.6 0.8 iota_add_fusion.key_col
  39.4 7.7 %plan.1 = (s32[8,888]{1,0:T(8,128)}, bf16[8,336,512]{2,1,0:T(8,128)(2,1)}) custom-call(s32[2,888]{1,0:T(2,128)} %bitcast.48, s32[888,1]{1,0:T(8,128)} %iota_add_fusion.key_col, s32[1,888]{1,0:T(1,128)} %bitcast_add_fusion.key_row, bf16[888,512]{1,0:T(8,128)(2,1)} %bitcast.43), custom_call_target="tpu_custom_call" | custom-call | flops 2444230656 | bytes 5505024 | tf_op jit(solution)/shard_map/plan/pallas_call | solution.py:699
  47.0 16.9 %forward.1 = (bf16[888,512]{1,0:T(8,128)(2,1)}, bf16[3,608,512]{2,1,0:T(8,128)(2,1)}, bf16[3,608,512]{2,1,0:T(8,128)(2,1)}, bf16[3,8,296,608]{3,2,1,0:T(8,128)(2...) custom-call(bf16[888,512]{1,0:T(8,128)(2,1)} %bitcast.32, ...), custom_call_target="tpu_custom_call" | custom-call | flops 5004853248 | bytes 9093120 | tf_op jit(solution)/shard_map/forward/pallas_call | solution.py:720
  63.9 24.3 %all-gather.5.cloned.1.call-done.w_in = bf16[2,512,2048]{2,1,0:T(8,128)(2,1)} async-done(((bf16[2,128,2048]{2,1,0:T(8,128)(2,1)}), bf16[2,512,2048]{2,1,0:T(8,128)(2,1)}) %all-gather.5.cloned.1.call-update) | async-done | bytes 4194320 | tf_op jit(solution)/shard_map/all_gather | solution.py:693
  88.3 54.6 %all-gather.7.cloned.1.call-done.w_back = bf16[2,2048,512]{2,1,0:T(8,128)(2,1)} async-done(((bf16[2,512,512]{2,1,0:T(8,128)(2,1)}), bf16[2,2048,512]{2,1,0:T(8,128)(2,1)}) %all-gather.7.cloned.1.call-update) | async-done | bytes 4194320 | tf_op jit(solution)/shard_map/all_gather | solution.py:694
  142.9 187.7 %experts.1 = (bf16[8,336,512]{2,1,0:T(8,128)(2,1)}, bf16[4,2,336,512]{3,2,1,0:T(8,128)(2,1)}, bf16[2,512,2048]{2,1,0:T(8,128)(2,1)}, f32[2,1,2048]{2,1,0:T(1,128...) custom-call(bf16[888,512]{1,0:T(8,128)(2,1)} %get-tuple-element.57.acts.a_ref, bf16[8,512]{1,0:T(8,128)(2,1)} %copy.30.router, ...), custom_call_target="tpu_custom_call" | custom-call | flops 33822867456 | bytes 27787264 | tf_op jit(solution)/shard_map/experts/pallas_call | solution.py:741
  330.6 0.0 reduce-scatter.3.cloned.1.call-update
  330.6 0.0 reduce-scatter.5.cloned.1.call-start
  330.7 0.5 reduce-scatter.5.cloned.1.call-update
  331.2 0.0 copy-start.6
  331.2 4.6 all-to-all-start
  335.8 0.0 all-gather.9.cloned.1.call-start
  335.9 1.0 copy.28
  336.9 43.3 %reduce-scatter.3.cloned.1.call-done = bf16[2,64,2048]{2,1,0:T(8,128)(2,1)} async-done(((bf16[2,512,2048]{2,1,0:T(8,128)(2,1)}), bf16[2,64,2048]{2,1,0:T(8,128)(2,1)}) %reduce-scatter.3.cloned.1.call-update) | async-done | bytes 524304 | tf_op jit(solution)/shard_map/reduce_scatter | solution.py:780
  380.2 0.0 all-gather.9.cloned.1.call-update
  380.2 0.2 all-gather.11.cloned.1.call-start
  380.5 33.1 %backward.1 = (f32[888,512]{1,0:T(8,128)}, bf16[888,512]{1,0:T(8,128)(2,1)}, bf16[2,888,512]{2,1,0:T(8,128)(2,1)}, bf16[2,888,512]{2,1,0:T(8,128)(2,1)}, f32[512...) custom-call(bf16[888,512]{1,0:T(8,128)(2,1)} %bitcast.44, bf16[2688,512]{1,0:T(8,128)(2,1)} %bitcast.50, ...), custom_call_target="tpu_custom_call" | custom-call | flops 7798259712 | bytes 13639680 | tf_op jit(solution)/shard_map/backward/pallas_call | solution.py:788
  413.5 1.4 slice_bitcast_fusion.1
  414.9 0.1 collective-permute-start
  415.0 0.3 copy-done
  415.3 0.1 slice_bitcast_fusion
  415.3 0.3 collective-permute-start.1
  415.6 19.5 %reduce-scatter.5.cloned.1.call-done = bf16[2,256,512]{2,1,0:T(8,128)(2,1)} async-done(((bf16[2,2048,512]{2,1,0:T(8,128)(2,1)}), bf16[2,256,512]{2,1,0:T(8,128)(2,1)}) %reduce-scatter.5.cloned.1.call-update) | async-done | bytes 524304 | tf_op jit(solution)/shard_map/reduce_scatter | solution.py:780
  435.1 0.0 all-gather.11.cloned.1.call-update
  435.2 0.6 copy.37
  435.8 0.0 copy-done.11
  435.8 0.6 copy.38
  436.4 0.0 collective-permute-done.dk_got
  436.4 0.0 collective-permute-done.1.dv_got
  436.4 0.9 copy-done.2
  437.3 11.2 %input.1 = (bf16[888,512]{1,0:T(8,128)(2,1)}, f32[512,1536]{1,0:T(8,128)}, f32[8,512]{1,0:T(8,128)}) custom-call(bf16[888,512]{1,0:T(8,128)(2,1)} %bitcast.33, f32[888,512]{1,0:T(8,128)} %get-tuple-element.72.dh_ref, bf16[888,512]{1,0:T(8,128)(2,1)} %get-tuple-element.73.dq_ref, bf16[2,888,512]{2,1,0:T(8,128)(2,1)} %get-tuple-element.74.dk_own, ...), custom_call_target="tpu_custom_call" | custom-call | flops 2793406464 | bytes 9093120 | tf_op jit(solution)/shard_map/input/pallas_call | solution.py:810
  448.5 40.8 %reduce.1 = (f32[128,1536]{1,0:T(8,128)}, f32[128,512]{1,0:T(8,128)}, f32[128,8]{1,0:T(8,128)}, f32[7,128]{1,0:T(8,128)}, f32[2,512]{1,0:T(2,128)}, /*index=5*/f32[2,128]{1,0:T(2,128)}) custom-call(f32[512,1536]{1,0:T(8,128)} %get-tuple-element.77.g_qkv, f32[512,512]{1,0:T(8,128)} %get-tuple-element.78.g_out, f32[512,128]{1,0:T(8,128)} %get-tuple-element.79.g_router, ...), custom_call_target="tpu_custom_call" | custom-call | bytes 22282240 | tf_op jit(solution)/shard_map/reduce/pallas_call | solution.py:836
  489.3 1.5 copy.32
  490.8 0.0 all-to-all-done
  490.8 6.3 %combine.1 = bf16[888,512]{1,0:T(8,128)(2,1)} custom-call(s32[888,8]{1,0:T(8,128)} %bitcast.37, bf16[2688,512]{1,0:T(8,128)(2,1)} %bitcast.14.table, f32[888,512]{1,0:T(8,128)} %get-tuple-element.65.h_ref), custom_call_target="tpu_custom_call" | custom-call | flops 2444230656 | bytes 4546560 | tf_op jit(solution)/shard_map/combine/pallas_call | solution.py:824
  497.2 2.8 convert_element_type.14
  500.0 0.0 all-gather.11.cloned.1.call-done
  500.0 2.9 convert_element_type.15
  503.0 0.6 copy.44
  503.5 0.9 copy.45
  504.4 0.7 copy.46
  505.1 0.6 copy.47
  505.7 0.6 copy.48
  (29 shorter events, 0.1 us)
Async XLA Ops:
  7.2 4.3 copy-start.1
  7.2 81.1 %all-gather.5.cloned.1.call-start = ((), (), s32[]{:S(2)}) async-start(), calls=%async_computation.3 | async-start | bytes 5242880 | tf_op jit(solution)/shard_map/all_gather | solution.py:693
  12.6 22.5 %copy-start.9 = (s32[3,592]{1,0:T(4,128)S(1)}, s32[3,592]{1,0:T(4,128)}, u32[]{:S(2)}) copy-start(s32[3,592]{1,0:T(4,128)} %param.14) | copy-start | bytes 21316
  12.6 25.1 %copy-start.8 = (s32[1,1,888]{2,1,0:T(1,128)S(1)}, s32[1,1,888]{2,1,0:T(1,128)}, u32[]{:S(2)}) copy-start(s32[1,1,888]{2,1,0:T(1,128)} %param.16) | copy-start | bytes 10660
  34.2 1.6 copy-start.5
  34.2 2.3 copy-start.10
  34.2 2.9 copy-start.12
  34.3 108.6 %all-gather.7.cloned.1.call-start = ((), (), s32[]{:S(2)}) async-start(), calls=%async_computation.4 | async-start | bytes 5242880 | tf_op jit(solution)/shard_map/all_gather | solution.py:694
  35.0 345.2 %reduce-scatter.3.cloned.1.call-start = ((), (), s32[]{:S(2)}) async-start(), calls=%async_computation.5 | async-start | bytes 4718592 | tf_op jit(solution)/shard_map/reduce_scatter | solution.py:780
  330.6 104.5 %reduce-scatter.5.cloned.1.call-start = ((), (), s32[]{:S(2)}) async-start(), calls=%async_computation.7 | async-start | bytes 4718592 | tf_op jit(solution)/shard_map/reduce_scatter | solution.py:780
  331.2 4.7 copy-start.6
  331.2 159.6 %all-to-all-start = ((bf16[4,672,512]{2,1,0:T(8,128)(2,1)}), bf16[4,672,512]{2,1,0:T(8,128)(2,1)}, u32[]{:S(2)}, u32[]{:S(2)}) async-start(bf16[4,672,512]{2,1,0:T(8,128)(2,1)} %bitcast.13), calls=%async_computation | async-start | bytes 5505024 | tf_op jit(solution)/shard_map/all_to_all | solution.py:777
  335.8 161.4 %all-gather.9.cloned.1.call-start = ((), (), s32[]{:S(2)}) async-start(), calls=%async_computation.6 | async-start | bytes 1572864 | tf_op jit(solution)/shard_map/all_gather | solution.py:781
  380.2 119.8 %all-gather.11.cloned.1.call-start = ((), (), s32[]{:S(2)}) async-start(), calls=%async_computation.8 | async-start | bytes 1572864 | tf_op jit(solution)/shard_map/all_gather | solution.py:781
  413.5 1.8 copy-start
  413.5 21.6 %copy-start.7 = (f32[2,1,2048]{2,1,0:T(1,128)S(1)}, f32[2,1,2048]{2,1,0:T(1,128)}, u32[]{:S(2)}) copy-start(f32[2,1,2048]{2,1,0:T(1,128)} %get-tuple-element.82) | copy-start | bytes 49156
  413.5 22.3 %copy-start.11 = (f32[2,1,512]{2,1,0:T(1,128)S(1)}, f32[2,1,512]{2,1,0:T(1,128)}, u32[]{:S(2)}) copy-start(f32[2,1,512]{2,1,0:T(1,128)} %get-tuple-element.83) | copy-start | bytes 12292
  414.9 21.5 %collective-permute-start = (bf16[888,512]{1,0:T(8,128)(2,1)S(1)}, bf16[888,512]{1,0:T(8,128)(2,1)S(1)}, u32[]{:S(2)}, u32[]{:S(2)}) collective-permute-start(bf16[888,512]{1,0:T(8,128)(2,1)S(1)} %slice_bitcast_fusion.1), channel_id=1, source_target_pairs={{0,1},{1,0},{2,3},{3,2},{4,5},{5,4},{6,7},{7,6},{8,9},{9,8},{10,11... | collective-permute-start | bytes 2727944 | tf_op jit(solution)/shard_map/ppermute | solution.py:807
  415.3 21.1 %collective-permute-start.1 = (bf16[888,512]{1,0:T(8,128)(2,1)S(1)}, bf16[888,512]{1,0:T(8,128)(2,1)}, u32[]{:S(2)}, u32[]{:S(2)}) collective-permute-start(bf16[888,512]{1,0:T(8,128)(2,1)S(1)} %slice_bitcast_fusion), channel_id=1, source_target_pairs={{0,1},{1,0},{2,3},{3,2},{4,5},{5,4},{6,7},{7,6},{8,9},{9,8},{10,11... | collective-permute-start | bytes 2727944 | tf_op jit(solution)/shard_map/ppermute | solution.py:808
  436.4 0.9 copy-start.2
  500.0 3.0 copy-start.14
  500.0 3.6 copy-start.3
  500.0 4.4 copy-start.4
  500.0 5.1 %copy-start.13 = (f32[2,512]{1,0:T(2,128)S(1)}, f32[2,512]{1,0:T(2,128)}, u32[]{:S(2)}) copy-start(f32[2,512]{1,0:T(2,128)} %get-tuple-element.131) | copy-start | bytes 12292
  500.0 5.7 %copy-start.15 = (f32[2,128]{1,0:T(2,128)S(1)}, f32[2,128]{1,0:T(2,128)}, u32[]{:S(2)}) copy-start(f32[2,128]{1,0:T(2,128)} %get-tuple-element.133) | copy-start | bytes 3076
Sparse Core Ops, SparseCore 0:
  34.4 53.8 all-gather.4
  90.1 52.6 all-gather.6
  330.7 49.4 reduce-scatter.2
  383.8 51.3 reduce-scatter.4
  436.5 9.0 all-gather.8
  447.0 10.5 all-gather.10

commit v4 on v3

v4 whole, which is shorter than its diff:
```python
from functools import partial

import jax
import jax.numpy as jnp
from jax import lax
from jax.experimental import pallas as pl
from jax.experimental.pallas import tpu as pltpu
from jax.sharding import PartitionSpec as P

HEADS = 8
EPSILON = 1e-06
LANES = 128
BF = jnp.bfloat16
F32 = jnp.float32
I32 = jnp.int32
MIB = 1 << 20


def up(size, unit):
    return -(-size // unit) * unit


def nn(a, b):
    return jnp.dot(a, b, preferred_element_type=F32)


def nt(a, b):
    return lax.dot_general(a, b, (((1,), (1,)), ((), ())), preferred_element_type=F32)


def tn(a, b):
    return lax.dot_general(a, b, (((0,), (0,)), ((), ())), preferred_element_type=F32)


def iota(shape, dim):
    return lax.broadcasted_iota(I32, shape, dim)


def call(body, name, grid, ins, outs, scratch=(), flops=0, moved=0, vmem=56, aliases=None):
    in_specs = [pl.BlockSpec(*spec) if spec else pl.BlockSpec(memory_space=pltpu.VMEM) for spec in ins]
    out_specs = [pl.BlockSpec(*spec) if spec else pl.BlockSpec(memory_space=pltpu.VMEM) for spec, _ in outs]
    return pl.pallas_call(
        body,
        name=name,
        grid=grid,
        in_specs=in_specs,
        out_specs=out_specs,
        out_shape=[jax.ShapeDtypeStruct(*shape) for _, shape in outs],
        scratch_shapes=list(scratch),
        input_output_aliases=aliases or {},
        cost_estimate=pl.CostEstimate(flops=int(flops), bytes_accessed=int(moved), transcendentals=0),
        compiler_params=pltpu.CompilerParams(vmem_limit_bytes=vmem * MIB),
    )


def normed(values):
    average = jnp.mean(values, axis=-1, keepdims=True)
    centred = values - average
    inv_scale = lax.rsqrt(jnp.mean(centred * centred, axis=-1, keepdims=True) + EPSILON)
    return centred * inv_scale, inv_scale


def norm_backward(grad, unit, inv_scale, gain):
    scaled = grad * gain
    centre = jnp.mean(scaled, axis=-1, keepdims=True)
    along = jnp.mean(scaled * unit, axis=-1, keepdims=True)
    return inv_scale * (scaled - centre - unit * along)


def split3(value):
    high = value.astype(BF).astype(F32)
    rest = value - high
    mid = rest.astype(BF).astype(F32)
    return high, mid, rest - mid


def pick(slots, first, rows):
    own = iota((rows, slots.shape[1]), 0) + first
    hit = (own == slots[0:1, :]) | (own == slots[1:2, :])
    return jnp.where(hit, 1.0, 0.0).astype(BF)


def gelu_parts(z):
    share = 0.5 * (1.0 + lax.erf(z * 0.7071067811865476))
    slope = share + z * (0.3989422804014327 * jnp.exp(-0.5 * z * z))
    return z * share, slope


def experts_kernel(
    groups, dps, images, cap_pad, acts, grad, after, router, routes, slots, b_in, b_back, *rest
):
    hosted = groups // 2
    w_in, kin_in, w_back, kin_back, rest = *rest[:4], rest[4:]
    back_rows, output, g_router, g_in, g_back, g_in_other, g_back_other, g_b_in, g_b_back = rest[:9]
    w_in_far, w_back_far, rest = rest[9], rest[10], rest[11:]
    tok, info, made_rows, w_in_v, w_back_v, rows_v, hidden, grad_pre, delta, slope = rest[:10]
    in_send, in_recv, back_send, back_recv, dots, dots_got, to_near, from_near, to_far, from_far = rest[10:20]
    places, x_s, x_r, w_sem, r_s, r_r, p_s, p_r, store_sem, load_sem, w_s, w_r, w_own = rest[20:]
    dp, group, core = lax.axis_index("dp"), lax.axis_index("expert"), lax.axis_index("context")
    tokens, width = output.shape
    ff = w_in_v.shape[1]
    rows_in, rows_back = width // dps, ff // dps
    mate = group + 1 - 2 * lax.rem(group, 2)
    near, across, diagonal = (dp, group, 1 - core), (dp, mate, core), (dp, mate, 1 - core)

    def remote(src, dst, sems, slot, target):
        return pltpu.make_async_remote_copy(
            src_ref=src, dst_ref=dst, send_sem=sems[0].at[slot], recv_sem=sems[1].at[slot],
            device_id=target, device_id_type=MESH,
        )

    pools = (info, tok.at[0], tok.at[1])
    moves = {}
    for at, pool in enumerate(pools):
        moves[at, 1] = remote(pool.at[0], pool.at[1], (x_s, x_r), 3 * at, near)
        moves[at, 2] = remote(pool.at[0], pool.at[2], (x_s, x_r), 3 * at + 1, across)
        moves[at, 3] = remote(pool.at[2], pool.at[3], (x_s, x_r), 3 * at + 2, near)

    def along(step):
        return (lax.rem(dp + step, dps), group, core)

    def sum_out(which, step):
        src, dst = ((in_send, in_recv), (back_send, back_recv))[which]
        return remote(src.at[step], dst.at[step - 1], (r_s, r_r), which * dps + step, along(step))

    def gather(at, which, step):
        kin, far = ((kin_in, w_in_far), (kin_back, w_back_far))[which]
        size = kin.shape[1]
        part = far.at[at, pl.ds(pl.multiple_of(dp * size, size), size)]
        if step == 0:
            return pltpu.make_async_copy(kin.at[at], part, w_own.at[2 * at + which])
        return remote(kin.at[at], part, (w_s, w_r), (2 * at + which) * dps + step, along(step))

    def load(which, wait):
        for at in range(hosted):
            copies = (
                pltpu.make_async_copy(w_in_far.at[at - 1] if at else w_in, w_in_v, w_sem.at[0]),
                pltpu.make_async_copy(w_back_far.at[at - 1] if at else w_back, w_back_v, w_sem.at[1]),
            )

            @pl.when(which == at)
            def _():
                if at and not wait:
                    for part in range(2):
                        for step in range(dps):
                            gather(at - 1, part, step).wait()
                for copy in copies:
                    copy.wait() if wait else copy.start()

    def store(which, to, step):
        return (
            pltpu.make_async_copy(
                in_send.at[step],
                g_in_other.at[which - 1, pl.ds(pl.multiple_of(to * rows_in, rows_in), rows_in)],
                store_sem.at[step],
            ),
            pltpu.make_async_copy(
                back_send.at[step],
                g_back_other.at[which - 1, pl.ds(pl.multiple_of(to * rows_back, rows_back), rows_back)],
                store_sem.at[dps + step],
            ),
        )

    mine = (
        pltpu.make_async_copy(acts, tok.at[0, 0], load_sem.at[0]),
        pltpu.make_async_copy(grad, tok.at[1, 0], load_sem.at[1]),
    )
    for copy in mine:
        copy.start()
    load(0, False)
    greet([near, across, diagonal] + [along(step) for step in range(1, dps)])
    mine[0].wait()
    for hop in (2, 1):
        moves[1, hop].start()
    for at in range(hosted - 1):
        for part in range(2):
            for step in range(dps):
                gather(at, part, step).start()
    logits = nt(router[...], tok[0, 0])
    logits = jnp.exp(logits - jnp.max(logits, axis=0, keepdims=True))
    probs = logits / jnp.sum(logits, axis=0, keepdims=True)
    ids = iota(probs.shape, 0)
    info[0, 2:4, :] = slots[0:2, :].astype(F32)
    for choice in range(2):
        info[0, choice : choice + 1, :] = jnp.sum(
            jnp.where(routes[choice : choice + 1, :] == ids, probs, 0.0), axis=0, keepdims=True
        )
    info[0, 4:8, :] = jnp.zeros((4, tokens), F32)
    mine[1].wait()
    for hop in (2, 1):
        moves[0, hop].start()
        moves[2, hop].start()
    g_b_in[...] = jnp.zeros_like(g_b_in)
    g_b_back[...] = jnp.zeros_like(g_b_back)

    def near_out(at):
        return remote(to_near.at[at], from_near.at[at], (p_s, p_r), at, near)

    def far_out(at):
        return remote(to_far.at[at], from_far.at[at], (p_s, p_r), 4 + at, across)

    def dots_out(source, target):
        return remote(dots.at[source], dots_got.at[source - 1], (p_s, p_r), 5 + source, target)

    def own_row(pair):
        pair = pair.astype(F32)
        return jnp.where(core == 0, pair[0:1], pair[1:2])

    half = tokens // images
    deep = hosted * cap_pad
    slot_ids = jnp.zeros((1, deep), F32)
    lane = iota((1, deep), 1)
    for which in range(hosted):
        first = (lax.rem(group + 2 * which, groups) * 2 + core - which) * cap_pad
        slot_ids = jnp.where(lane // cap_pad == which, (lane + first).astype(F32), slot_ids)

    def place(source):
        slot = info[source, 2:4, :]
        high = jnp.floor(slot * (1.0 / 64.0))
        parts = jnp.concatenate([high, slot - 64.0 * high, jnp.zeros((4, tokens), F32)], axis=0).astype(BF)
        row, col = iota((8, LANES), 0), iota((8, LANES), 1)
        weight = jnp.where(row == col, 64.0, jnp.where(row == col + 2, 1.0, 0.0))
        weight = jnp.where(col < 2, weight, 0.0).astype(BF)
        places[...] = tn(parts, weight)

    def summed(source, image):
        rows = pl.ds(pl.multiple_of(image * half, 8), half)
        hit = (places[rows, 0:1] == slot_ids) | (places[rows, 1:2] == slot_ids)
        return rows, nn(jnp.where(hit, 1.0, 0.0).astype(BF), made_rows[source])

    def to_core(source, at):
        place(source)

        def chunk(image, _):
            rows, part = summed(source, image)
            to_near[at, rows, :] = part[:, :width].astype(BF)
            to_near[at + 1, rows, :] = part[:, width:].astype(BF)
            return 0

        lax.fori_loop(0, images, chunk, 0)
        near_out(at).start()
        near_out(at + 1).start()

    def to_chip():
        place(2)
        near_out(0).wait_recv()
        near_out(1).wait_recv()

        def chunk(image, _):
            rows, part = summed(2, image)
            to_far[0, rows, :] = (part[:, :width] + from_near[0, rows, :].astype(F32)).astype(BF)
            to_far[1, rows, :] = (part[:, width:] + from_near[1, rows, :].astype(F32)).astype(BF)
            return 0

        lax.fori_loop(0, images, chunk, 0)
        far_out(0).start()
        far_out(1).start()

    def expert(which, _):
        load(which, True)
        own = lax.rem(group + 2 * which, groups) * 2 + core
        last = which // (hosted - 1)

        def block(turn, _):
            source = turn + (3 - 2 * turn) * last

            @pl.when(jnp.logical_and(which == 0, source == 1))
            def _():
                for at in range(3):
                    moves[at, 1].wait_recv()

            @pl.when(jnp.logical_and(which == 0, source == 2))
            def _():
                for at in range(3):
                    moves[at, 2].wait_recv()
                    moves[at, 3].start()

            @pl.when(jnp.logical_and(which == 0, source == 3))
            def _():
                for at in range(3):
                    moves[at, 3].wait_recv()

            rows = pl.ds(pl.multiple_of(source * cap_pad, 16), cap_pad)
            spot = pl.ds(pl.multiple_of(which * cap_pad, 16), cap_pad)
            ids = iota((cap_pad, tokens), 0) + own * cap_pad
            hit_first = ids == info[source, 2:3, :].astype(I32)
            hit_second = ids == info[source, 3:4, :].astype(I32)
            hit = jnp.logical_or(hit_first, hit_second)
            one_hot = jnp.where(hit, 1.0, 0.0).astype(BF)
            gate = jnp.where(hit_first, info[source, 0:1, :], 0.0) + jnp.where(hit_second, info[source, 1:2, :], 0.0)
            gate = jnp.sum(gate, axis=1, keepdims=True)
            acts_in = nn(one_hot, tok[0, source]).astype(BF)
            for part in range(dps):
                rows_v[part, rows, :] = acts_in[:, part * rows_in : (part + 1) * rows_in]
            for part in range(dps):
                cols = slice(part * rows_back, (part + 1) * rows_back)
                z = nn(acts_in, w_in_v[:, cols]) + own_row(b_in[which, part])
                value, rise = gelu_parts(z)
                hidden[rows, cols] = value.astype(BF)
                slope[:, cols] = rise.astype(BF)
            bias = jnp.concatenate([own_row(b_back[which, part]) for part in range(dps)], axis=1)
            made = (nn(hidden[rows, :], w_back_v[...]) + bias).astype(BF).astype(F32)
            made_rows[source, spot, width:] = (gate * made).astype(BF)
            got_grad = nn(one_hot, tok[1, source])
            low = (gate * got_grad).astype(BF)
            delta[rows, :] = low
            g_b_back[which, core] += jnp.sum(low.astype(F32), axis=0, keepdims=True)
            dot = jnp.sum(made * got_grad, axis=1, keepdims=True)
            dots[source, which] = jnp.sum(jnp.where(hit, dot, 0.0), axis=0, keepdims=True)
            for part in range(dps):
                cols = slice(part * rows_back, (part + 1) * rows_back)
                dz = nt(low, w_back_v[cols, :]) * slope[:, cols].astype(F32)
                g_b_in[which, core, :, cols] += jnp.sum(dz, axis=0, keepdims=True)
                grad_pre[rows, cols] = dz.astype(BF)
            made_rows[source, spot, :width] = nt(grad_pre[rows, :], w_in_v[...]).astype(BF)

            @pl.when(jnp.logical_and(last == 1, source == 3))
            def _():
                dots_out(3, diagonal).start()
                to_core(3, 0)

            @pl.when(jnp.logical_and(last == 1, source == 2))
            def _():
                dots_out(2, across).start()
                to_chip()

            @pl.when(jnp.logical_and(last == 1, source == 1))
            def _():
                dots_out(1, near).start()
                to_core(1, 2)

            return 0

        lax.fori_loop(0, 4, block, 0)
        @pl.when(which + 1 < hosted)
        def _():
            load(which + 1, False)

        def weights(step, _):
            step = lax.rem(step + 1, dps)
            to = lax.rem(dp + step, dps)
            part_back = tn(hidden[:, pl.ds(pl.multiple_of(to * rows_back, LANES), rows_back)], delta[...])
            part_in = tn(rows_v[to], grad_pre[...])

            @pl.when(jnp.logical_and(which == 1, step > 0))
            def _():
                sum_out(0, step).wait_send()
                sum_out(1, step).wait_send()

            @pl.when(which > 1)
            def _():
                for copy in store(which - 1, to, step):
                    copy.wait()

            back_send[step] = part_back.astype(BF)
            in_send[step] = part_in.astype(BF)

            @pl.when(jnp.logical_and(which == 0, step > 0))
            def _():
                sum_out(1, step).start()
                sum_out(0, step).start()

            @pl.when(jnp.logical_and(which == 0, step == 0))
            def _():
                g_back[...] = part_back
                g_in[...] = part_in

            @pl.when(which > 0)
            def _():
                for copy in store(which, to, step):
                    copy.start()

            return 0

        lax.fori_loop(0, dps, weights, 0)
        return 0

    lax.fori_loop(0, hosted, expert, 0)
    for source, target in ((1, near), (2, across), (3, diagonal)):
        dots_out(source, target).wait_recv()
    at_near, at_far = 1 - core, core
    whole = jnp.zeros(probs.shape, F32)
    for which in range(hosted):
        here, there = lax.rem(group + 2 * which, groups) * 2, lax.rem(mate + 2 * which, groups) * 2
        whole = jnp.where(ids == here + core, dots[0, which], whole)
        whole = jnp.where(ids == here + at_near, dots_got[0, which], whole)
        whole = jnp.where(ids == there + at_far, dots_got[1, which], whole)
        whole = jnp.where(ids == there + at_near, dots_got[2, which], whole)
    low = (probs * (whole - jnp.sum(probs * whole, axis=0, keepdims=True))).astype(BF)
    g_router[...] = nn(low, tok[0, 0])
    back_rows[...] = tn(low, router[...])
    place(0)
    near_out(2).wait_recv()
    near_out(3).wait_recv()
    far_out(0).wait_recv()
    far_out(1).wait_recv()

    def chunk(image, _):
        rows, part = summed(0, image)
        back_rows[rows, :] += part[:, :width] + from_near[2, rows, :].astype(F32) + from_far[0, rows, :].astype(F32)
        out = part[:, width:] + from_near[3, rows, :].astype(F32) + from_far[1, rows, :].astype(F32)
        output[rows, :] = (after[rows, :] + out).astype(BF)
        return 0

    lax.fori_loop(0, images, chunk, 0)
    for step in range(1, dps):
        for which in range(2):
            sum_out(which, step).wait_recv()
        g_back[...] += back_recv[step - 1].astype(F32)
        g_in[...] += in_recv[step - 1].astype(F32)

    for step in range(dps):
        for copy in store(hosted - 1, lax.rem(dp + step, dps), step):
            copy.wait()
    for copy in moves.values():
        copy.wait_send()
    for at in range(4):
        near_out(at).wait_send()
    for at in range(2):
        far_out(at).wait_send()
    for source, target in ((1, near), (2, across), (3, diagonal)):
        dots_out(source, target).wait_send()


def forward_image(
    half, image, dps, x, x_other, bias, vec, w_qkv, w_out, q_ref, k_ref, v_ref, p_ref, o_ref, h_ref, a_ref
):
    width = x.shape[1]
    rows = pl.ds(pl.multiple_of(image * half, 8), half)
    half_pad = up(half, 16)
    head_dim = width // HEADS
    scale = head_dim ** (-0.5)
    gain, offset, bias_q, bias_v = (vec[row : row + 1, :] for row in range(4))
    own = x[rows, :].astype(F32)
    unit, _ = normed(own)
    acts = (unit * gain + offset).astype(BF)
    unit, _ = normed(x_other[rows, :].astype(F32))
    other = (unit * gain + offset).astype(BF)

    def weight(at):
        return w_qkv[:, :, at * width : (at + 1) * width].reshape(width, width)

    q_ref[rows, :] = ((nn(acts, weight(0)) + bias_q).astype(BF).astype(F32) * scale).astype(BF)
    pad = jnp.zeros((half_pad - half, width), BF)
    for part, piece in enumerate((acts, other)):
        start = part * half_pad
        k_ref[image, pl.ds(start, half), :] = nn(piece, weight(1)).astype(BF)
        v_ref[image, pl.ds(start, half), :] = (nn(piece, weight(2)) + bias_v).astype(BF)
        if half_pad > half:
            k_ref[image, pl.ds(start + half, half_pad - half), :] = pad
            v_ref[image, pl.ds(start + half, half_pad - half), :] = pad
    low = iota((1, LANES), 1) < head_dim
    zero = jnp.zeros((), BF)
    for pair in range(width // LANES):
        cols = pl.ds(pair * LANES, LANES)
        q_pair, k_pair, v_pair = q_ref[rows, cols], k_ref[image, :, cols], v_ref[image, :, cols]
        mixed = []
        for sub in range(2):
            mask = low if sub == 0 else jnp.logical_not(low)
            scores = nt(jnp.where(mask, q_pair, zero), k_pair) + bias[image]
            raised = jnp.exp(scores - jnp.max(scores, axis=1, keepdims=True))
            probs = (raised * (1.0 / jnp.sum(raised, axis=1, keepdims=True))).astype(BF)
            p_ref[image, 2 * pair + sub] = probs
            mixed.append(nn(probs, v_pair))
        o_ref[rows, cols] = jnp.where(low, mixed[0], mixed[1]).astype(BF)
    after = own + nn(o_ref[rows, :], w_out[...].reshape(width, width)) + vec[4:5, :]
    h_ref[rows, :] = after
    unit, _ = normed(after)
    a_ref[rows, :] = (unit * vec[5:6, :] + vec[6:7, :]).astype(BF)


def backward_kernel(
    grad, back_ref, h_ref, o_ref, vec, w_out, q_ref, k_ref, v_ref, p_ref,
    dh_ref, dq_ref, dk_ref, dv_ref, g_out, g_vec,
):
    image = pl.program_id(0)
    half, width = grad.shape
    head_dim = width // HEADS
    half_pad = up(half, 16)
    lane = iota((1, LANES), 1)
    back = back_ref[...]
    unit, inv_scale = normed(h_ref[...])
    out_grad = grad[...].astype(F32)
    dh = out_grad + norm_backward(back, unit, inv_scale, vec[5:6, :])
    dh_ref[...] = dh
    dh_low = dh.astype(BF)
    part_out = tn(o_ref[...], dh_low)
    rows = [
        jnp.sum(dh, axis=0, keepdims=True),
        jnp.sum(back * unit, axis=0, keepdims=True),
        jnp.sum(back, axis=0, keepdims=True),
    ]
    part_vec = jnp.concatenate(rows + [jnp.zeros((5, width), F32)], axis=0)

    @pl.when(image == 0)
    def _():
        g_out[...] = part_out
        g_vec[...] = part_vec

    @pl.when(image > 0)
    def _():
        g_out[...] += part_out
        g_vec[...] += part_vec

    do = nt(dh_low, w_out[...]).astype(BF)
    low = lane < head_dim
    zero = jnp.zeros((), BF)
    scale = head_dim ** (-0.5)
    for pair in range(width // LANES):
        cols = slice(pair * LANES, (pair + 1) * LANES)
        do_pair = do[:, cols]
        q_pair, k_pair, v_pair = q_ref[:, cols], k_ref[0, :, cols], v_ref[0, :, cols]
        dq, dk, dv = [], [], []
        for sub in range(2):
            mask = low if sub == 0 else jnp.logical_not(low)
            p_low = p_ref[0, 2 * pair + sub]
            p = p_low.astype(F32)
            dp = nt(jnp.where(mask, do_pair, zero), v_pair)
            inner = jnp.sum(p * dp, axis=1, keepdims=True)
            ds = (p * (dp - inner)).astype(BF)
            dv.append(tn(p_low, do_pair))
            dk.append(tn(ds, q_pair))
            dq.append(nn(ds, k_pair))
        dq_ref[:, cols] = (jnp.where(low, dq[0], dq[1]) * scale).astype(BF)
        dk_pair = jnp.where(low, dk[0], dk[1]).astype(BF)
        dv_pair = jnp.where(low, dv[0], dv[1]).astype(BF)
        for part in range(2):
            dk_ref[part, :, cols] = dk_pair[part * half_pad : part * half_pad + half]
            dv_ref[part, :, cols] = dv_pair[part * half_pad : part * half_pad + half]


def input_kernel(x_ref, dh_ref, dq_ref, dk_own, dk_got, dv_own, dv_got, vec, w_qkv, dx_ref, g_qkv, g_vec):
    image = pl.program_id(0)
    width = x_ref.shape[1]
    unit, inv_scale = normed(x_ref[...].astype(F32))
    acts = (unit * vec[0:1, :] + vec[1:2, :]).astype(BF)
    dq = dq_ref[...]
    dk = (dk_own[0].astype(F32) + dk_got[...].astype(F32)).astype(BF)
    dv = (dv_own[0].astype(F32) + dv_got[...].astype(F32)).astype(BF)
    da = jnp.zeros(unit.shape, F32)
    parts = []
    for at, piece in enumerate((dq, dk, dv)):
        parts.append(tn(acts, piece))
        da = da + nt(piece, w_qkv[:, at * width : (at + 1) * width])
    dx_ref[...] = (dh_ref[...] + norm_backward(da, unit, inv_scale, vec[0:1, :])).astype(BF)
    rows = [
        jnp.sum(da * unit, axis=0, keepdims=True),
        jnp.sum(da, axis=0, keepdims=True),
        jnp.sum(dq.astype(F32), axis=0, keepdims=True),
        jnp.sum(dv.astype(F32), axis=0, keepdims=True),
    ]
    part_vec = jnp.concatenate(rows + [jnp.zeros((4, width), F32)], axis=0)

    @pl.when(image == 0)
    def _():
        g_vec[...] = part_vec
        for at in range(3):
            g_qkv[:, at * width : (at + 1) * width] = parts[at]

    @pl.when(image > 0)
    def _():
        g_vec[...] += part_vec
        for at in range(3):
            g_qkv[:, at * width : (at + 1) * width] += parts[at]


MESH = pl.DeviceIdType.MESH


def send(src, dst, sems, slot, device):
    copy = pltpu.make_async_remote_copy(
        src_ref=src, dst_ref=dst, send_sem=sems[0].at[slot], recv_sem=sems[1].at[slot],
        device_id=device, device_id_type=MESH,
    )
    copy.start()
    return copy


def greet(devices):
    barrier = pltpu.get_barrier_semaphore()
    for device in devices:
        pl.semaphore_signal(barrier, inc=1, device_id=device, device_id_type=MESH)
    pl.semaphore_wait(barrier, len(devices))


def comm_call(body, name, number, ins, outs, scratch, flops=0, moved=0, vmem=56):
    return pl.pallas_call(
        body,
        name=name,
        in_specs=[pl.BlockSpec(memory_space=space) for space in ins],
        out_specs=[pl.BlockSpec(memory_space=space) for _, _, space in outs],
        out_shape=[jax.ShapeDtypeStruct(shape, dtype) for shape, dtype, _ in outs],
        scratch_shapes=list(scratch),
        cost_estimate=pl.CostEstimate(flops=int(flops), bytes_accessed=int(moved), transcendentals=0),
        compiler_params=pltpu.CompilerParams(
            vmem_limit_bytes=vmem * MIB, collective_id=number, has_side_effects=True
        ),
    )


def start_kernel(
    dps, groups, images, cap, cap_pad, x, w_qkv, w_out, w_router, vectors, b_in, b_back, routes, key_col, key_row, bias,
    w_in, w_back,
    qkv_all, out_all, router_rows, b_in_all, back_all, vec, slots,
    q_ref, k_ref, v_ref, p_ref, o_ref, h_ref, a_ref, in_all, in_kin, back_w_all, back_kin,
    x_other, router_all, vec_all, p_all, w_in_f, w_back_f, w_in_v, w_back_v,
    far_send, far_recv, near_send, near_recv, deep_send, deep_recv, w_s, w_r, local,
):
    dp, group, core = lax.axis_index("dp"), lax.axis_index("expert"), lax.axis_index("context")
    rows = w_qkv.shape[0]
    half = rows // 2
    hosted = groups // 2
    near = (dp, group, 1 - core)
    peers = [(lax.rem(dp + step, dps), group, core) for step in range(1, dps)]
    kin = [(dp, lax.rem(group + 2 * step, groups), core) for step in range(1, hosted)]
    loads = [
        pltpu.make_async_copy(w_in.at[core], w_in_f, local.at[0]),
        pltpu.make_async_copy(w_back.at[core], w_back_f, local.at[1]),
    ]
    for copy in loads:
        copy.start()
    greet(peers + kin + [near])
    far, close, deep = (far_send, far_recv), (near_send, near_recv), (deep_send, deep_recv)
    waits = [send(x, x_other, close, 0, near)]
    qkv_all[dp] = w_qkv[...].astype(BF)
    own = pl.ds(pl.multiple_of(core * half, half), half)
    copies = []
    for step, peer in enumerate(peers):
        copies.append(send(qkv_all.at[dp, own], qkv_all.at[dp, own], far, step * 6, peer))
    out_all[dp] = w_out[...].astype(BF)
    spare = router_all.shape[2] - w_router.shape[1]
    router_all[dp] = jnp.concatenate([w_router[...], jnp.zeros((rows, spare), F32)], axis=1).astype(BF)
    vec_all[dp] = jnp.concatenate([vectors[...], jnp.zeros((1, rows), F32)], axis=0).astype(BF)
    b_in_all[0, dp] = b_in[...].astype(BF)
    back_all[0, dp] = b_back[...].astype(BF)
    for step, peer in enumerate(peers):
        copies.append(send(out_all.at[dp, own], out_all.at[dp, own], far, step * 6 + 1, peer))
    smalls, biases = [], []
    for step, peer in enumerate(peers):
        for at, ref in enumerate((router_all, vec_all)):
            smalls.append(send(ref.at[dp], ref.at[dp], far, step * 6 + 2 + at, peer))
        for at, ref in enumerate((b_in_all, back_all)):
            biases.append(send(ref.at[0, dp], ref.at[0, dp], far, step * 6 + 4 + at, peer))
    own_copies = []
    for at, (wide, low, out, kin_out) in enumerate(
        ((w_in_f, w_in_v, in_all, in_kin), (w_back_f, w_back_v, back_w_all, back_kin))
    ):
        loads[at].wait()
        low[...] = wide[...].astype(BF)
        size = low.shape[0]
        part = pl.ds(pl.multiple_of(dp * size, size), size)
        for step, peer in enumerate(kin):
            own_copies.append(
                send(low, kin_out.at[hosted - 2 - step], (w_s, w_r), at * (dps + hosted) + dps + step, peer)
            )
        for step, peer in enumerate(peers):
            own_copies.append(send(low, out.at[part], (w_s, w_r), at * (dps + hosted) + step, peer))
        here = pltpu.make_async_copy(low, out.at[part], local.at[2 + at])
        here.start()
        own_copies.append(here)

    tokens = routes.shape[1]
    experts = w_router.shape[1]
    ids = iota((experts, tokens), 0)
    before = jnp.where(key_col[...] < key_row[...], 1.0, 0.0).astype(BF)
    first = jnp.where(routes[0:1, :] == ids, 1.0, 0.0)
    second = jnp.where(routes[1:2, :] == ids, 1.0, 0.0)
    count = jnp.sum(first, axis=1, keepdims=True)
    rank_first = jnp.sum(nn(first.astype(BF), before) * first, axis=0, keepdims=True)
    rank_second = jnp.sum((nn(second.astype(BF), before) + count) * second, axis=0, keepdims=True)
    ranks = jnp.concatenate([rank_first, rank_second], axis=0).astype(I32)
    owned = jnp.where(ranks < cap, routes[...] * cap_pad + ranks, -1)
    slots[...] = jnp.concatenate([owned, jnp.full((6, tokens), -1, I32)], axis=0)

    for copy in biases:
        copy.wait()
    for step, peer in enumerate(kin):
        for at, ref in enumerate((b_in_all, back_all)):
            waits.append(send(ref.at[0], ref.at[hosted - 1 - step], deep, 2 * step + at, peer))
    for at, copy in enumerate(copies):
        step, ref = at % len(peers), (qkv_all, out_all)[at // len(peers)]
        copy.wait()
        source = lax.rem(dp - step - 1 + dps, dps)
        waits.append(send(ref.at[source, own], ref.at[source, own], close, 1 + at, near))
    for copy in smalls:
        copy.wait()
    vec[...] = jnp.concatenate([vec_all[at].astype(F32) for at in range(dps)], axis=1)
    turned = [router_all[at].astype(F32).T[: w_router.shape[1]] for at in range(dps)]
    router_rows[...] = jnp.concatenate(turned, axis=1).astype(BF)
    for copy in waits:
        copy.wait()

    half = tokens // images

    def image_step(image, _):
        forward_image(
            half, image, dps, x, x_other, bias, vec, qkv_all, out_all, q_ref, k_ref, v_ref, p_all, o_ref, h_ref, a_ref
        )
        pltpu.make_async_copy(p_all.at[image], p_ref.at[image], local.at[4]).start()
        return 0

    lax.fori_loop(0, images, image_step, 0)
    pltpu.make_async_copy(p_all, p_ref, local.at[4]).wait()
    for copy in own_copies:
        copy.wait()


def reduce_kernel(
    dps, groups, g_qkv, g_out, g_router, g_one, g_two, b_in, b_back,
    o_qkv, o_out, o_router, o_vec, o_in, o_back,
    near_out, near_in, far_out, far_in, deep_out, deep_in, total,
    small_near, small_far, small_got, small_deep, bin_near, bin_far, bin_got, bin_deep,
    near_s, near_r, far_s, far_r, deep_s, deep_r, last_s, last_r,
):
    dp, group, core = lax.axis_index("dp"), lax.axis_index("expert"), lax.axis_index("context")
    width = g_out.shape[0]
    rows = width // dps
    half = rows // 2
    near = (dp, group, 1 - core)
    peers = [(lax.rem(dp + step, dps), group, core) for step in range(1, dps)]
    others = [(dp, lax.rem(group + step, groups), core) for step in range(1, groups)]
    greet(peers + others + [near])
    near_sems, far_sems, deep_sems, last_sems = (near_s, near_r), (far_s, far_r), (deep_s, deep_r), (last_s, last_r)
    sources = [(g_qkv, at) for at in range(0, g_qkv.shape[1], width)] + [(g_out, 0)]
    sizes = [width] * len(sources)
    starts = [width * at for at in range(len(sources))]

    deep = small_near.shape[2]
    hosted = groups // 2
    tall = 2 * hosted
    router = 8 + tall
    bias_rows = [b_back[at // 2, at % 2] for at in range(tall)]
    bias_in = jnp.concatenate([b_in[at // 2, at % 2] for at in range(tall)], axis=0)
    small = [g_one[0:4], g_two[0:3], jnp.zeros((1, width), F32)] + bias_rows + [g_router[...]]
    spare = deep - router - g_router.shape[0]
    small = jnp.concatenate(small + ([jnp.zeros((spare, width), F32)] if spare else []), axis=0)
    for at in range(dps):
        small_near[0, at] = small[:, at * rows : (at + 1) * rows]
        bin_near[0, at] = bias_in[:, at * bin_near.shape[3] : (at + 1) * bin_near.shape[3]]
    first = [
        send(small_near.at[0], small_near.at[1], near_sems, 0, near),
        send(bin_near.at[0], bin_near.at[1], near_sems, 1, near),
    ]
    theirs = pl.multiple_of((1 - core) * half, half)
    ours = pl.multiple_of(core * half, half)
    for at, (ref, lane) in enumerate(sources):
        cols = pl.ds(starts[at], sizes[at])
        for block in range(dps):
            near_out[block, :, cols] = ref[pl.ds(block * rows + theirs, half), lane : lane + sizes[at]].astype(BF)
        first.append(send(near_out.at[:, :, cols], near_in.at[:, :, cols], near_sems, 2 + at, near))
    second = []
    for copy in first[:2]:
        copy.wait()
    small_far[...] = small_near[0] + small_near[1]
    bin_far[...] = bin_near[0] + bin_near[1]
    smalls = []
    for step, peer in enumerate(peers):
        target = lax.rem(dp + step + 1, dps)
        smalls.append(send(small_far.at[target], small_got.at[step], far_sems, step, peer))
        smalls.append(send(bin_far.at[target], bin_got.at[step], far_sems, dps + step, peer))
    for at, (ref, lane) in enumerate(sources):
        cols = pl.ds(starts[at], sizes[at])
        first[2 + at].wait()
        for step, peer in enumerate(peers):
            target = lax.rem(dp + step + 1, dps)
            block = ref[pl.ds(pl.multiple_of(target * rows, rows) + ours, half), lane : lane + sizes[at]]
            far_out[step, :, cols] = (block + near_in[target, :, cols].astype(F32)).astype(BF)
            second.append(
                send(far_out.at[step, :, cols], far_in.at[step, :, cols], far_sems, (2 + at) * dps + step, peer)
            )
    for copy in smalls:
        copy.wait()
    lone = small_far[dp]
    lone_in = bin_far[dp]
    for step in range(dps - 1):
        lone = lone + small_got[step]
        lone_in = lone_in + bin_got[step]
    small_deep[group] = lone
    bin_deep[group] = lone_in
    third, deep_bin = [], []
    for step, peer in enumerate(others):
        third.append(send(small_deep.at[group], small_deep.at[group], deep_sems, step, peer))
        deep_bin.append(
            send(bin_deep.at[group], bin_deep.at[group], deep_sems, (1 + len(sources)) * groups + step, peer)
        )
    for at, (ref, lane) in enumerate(sources):
        cols = pl.ds(starts[at], sizes[at])
        mine = ref[pl.ds(pl.multiple_of(dp * rows, rows) + ours, half), lane : lane + sizes[at]]
        mine = mine + near_in[dp, :, cols].astype(F32)
        for step in range(dps - 1):
            second[at * (dps - 1) + step].wait()
            mine = mine + far_in[step, :, cols].astype(F32)
        deep_in[group, :, cols] = mine.astype(BF)
        for step, peer in enumerate(others):
            third.append(
                send(deep_in.at[group, :, cols], deep_in.at[group, :, cols], deep_sems, (1 + at) * groups + step, peer)
            )
    for copy in third[: groups - 1]:
        copy.wait()
    for copy in deep_bin:
        copy.wait()
    lone = small_deep[0]
    for at in range(1, groups):
        lone = lone + small_deep[at]
    o_vec[...] = lone[0:7]
    o_router[...] = lone[router : router + o_router.shape[0]]
    grad_in, grad_back = jnp.zeros(o_in.shape, F32), jnp.zeros(o_back.shape, F32)
    for at in range(groups):
        away = lax.rem(group - at + groups, groups)
        kin = lax.rem(away, 2) == 0
        pick_in, pick_back = jnp.zeros(o_in.shape, F32), jnp.zeros(o_back.shape, F32)
        for which in range(hosted):
            here = away // 2 == which
            pick_in = jnp.where(here, bin_deep[at, 2 * which : 2 * which + 2], pick_in)
            pick_back = jnp.where(here, small_deep[at, 8 + 2 * which : 10 + 2 * which], pick_back)
        grad_in = grad_in + jnp.where(kin, pick_in, 0.0)
        grad_back = grad_back + jnp.where(kin, pick_back, 0.0)
    o_in[...] = grad_in
    o_back[...] = grad_back
    last = []
    here = pl.ds(ours, half)
    for at in range(len(sources)):
        cols = pl.ds(starts[at], sizes[at])
        for step in range(groups - 1):
            third[(1 + at) * (groups - 1) + step].wait()
        done = deep_in[0, :, cols].astype(F32)
        for source in range(1, groups):
            done = done + deep_in[source, :, cols].astype(F32)
        total[here, cols] = done
        last.append(send(total.at[here, cols], total.at[here, cols], last_sems, at, near))
    for at in range(len(sources)):
        last[at].wait()
    o_qkv[...] = total[:, : 3 * width]
    o_out[...] = total[:, 3 * width : 4 * width]


def finish_kernel(count, g_in, g_back, *rest):
    others, rest = rest[: 2 * count], rest[2 * count :]
    _, o_in, o_back, sum_in, sum_back, sems_s, sems_r, local = rest
    dp, group, core = lax.axis_index("dp"), lax.axis_index("expert"), lax.axis_index("context")
    near = (dp, group, 1 - core)
    greet([near])
    copies = []
    for at, (own, total, out) in enumerate(((g_in, sum_in, o_in), (g_back, sum_back, o_back))):
        value = own[...]
        for other in others[at * count : (at + 1) * count]:
            value = value + other[...].astype(F32)
        total[...] = value
        copies.append(send(total, out.at[core], (sems_s, sems_r), at, near))
        here = pltpu.make_async_copy(total, out.at[core], local.at[at])
        here.start()
        copies.append(here)
    for copy in copies:
        copy.wait()


def shards(
    inputs, key_mask, routes, priority, vectors, w_qkv, w_out, w_router, w_in, b_in, w_back, b_back, cotangent
):
    images, half, width = inputs.shape
    tokens = images * half
    groups = lax.axis_size("expert")
    dps = lax.axis_size("dp")
    per_device = w_in.shape[0]
    experts = groups * per_device
    ff = w_in.shape[2]
    cap = max(2, 3 * tokens // experts)
    cap_pad = up(cap, 16)
    half_pad = up(half, 16)
    hosted = groups // 2
    context = lax.axis_index("context")
    swap = [(0, 1), (1, 0)]
    V, A = pltpu.VMEM, pl.ANY
    dma = pltpu.SemaphoreType.DMA
    rows = w_qkv.shape[0]
    rows_back = ff // dps

    x = inputs.reshape(tokens, width)
    grad = cotangent.reshape(tokens, width)
    route_rows = routes.reshape(tokens, 2).T
    keys = priority.reshape(tokens) * tokens + jnp.arange(tokens, dtype=I32)

    mask = jnp.where(key_mask > 0, 0.0, -1e30).astype(F32)
    first, second = mask[:, :half], mask[:, half:]
    own = jnp.where(context == 0, first, second)
    other = jnp.where(context == 0, second, first)
    off = jnp.full((images, half_pad - half), -1e30, F32)
    bias = jnp.concatenate([own, off, other, off], axis=1)[:, None, :]
    keys_pad = 2 * half_pad

    made = comm_call(
        partial(start_kernel, dps, groups, images, cap, cap_pad),
        "front",
        0,
        [V] * 11 + [A] * 2,
        [
            ((dps, rows, 3 * width), BF, V),
            ((dps, rows, width), BF, V),
            ((experts, width), BF, V),
            ((hosted, dps, per_device, rows_back), BF, V),
            ((hosted, dps, per_device, rows), BF, V),
            ((8, width), F32, V),
            ((8, tokens), I32, V),
            ((tokens, width), BF, V),
            ((images, keys_pad, width), BF, V),
            ((images, keys_pad, width), BF, V),
            ((images, HEADS, half, keys_pad), BF, A),
            ((tokens, width), BF, V),
            ((tokens, width), F32, V),
            ((tokens, width), BF, V),
            ((width, ff), BF, A),
            ((hosted - 1, rows, ff), BF, A),
            ((ff, width), BF, A),
            ((hosted - 1, rows_back, width), BF, A),
        ],
        [
            pltpu.VMEM((tokens, width), BF),
            pltpu.VMEM((dps, rows, LANES), BF),
            pltpu.VMEM((dps, 8, rows), BF),
            pltpu.VMEM((images, HEADS, half, keys_pad), BF),
            pltpu.VMEM((rows, ff), F32),
            pltpu.VMEM((rows_back, width), F32),
            pltpu.VMEM((rows, ff), BF),
            pltpu.VMEM((rows_back, width), BF),
        ]
        + [dma((6 * (dps - 1),))] * 2
        + [dma((1 + 2 * (dps - 1),))] * 2
        + [dma((2 * hosted,))] * 2
        + [dma((2 * (dps + hosted),))] * 2
        + [dma((5,))],
        flops=2 * tokens * width * (8 * width + 4 * keys_pad),
        moved=40 * tokens * width,
    )(x, w_qkv, w_out, w_router, vectors, b_in, b_back, route_rows, keys[:, None], keys[None, :], bias, w_in, w_back)
    qkv_all, out_all, router_rows, b_ins, b_backs, vec, slots, q, k, v, p, o, after, acts, *expert_w = made
    qkv_all = qkv_all.reshape(width, 3 * width)
    out_all = out_all.reshape(width, width)
    row = ((half, width), lambda i: (i, 0))
    cube = ((1, keys_pad, width), lambda i: (i, 0, 0))
    prob = ((1, HEADS, half, keys_pad), lambda i: (i, 0, 0, 0))

    rows_all = 4 * cap_pad
    deep = hosted * cap_pad
    made = comm_call(
        partial(experts_kernel, groups, dps, images, cap_pad),
        "experts",
        2,
        [A, A, V, V, V, V, V, V] + [A] * 4,
        [
            ((tokens, width), F32, V),
            ((tokens, width), BF, V),
            ((experts, width), F32, V),
            ((rows, ff), F32, V),
            ((rows_back, width), F32, V),
            ((hosted - 1, width, ff), BF, A),
            ((hosted - 1, ff, width), BF, A),
            ((hosted, 2, 1, ff), F32, V),
            ((hosted, 2, 1, width), F32, V),
            ((hosted - 1, width, ff), BF, A),
            ((hosted - 1, ff, width), BF, A),
        ],
        [
            pltpu.VMEM((2, 4, tokens, width), BF),
            pltpu.VMEM((4, 8, tokens), F32),
            pltpu.VMEM((4, deep, 2 * width), BF),
            pltpu.VMEM((width, ff), BF),
            pltpu.VMEM((ff, width), BF),
            pltpu.VMEM((dps, rows_all, rows), BF),
            pltpu.VMEM((rows_all, ff), BF),
            pltpu.VMEM((rows_all, ff), BF),
            pltpu.VMEM((rows_all, width), BF),
            pltpu.VMEM((cap_pad, ff), BF),
            pltpu.VMEM((dps, rows, ff), BF),
            pltpu.VMEM((dps - 1, rows, ff), BF),
            pltpu.VMEM((dps, rows_back, width), BF),
            pltpu.VMEM((dps - 1, rows_back, width), BF),
            pltpu.VMEM((4, hosted, 1, tokens), F32),
            pltpu.VMEM((3, hosted, 1, tokens), F32),
            pltpu.VMEM((4, tokens, width), BF),
            pltpu.VMEM((4, tokens, width), BF),
            pltpu.VMEM((2, tokens, width), BF),
            pltpu.VMEM((2, tokens, width), BF),
            pltpu.VMEM((tokens, LANES), F32),
            dma((9,)),
            dma((9,)),
            dma((2,)),
            dma((2 * dps,)),
            dma((2 * dps,)),
            dma((9,)),
            dma((9,)),
            dma((2 * dps,)),
            dma((2,)),
            dma((2 * hosted * dps,)),
            dma((2 * hosted * dps,)),
            dma((2 * hosted,)),
        ],
        flops=14 * hosted * rows_all * width * ff,
        moved=20 * tokens * width + 8 * hosted * width * ff,
        vmem=63,
    )(acts, grad, after, router_rows, route_rows, slots, b_ins, b_backs, *expert_w)
    back_rows, output, g_router, g_in, g_back, g_in_other, g_back_other, g_b_in, g_b_back, *_ = made

    others = []
    for part in (g_in_other, g_back_other):
        part = lax.psum_scatter(part, "dp", scatter_dimension=1, tiled=True)
        for step in range(1, hosted):
            perm = [(at, (at + 2 * step) % groups) for at in range(groups)]
            others.append(lax.ppermute(part[step - 1], "expert", perm))

    halves = ((2, half, width), lambda i: (0, i, 0))
    fixed = lambda i: (0, 0)
    dh, dq, dk, dv, g_out, g_vec_two = call(
        backward_kernel,
        "backward",
        (images,),
        [row, row, row, row, None, None, row, cube, cube, prob],
        [
            (row, ((tokens, width), F32)),
            (row, ((tokens, width), BF)),
            (halves, ((2, tokens, width), BF)),
            (halves, ((2, tokens, width), BF)),
            (((width, width), fixed), ((width, width), F32)),
            (((8, width), fixed), ((8, width), F32)),
        ],
        flops=2 * tokens * width * (2 * width + 8 * keys_pad),
        moved=30 * tokens * width,
    )(grad, back_rows, after, o, vec, out_all, q, k, v, p)

    dk_got = lax.ppermute(dk[1], "context", swap)
    dv_got = lax.ppermute(dv[1], "context", swap)
    own_half = ((1, half, width), lambda i: (0, i, 0))
    dx, g_qkv, g_vec_one = call(
        input_kernel,
        "input",
        (images,),
        [row, row, row, own_half, row, own_half, row, None, None],
        [
            (row, ((tokens, width), BF)),
            (((width, 3 * width), fixed), ((width, 3 * width), F32)),
            (((8, width), fixed), ((8, width), F32)),
        ],
        flops=12 * tokens * width * width,
        moved=20 * tokens * width,
    )(x, dh, dq, dk, dk_got, dv, dv_got, vec, qkv_all)

    wide = 4 * width
    halves_of = rows // 2
    small = up(8 + 2 * hosted + experts, 8)
    grad_qkv, grad_out, grad_router, grad_vec, grad_b_in, grad_b_back = comm_call(
        partial(reduce_kernel, dps, groups),
        "reduce",
        1,
        [V] * 7,
        [
            ((rows, 3 * width), F32, V),
            ((rows, width), F32, V),
            ((experts, rows), F32, V),
            ((7, rows), F32, V),
            ((per_device, rows_back), F32, V),
            ((per_device, rows), F32, V),
        ],
        [
            pltpu.VMEM((dps, halves_of, wide), BF),
            pltpu.VMEM((dps, halves_of, wide), BF),
            pltpu.VMEM((dps - 1, halves_of, wide), BF),
            pltpu.VMEM((dps - 1, halves_of, wide), BF),
            pltpu.VMEM((8, LANES), BF),
            pltpu.VMEM((groups, halves_of, wide), BF),
            pltpu.VMEM((rows, wide), F32),
            pltpu.VMEM((2, dps, small, rows), F32),
            pltpu.VMEM((dps, small, rows), F32),
            pltpu.VMEM((dps - 1, small, rows), F32),
            pltpu.VMEM((groups, small, rows), F32),
            pltpu.VMEM((2, dps, 2 * hosted, rows_back), F32),
            pltpu.VMEM((dps, 2 * hosted, rows_back), F32),
            pltpu.VMEM((dps - 1, 2 * hosted, rows_back), F32),
            pltpu.VMEM((groups, 2 * hosted, rows_back), F32),
            dma((6,)), dma((6,)), dma((6 * dps,)), dma((6 * dps,)),
            dma((6 * groups,)), dma((6 * groups,)), dma((4,)), dma((4,)),
        ],
        moved=20 * width * wide,
    )(g_qkv, g_out, g_router, g_vec_one, g_vec_two, g_b_in, g_b_back)

    grad_w_in, grad_w_back = comm_call(
        partial(finish_kernel, hosted - 1),
        "finish",
        3,
        [V] * (2 * hosted + 1),
        [(w_in.shape, F32, A), (w_back.shape, F32, A)],
        [pltpu.VMEM((rows, ff), F32), pltpu.VMEM((rows_back, width), F32), dma((2,)), dma((2,)), dma((2,))],
        moved=16 * rows * ff,
    )(g_in, g_back, *others, grad_vec)
    return (
        output.reshape(images, half, width),
        dx.reshape(images, half, width),
        grad_vec,
        grad_qkv,
        grad_out,
        grad_router.T,
        grad_w_in,
        grad_b_in,
        grad_w_back,
        grad_b_back,
    )


def solution(mesh):
    tokens = P(("dp", "expert"), "context", None)
    by_rows = P("dp", None)
    experts = P("expert", "dp", None)
    expert_bias = P("expert", "dp")
    return jax.shard_map(
        shards,
        mesh=mesh,
        in_specs=(
            tokens,
            P(("dp", "expert"), None),
            P(("dp", "expert"), "context", None, None),
            tokens,
            P(None, "dp"),
            by_rows,
            by_rows,
            by_rows,
            experts,
            expert_bias,
            experts,
            expert_bias,
            tokens,
        ),
        out_specs=(
            tokens,
            tokens,
            P(None, "dp"),
            by_rows,
            by_rows,
            by_rows,
            experts,
            expert_bias,
            experts,
            expert_bias,
        ),
        check_vma=False,
    )
```

time: 514 us -> 358 us (0.70)
  waiting for transfers between devices: 143 us -> 43.1 us
  Pallas kernels: 325 us -> 277 us
  other arithmetic: 11.1 us -> 3.62 us
    all_gather x4 -> x0, waiting for transfers between devices: 79 us -> none  [the longest x1 54.6 us: shards(): back_w = lax.all_gather(back_w, 'dp', axis=1, tiled=True)]
    pallas_call x6 -> x4, Pallas kernels: 273 us -> 227 us  [the longest x1 121 us: shards(): comm_call(partial(experts_kernel, groups, dps, images, cap_pad), 'experts...]
    reduce_scatter x2, waiting for transfers between devices: 62.9 us -> 42.4 us  [shards(): part = lax.psum_scatter(part, 'dp', scatter_dimension=1, tiled=True)]
    convert_element_type x4 -> x0, other arithmetic: 9.53 us -> none  [the longest x2 5.7 us: expert_sum(): return lax.all_gather(share, 'context', axis=1, tiled=True).astype(F32)]
    unnamed x41 -> x36, local copies, waits for them, and re-layouts: 8.86 us -> 11.6 us
  transfers between devices with their start and end apart: 9 -> 6, of which waited for: 4 -> 2; matrix products, arithmetic and copies ran while one was open for 2% -> 1% of each run, Pallas kernels for 23% -> 21%
where the time goes in v4:
time: 358 us; the launch traced here: 357 us
  Pallas kernels  277 us (77%)
  waiting for transfers between devices  43.1 us (12%)
  local copies, waits for them, and re-layouts  14.7 us (4%)
  between operations  14.2 us (4%)
  starting transfers between devices  5.11 us (1%)
  other arithmetic  3.62 us (1%)
    pallas_call x1, Pallas kernels, shards(): comm_call(partial(experts_kernel, groups, dps, images, cap_pad), 'experts...  121 us
    pallas_call x1, Pallas kernels, shards(): comm_call(partial(start_kernel, dps, groups, images, cap, cap_pad), 'fron...  73.3 us
    reduce_scatter x2, waiting for transfers between devices, shards(): part = lax.psum_scatter(part, 'dp', scatter_dimension=1, tiled=True)  42.4 us
    pallas_call x1, Pallas kernels, shards(): comm_call(partial(reduce_kernel, dps, groups), 'reduce', 1, [V] * 7, [((r...  38.6 us
    pallas_call x1, Pallas kernels, shards(): call(backward_kernel, 'backward', (images,), [row, row, row, row, None, N...  26.1 us
    unnamed x36, local copies, waits for them, and re-layouts  11.6 us
    pallas_call x1, Pallas kernels, shards(): call(input_kernel, 'input', (images,), [row, row, row, own_half, row, own...  11.2 us
  transfers between devices with their start and end apart: 6, of which 2 were waited for; matrix products, arithmetic and copies ran while one was open for 1% of the time, Pallas kernels for 21%

profile of v4, /device:TPU:0, one launch (start us, length us, event | category | flops | bytes accessed | tf_op | source)
XLA Modules:
  0.0 357.4 jit_solution(2859775702243678309)
XLA Ops:
  7.2 0.0 reduce-scatter.5.cloned.1.call-start
  7.2 1.3 bitcast_add_fusion.key_row
  8.5 0.7 multiply_bitcast_fusion
  9.2 0.7 compare_select_fusion
  9.9 0.1 slice_select_fusion.1
  10.0 0.1 pad_maximum_fusion
  10.0 0.6 broadcast_in_dim.15.bias
  10.7 1.4 copy.25.w_router
  12.1 0.2 copy.24
  12.3 0.8 iota_add_fusion.key_col
  13.1 73.3 %front.1 = (bf16[4,128,1536]{2,1,0:T(8,128)(2,1)}, bf16[4,128,512]{2,1,0:T(8,128)(2,1)}, bf16[8,512]{1,0:T(8,128)(2,1)}, bf16[2,4,2,512]{3,2,1,0:T(2,128)(2,1)},...) custom-call(bf16[888,512]{1,0:T(8,128)(2,1)} %bitcast.22, ...), custom_call_target="tpu_custom_call" | custom-call | flops 5935988736 | bytes 18186240 | tf_op jit(solution)/shard_map/front/pallas_call | solution.py:891
  86.4 121.0 %experts.1 = (f32[888,512]{1,0:T(8,128)}, bf16[888,512]{1,0:T(8,128)(2,1)}, f32[8,512]{1,0:T(8,128)}, f32[128,2048]{1,0:T(8,128)}, f32[512,512]{1,0:T(8,128)}, /...) custom-call(bf16[888,512]{1,0:T(8,128)(2,1)} %get-tuple-element.54.a, ...), custom_call_target="tpu_custom_call" | custom-call | flops 39460012032 | bytes 25870336 | tf_op jit(solution)/shard_map/experts/pallas_call | solution.py:943
  207.4 0.0 reduce-scatter.5.cloned.1.call-update
  207.4 0.0 reduce-scatter.3.cloned.1.call-start
  207.4 0.7 reduce-scatter.3.cloned.1.call-update
  208.1 26.1 %backward.1 = (f32[888,512]{1,0:T(8,128)}, bf16[888,512]{1,0:T(8,128)(2,1)}, bf16[2,888,512]{2,1,0:T(8,128)(2,1)}, bf16[2,888,512]{2,1,0:T(8,128)(2,1)}, f32[512,512]{1,0:T(8,128)}, /*index=5*/f32[8,512]{1,0:T(8,128)}) custom-call(bf16[888,512]{1,0:T(8,128)(2,1)} %bitcast.26, f32[888,512]{1,0:T(8,128)} %get-tuple-element.65.back_ref, ...), custom_call_target="tpu_custom_call" | custom-call | flops 5354029056 | bytes 13639680 | tf_op jit(solution)/shard_map/backward/pallas_call | solution.py:1011
  234.3 0.0 copy-start
  234.3 1.4 slice_bitcast_fusion
  235.7 0.1 collective-permute-start.1
  235.8 0.3 copy-done
  236.1 1.0 slice_bitcast_fusion.1
  237.1 0.2 collective-permute-start
  237.3 6.3 %reduce-scatter.5.cloned.1.call-done = bf16[1,512,512]{2,1,0:T(8,128)(2,1)} async-done(((bf16[1,2048,512]{2,1,0:T(8,128)(2,1)}), bf16[1,512,512]{2,1,0:T(8,128)(2,1)}) %reduce-scatter.5.cloned.1.call-update) | async-done | bytes 524304 | tf_op jit(solution)/shard_map/reduce_scatter | solution.py:1004
  243.5 2.4 collective-permute-start.3
  245.9 36.1 %reduce-scatter.3.cloned.1.call-done = bf16[1,128,2048]{2,1,0:T(8,128)(2,1)} async-done(((bf16[1,512,2048]{2,1,0:T(8,128)(2,1)}), bf16[1,128,2048]{2,1,0:T(8,128)(2,1)}) %reduce-scatter.3.cloned.1.call-update) | async-done | bytes 524304 | tf_op jit(solution)/shard_map/reduce_scatter | solution.py:1004
  282.0 2.4 collective-permute-start.2
  284.4 0.0 collective-permute-done.1.dv_got
  284.4 0.0 collective-permute-done.dk_got
  284.4 0.0 copy-start.4
  284.4 0.9 copy-done.4
  285.3 11.2 %input.1 = (bf16[888,512]{1,0:T(8,128)(2,1)}, f32[512,1536]{1,0:T(8,128)}, f32[8,512]{1,0:T(8,128)}) custom-call(bf16[888,512]{1,0:T(8,128)(2,1)} %bitcast.23, f32[888,512]{1,0:T(8,128)} %get-tuple-element.73.dh_ref, bf16[888,512]{1,0:T(8,128)(2,1)} %get-tuple-element.74.dq_ref, bf16[2,888,512]{2,1,0:T(8,128)(2,1)} %get-tuple-element.75.dk_own, ...), custom_call_target="tpu_custom_call" | custom-call | flops 2793406464 | bytes 9093120 | tf_op jit(solution)/shard_map/input/pallas_call | solution.py:1031
  296.6 38.6 %reduce.1 = (f32[128,1536]{1,0:T(8,128)}, f32[128,512]{1,0:T(8,128)}, f32[8,128]{1,0:T(8,128)}, f32[7,128]{1,0:T(8,128)}, f32[2,512]{1,0:T(2,128)}, /*index=5*/f32[2,128]{1,0:T(2,128)}) custom-call(f32[512,1536]{1,0:T(8,128)} %get-tuple-element.79.g_qkv, f32[512,512]{1,0:T(8,128)} %get-tuple-element.80.g_out, f32[8,512]{1,0:T(8,128)} %get-tuple-element.81.g_router, ...), custom_call_target="tpu_custom_call" | custom-call | bytes 20971520 | tf_op jit(solution)/shard_map/reduce/pallas_call | solution.py:1048
  335.2 0.0 copy-start.3
  335.2 0.0 collective-permute-done.3.rest_1_
  335.2 0.0 copy-start.6
  335.2 0.0 collective-permute-done.2.rest_0_
  335.2 0.0 copy-start.7
  335.2 0.8 copy-done.6
  336.0 0.2 copy-done.7
  336.2 0.0 copy-start.9
  336.2 0.0 copy-start.5
  336.2 6.3 %finish.1 = (f32[2,128,2048]{2,1,0:T(8,128)}, f32[2,512,512]{2,1,0:T(8,128)}) custom-call(f32[128,2048]{1,0:T(8,128)} %get-tuple-element.90.g_in, f32[512,512]{1,0:T(8,128)} %get-tuple-element.91.g_back, bf16[128,2048]{1,0:T(8,128)(2,1)} %copy-done.7, bf16[512,512]{1,0:T(8,128)(2,1)} %copy-done.6, f32[7,128]{1,0:T(8,128)} %get-tuple-element.112.rest_2_), custom_call_target="tpu_custom_call" | custom-call | bytes 4194304 | tf_op jit(solution)/shard_map/finish/pallas_call | solution.py:1083
  342.5 0.0 copy-start.8
  342.5 0.0 copy-start.11
  342.5 0.0 copy-start.2
  342.6 0.0 copy-done.3
  342.6 0.9 copy.35
  343.5 0.0 copy-done.9
  343.5 0.6 copy.36
  344.1 0.0 copy-done.5
  344.1 0.9 copy.37
  345.0 0.0 copy-done.8
  345.0 0.7 copy.38
  345.7 0.0 copy-done.11
  345.7 0.6 copy.39
  346.3 0.0 copy-done.2
  346.3 0.0 copy-start.10
  346.3 1.3 copy.40
  347.6 0.0 copy-done.10
  347.6 0.6 copy.41
  348.2 0.4 copy-done.1
  348.6 1.3 copy.42
  349.9 0.0 copy-done.12
  349.9 0.6 copy.43
  (3 shorter events, 0.0 us)
Async XLA Ops:
  7.2 236.4 %reduce-scatter.5.cloned.1.call-start = ((), (), s32[]{:S(2)}) async-start(), calls=%async_computation.3 | async-start | bytes 2621440 | tf_op jit(solution)/shard_map/reduce_scatter | solution.py:1004
  207.4 74.6 %reduce-scatter.3.cloned.1.call-start = ((), (), s32[]{:S(2)}) async-start(), calls=%async_computation.2 | async-start | bytes 2621440 | tf_op jit(solution)/shard_map/reduce_scatter | solution.py:1004
  234.3 1.8 copy-start
  235.7 48.7 %collective-permute-start.1 = (bf16[888,512]{1,0:T(8,128)(2,1)S(1)}, bf16[888,512]{1,0:T(8,128)(2,1)}, u32[]{:S(2)}, u32[]{:S(2)}) collective-permute-start(bf16[888,512]{1,0:T(8,128)(2,1)S(1)} %slice_bitcast_fusion), channel_id=1, source_target_pairs={{0,1},{1,0},{2,3},{3,2},{4,5},{5,4},{6,7},{7,6},{8,9},{9,8},{10,11... | collective-permute-start | bytes 2727944 | tf_op jit(solution)/shard_map/ppermute | solution.py:1029
  237.1 47.3 %collective-permute-start = (bf16[888,512]{1,0:T(8,128)(2,1)}, bf16[888,512]{1,0:T(8,128)(2,1)S(1)}, u32[]{:S(2)}, u32[]{:S(2)}) collective-permute-start(bf16[888,512]{1,0:T(8,128)(2,1)} %slice_bitcast_fusion.1), channel_id=1, source_target_pairs={{0,1},{1,0},{2,3},{3,2},{4,5},{5,4},{6,7},{7,6},{8,9},{9,8},{10,11... | collective-permute-start | bytes 2727944 | tf_op jit(solution)/shard_map/ppermute | solution.py:1028
  243.5 91.7 %collective-permute-start.3 = (bf16[512,512]{1,0:T(8,128)(2,1)}, bf16[512,512]{1,0:T(8,128)(2,1)S(1)}, u32[]{:S(2)}, u32[]{:S(2)}) collective-permute-start(bf16[512,512]{1,0:T(8,128)(2,1)} %bitcast.28), channel_id=1, source_target_pairs={{0,4},{2,6},{4,0},{6,2},{1,5},{3,7},{5,1},{7,3},{8,12},{10,14},{12... | collective-permute-start | bytes 1572872 | tf_op jit(solution)/shard_map/ppermute | solution.py:1007
  282.0 53.2 %collective-permute-start.2 = (bf16[128,2048]{1,0:T(8,128)(2,1)}, bf16[128,2048]{1,0:T(8,128)(2,1)S(1)}, u32[]{:S(2)}, u32[]{:S(2)}) collective-permute-start(bf16[128,2048]{1,0:T(8,128)(2,1)} %bitcast.29), channel_id=1, source_target_pairs={{0,4},{2,6},{4,0},{6,2},{1,5},{3,7},{5,1},{7,3},{8,12},{10,14},{12... | collective-permute-start | bytes 1572872 | tf_op jit(solution)/shard_map/ppermute | solution.py:1007
  284.4 0.9 copy-start.4
  335.2 7.4 %copy-start.3 = (bf16[888,512]{1,0:T(8,128)(2,1)S(1)}, bf16[888,512]{1,0:T(8,128)(2,1)}, u32[]{:S(2)}) copy-start(bf16[888,512]{1,0:T(8,128)(2,1)} %get-tuple-element.64) | copy-start | bytes 2727940
  335.2 0.8 copy-start.6
  335.2 0.9 copy-start.7
  336.2 7.3 %copy-start.9 = (f32[7,128]{1,0:T(8,128)S(1)}, f32[7,128]{1,0:T(8,128)}, u32[]{:S(2)}) copy-start(f32[7,128]{1,0:T(8,128)} %get-tuple-element.112.rest_2_) | copy-start | bytes 10756
  336.2 7.9 %copy-start.5 = (f32[128,1536]{1,0:T(8,128)S(1)}, f32[128,1536]{1,0:T(8,128)}, u32[]{:S(2)}) copy-start(f32[128,1536]{1,0:T(8,128)} %get-tuple-element.113) | copy-start | bytes 2359300
  342.5 2.4 copy-start.8
  342.5 3.1 copy-start.11
  342.5 3.7 %copy-start.2 = (f32[2,128,2048]{2,1,0:T(8,128)S(1)}, f32[2,128,2048]{2,1,0:T(8,128)}, u32[]{:S(2)}) copy-start(f32[2,128,2048]{2,1,0:T(8,128)} %get-tuple-element.116) | copy-start | bytes 6291460
  346.3 1.3 copy-start.10
  346.3 2.4 copy-start.1
  348.6 1.3 copy-start.12
Sparse Core Ops, SparseCore 0:
  207.5 35.9 reduce-scatter.4
  246.8 35.1 reduce-scatter.2

commit v5 on v4

--- a/solution.py
+++ b/solution.py
@@ -36,23 +36,6 @@
     return lax.broadcasted_iota(I32, shape, dim)
 
 
-def call(body, name, grid, ins, outs, scratch=(), flops=0, moved=0, vmem=56, aliases=None):
-    in_specs = [pl.BlockSpec(*spec) if spec else pl.BlockSpec(memory_space=pltpu.VMEM) for spec in ins]
-    out_specs = [pl.BlockSpec(*spec) if spec else pl.BlockSpec(memory_space=pltpu.VMEM) for spec, _ in outs]
-    return pl.pallas_call(
-        body,
-        name=name,
-        grid=grid,
-        in_specs=in_specs,
-        out_specs=out_specs,
-        out_shape=[jax.ShapeDtypeStruct(*shape) for _, shape in outs],
-        scratch_shapes=list(scratch),
-        input_output_aliases=aliases or {},
-        cost_estimate=pl.CostEstimate(flops=int(flops), bytes_accessed=int(moved), transcendentals=0),
-        compiler_params=pltpu.CompilerParams(vmem_limit_bytes=vmem * MIB),
-    )
-
-
 def normed(values):
     average = jnp.mean(values, axis=-1, keepdims=True)
     centred = values - average
@@ -65,19 +48,6 @@
     centre = jnp.mean(scaled, axis=-1, keepdims=True)
     along = jnp.mean(scaled * unit, axis=-1, keepdims=True)
     return inv_scale * (scaled - centre - unit * along)
-
-
-def split3(value):
-    high = value.astype(BF).astype(F32)
-    rest = value - high
-    mid = rest.astype(BF).astype(F32)
-    return high, mid, rest - mid
-
-
-def pick(slots, first, rows):
-    own = iota((rows, slots.shape[1]), 0) + first
-    hit = (own == slots[0:1, :]) | (own == slots[1:2, :])
-    return jnp.where(hit, 1.0, 0.0).astype(BF)
 
 
 def gelu_parts(z):
@@ -469,51 +439,36 @@
     a_ref[rows, :] = (unit * vec[5:6, :] + vec[6:7, :]).astype(BF)
 
 
-def backward_kernel(
-    grad, back_ref, h_ref, o_ref, vec, w_out, q_ref, k_ref, v_ref, p_ref,
+def backward_image(
+    half, image, grad, back_ref, h_ref, o_ref, vec, w_out, q_ref, k_ref, v_ref, p_ref,
     dh_ref, dq_ref, dk_ref, dv_ref, g_out, g_vec,
 ):
-    image = pl.program_id(0)
-    half, width = grad.shape
+    width = grad.shape[1]
+    rows = pl.ds(pl.multiple_of(image * half, 8), half)
     head_dim = width // HEADS
     half_pad = up(half, 16)
     lane = iota((1, LANES), 1)
-    back = back_ref[...]
-    unit, inv_scale = normed(h_ref[...])
-    out_grad = grad[...].astype(F32)
-    dh = out_grad + norm_backward(back, unit, inv_scale, vec[5:6, :])
-    dh_ref[...] = dh
+    back = back_ref[rows, :]
+    unit, inv_scale = normed(h_ref[rows, :])
+    dh = grad[rows, :].astype(F32) + norm_backward(back, unit, inv_scale, vec[5:6, :])
+    dh_ref[rows, :] = dh
     dh_low = dh.astype(BF)
-    part_out = tn(o_ref[...], dh_low)
-    rows = [
-        jnp.sum(dh, axis=0, keepdims=True),
-        jnp.sum(back * unit, axis=0, keepdims=True),
-        jnp.sum(back, axis=0, keepdims=True),
-    ]
-    part_vec = jnp.concatenate(rows + [jnp.zeros((5, width), F32)], axis=0)
-
-    @pl.when(image == 0)
-    def _():
-        g_out[...] = part_out
-        g_vec[...] = part_vec
-
-    @pl.when(image > 0)
-    def _():
-        g_out[...] += part_out
-        g_vec[...] += part_vec
-
-    do = nt(dh_low, w_out[...]).astype(BF)
+    g_out[...] += tn(o_ref[rows, :], dh_low)
+    g_vec[4:5, :] += jnp.sum(dh, axis=0, keepdims=True)
+    g_vec[5:6, :] += jnp.sum(back * unit, axis=0, keepdims=True)
+    g_vec[6:7, :] += jnp.sum(back, axis=0, keepdims=True)
+    do = nt(dh_low, w_out[...].reshape(width, width)).astype(BF)
     low = lane < head_dim
     zero = jnp.zeros((), BF)
     scale = head_dim ** (-0.5)
     for pair in range(width // LANES):
         cols = slice(pair * LANES, (pair + 1) * LANES)
         do_pair = do[:, cols]
-        q_pair, k_pair, v_pair = q_ref[:, cols], k_ref[0, :, cols], v_ref[0, :, cols]
+        q_pair, k_pair, v_pair = q_ref[rows, cols], k_ref[image, :, cols], v_ref[image, :, cols]
         dq, dk, dv = [], [], []
         for sub in range(2):
             mask = low if sub == 0 else jnp.logical_not(low)
-            p_low = p_ref[0, 2 * pair + sub]
+            p_low = p_ref[2 * pair + sub]
             p = p_low.astype(F32)
             dp = nt(jnp.where(mask, do_pair, zero), v_pair)
             inner = jnp.sum(p * dp, axis=1, keepdims=True)
@@ -521,47 +476,32 @@
             dv.append(tn(p_low, do_pair))
             dk.append(tn(ds, q_pair))
             dq.append(nn(ds, k_pair))
-        dq_ref[:, cols] = (jnp.where(low, dq[0], dq[1]) * scale).astype(BF)
+        dq_ref[rows, cols] = (jnp.where(low, dq[0], dq[1]) * scale).astype(BF)
         dk_pair = jnp.where(low, dk[0], dk[1]).astype(BF)
         dv_pair = jnp.where(low, dv[0], dv[1]).astype(BF)
         for part in range(2):
-            dk_ref[part, :, cols] = dk_pair[part * half_pad : part * half_pad + half]
-            dv_ref[part, :, cols] = dv_pair[part * half_pad : part * half_pad + half]
-
-
-def input_kernel(x_ref, dh_ref, dq_ref, dk_own, dk_got, dv_own, dv_got, vec, w_qkv, dx_ref, g_qkv, g_vec):
-    image = pl.program_id(0)
+            dk_ref[part, rows, cols] = dk_pair[part * half_pad : part * half_pad + half]
+            dv_ref[part, rows, cols] = dv_pair[part * half_pad : part * half_pad + half]
+
+
+def input_image(half, image, x_ref, dh_ref, dq_ref, dk_ref, dk_got, dv_ref, dv_got, vec, w_qkv, dx_ref, g_qkv, g_vec):
     width = x_ref.shape[1]
-    unit, inv_scale = normed(x_ref[...].astype(F32))
+    rows = pl.ds(pl.multiple_of(image * half, 8), half)
+    unit, inv_scale = normed(x_ref[rows, :].astype(F32))
     acts = (unit * vec[0:1, :] + vec[1:2, :]).astype(BF)
-    dq = dq_ref[...]
-    dk = (dk_own[0].astype(F32) + dk_got[...].astype(F32)).astype(BF)
-    dv = (dv_own[0].astype(F32) + dv_got[...].astype(F32)).astype(BF)
+    dq = dq_ref[rows, :]
+    dk = (dk_ref[0, rows, :].astype(F32) + dk_got[rows, :].astype(F32)).astype(BF)
+    dv = (dv_ref[0, rows, :].astype(F32) + dv_got[rows, :].astype(F32)).astype(BF)
     da = jnp.zeros(unit.shape, F32)
-    parts = []
     for at, piece in enumerate((dq, dk, dv)):
-        parts.append(tn(acts, piece))
-        da = da + nt(piece, w_qkv[:, at * width : (at + 1) * width])
-    dx_ref[...] = (dh_ref[...] + norm_backward(da, unit, inv_scale, vec[0:1, :])).astype(BF)
-    rows = [
-        jnp.sum(da * unit, axis=0, keepdims=True),
-        jnp.sum(da, axis=0, keepdims=True),
-        jnp.sum(dq.astype(F32), axis=0, keepdims=True),
-        jnp.sum(dv.astype(F32), axis=0, keepdims=True),
-    ]
-    part_vec = jnp.concatenate(rows + [jnp.zeros((4, width), F32)], axis=0)
-
-    @pl.when(image == 0)
-    def _():
-        g_vec[...] = part_vec
-        for at in range(3):
-            g_qkv[:, at * width : (at + 1) * width] = parts[at]
-
-    @pl.when(image > 0)
-    def _():
-        g_vec[...] += part_vec
-        for at in range(3):
-            g_qkv[:, at * width : (at + 1) * width] += parts[at]
+        cols = slice(at * width, (at + 1) * width)
+        g_qkv[:, cols] += tn(acts, piece)
+        da = da + nt(piece, w_qkv[:, :, cols].reshape(width, width))
+    dx_ref[rows, :] = (dh_ref[rows, :] + norm_backward(da, unit, inv_scale, vec[0:1, :])).astype(BF)
+    g_vec[0:1, :] += jnp.sum(da * unit, axis=0, keepdims=True)
+    g_vec[1:2, :] += jnp.sum(da, axis=0, keepdims=True)
+    g_vec[2:3, :] += jnp.sum(dq.astype(F32), axis=0, keepdims=True)
+    g_vec[3:4, :] += jnp.sum(dv.astype(F32), axis=0, keepdims=True)
 
 
 MESH = pl.DeviceIdType.MESH
@@ -705,51 +645,191 @@
         copy.wait()
 
 
-def reduce_kernel(
-    dps, groups, g_qkv, g_out, g_router, g_one, g_two, b_in, b_back,
-    o_qkv, o_out, o_router, o_vec, o_in, o_back,
-    near_out, near_in, far_out, far_in, deep_out, deep_in, total,
+def back_kernel(
+    dps, groups, images, grad, back_rows, h_ref, o_ref, vec, w_out, q_ref, k_ref, v_ref, x_ref, w_qkv,
+    g_router, g_in, g_back, b_in, b_back, p_all, in_other, back_other,
+    dx_ref, o_qkv, o_out, o_router, o_vec, o_in, o_back, w_in_sum, w_back_sum, in_recv, back_recv,
+    sum_in, sum_back, p_two, dh_ref, dq_ref, dk_ref, dv_ref, dk_got, dv_got, g_out, g_qkv, g_vec,
+    in_stage, back_stage, in_to, back_to, in_from, back_from,
+    near_out, near_in, far_out, far_in, deep_in, total,
     small_near, small_far, small_got, small_deep, bin_near, bin_far, bin_got, bin_deep,
     near_s, near_r, far_s, far_r, deep_s, deep_r, last_s, last_r,
+    p_sem, d_s, d_r, e_s, e_r, stage_sem, kin_s, kin_r, home_s, home_r, home_sem,
 ):
     dp, group, core = lax.axis_index("dp"), lax.axis_index("expert"), lax.axis_index("context")
-    width = g_out.shape[0]
+    tokens, width = dx_ref.shape
+    hosted = groups // 2
+    token_half = tokens // images
     rows = width // dps
     half = rows // 2
     near = (dp, group, 1 - core)
     peers = [(lax.rem(dp + step, dps), group, core) for step in range(1, dps)]
     others = [(dp, lax.rem(group + step, groups), core) for step in range(1, groups)]
+
+    def remote(src, dst, sems, slot, target):
+        return pltpu.make_async_remote_copy(
+            src_ref=src, dst_ref=dst, send_sem=sems[0].at[slot], recv_sem=sems[1].at[slot],
+            device_id=target, device_id_type=MESH,
+        )
+
+    sets = (
+        (back_other, back_recv, back_stage, back_to, back_from, g_back, w_back_sum),
+        (in_other, in_recv, in_stage, in_to, in_from, g_in, w_in_sum),
+    )
+
+    def sum_out(which, part, at, step):
+        other, recv = sets[which][:2]
+        size = recv.shape[2]
+        piece = size // 2
+        target = lax.rem(dp + step, dps)
+        src = other.at[at, pl.ds(pl.multiple_of(target * size, size) + part * piece, piece)]
+        dst = recv.at[at, step - 1, pl.ds(part * piece, piece)]
+        slot = ((which * 2 + part) * (hosted - 1) + at) * dps + step
+        return remote(src, dst, (e_s, e_r), slot, peers[step - 1])
+
+    def home_out(which, part, at):
+        to, back = sets[which][3:5]
+        piece = to.shape[1] // 2
+        here = pl.ds(part * piece, piece)
+        target = (dp, lax.rem(group + 2 * (at + 1), groups), core)
+        slot = (which * 2 + part) * (hosted - 1) + at
+        return pltpu.make_async_remote_copy(
+            src_ref=to.at[at, here], dst_ref=back.at[hosted - 2 - at, here],
+            send_sem=kin_s.at[slot], recv_sem=kin_r.at[(which * 2 + part) * (hosted - 1) + hosted - 2 - at],
+            device_id=target, device_id_type=MESH,
+        )
+
+    def home_in(which, part, at):
+        to, back = sets[which][3:5]
+        piece = to.shape[1] // 2
+        here = pl.ds(part * piece, piece)
+        slot = (which * 2 + part) * (hosted - 1) + at
+        return pltpu.make_async_remote_copy(
+            src_ref=to.at[at, here], dst_ref=back.at[at, here], send_sem=kin_s.at[slot], recv_sem=kin_r.at[slot],
+            device_id=near, device_id_type=MESH,
+        )
+
+    def send_home(which, part):
+        other, recv, stage, to = sets[which][:4]
+        size = recv.shape[2]
+        piece = size // 2
+        here = pl.ds(part * piece, piece)
+        for at in range(hosted - 1):
+            for step in range(1, dps):
+                sum_out(which, part, at, step).wait_recv()
+            own = other.at[at, pl.ds(pl.multiple_of(dp * size, size) + part * piece, piece)]
+            copies = (
+                pltpu.make_async_copy(recv.at[at, :, here], stage.at[pl.ds(0, dps - 1)], stage_sem.at[0]),
+                pltpu.make_async_copy(own, stage.at[dps - 1], stage_sem.at[1]),
+            )
+            for copy in copies:
+                copy.start()
+            for copy in copies:
+                copy.wait()
+            value = stage[0].astype(F32)
+            for step in range(1, dps):
+                value = value + stage[step].astype(F32)
+            to[at, here, :] = value.astype(BF)
+            home_out(which, part, at).start()
+
+    def load(image):
+        slot = lax.rem(image, 2)
+        return pltpu.make_async_copy(p_all.at[image], p_two.at[slot], p_sem.at[slot])
+
+    def swap(image, which):
+        here = pl.ds(pl.multiple_of(image * token_half, 8), token_half)
+        src, dst = ((dk_ref, dk_got), (dv_ref, dv_got))[which]
+        return remote(src.at[1, here], dst.at[here], (d_s, d_r), 2 * image + which, near)
+
+    load(0).start()
     greet(peers + others + [near])
+    for which in range(2):
+        for part in range(2):
+            for at in range(hosted - 1):
+                for step in range(1, dps):
+                    sum_out(which, part, at, step).start()
+    g_out[...] = jnp.zeros_like(g_out)
+    g_qkv[...] = jnp.zeros_like(g_qkv)
+    g_vec[...] = jnp.zeros_like(g_vec)
+
+    def back_step(image, _):
+        load(image).wait()
+
+        @pl.when(image + 1 < images)
+        def _():
+            load(image + 1).start()
+
+        backward_image(
+            token_half, image, grad, back_rows, h_ref, o_ref, vec, w_out, q_ref, k_ref, v_ref,
+            p_two.at[lax.rem(image, 2)], dh_ref, dq_ref, dk_ref, dv_ref, g_out, g_vec,
+        )
+        swap(image, 0).start()
+        swap(image, 1).start()
+
+        @pl.when(image == images - 2)
+        def _():
+            send_home(0, 0)
+
+        return 0
+
+    lax.fori_loop(0, images, back_step, 0)
+    send_home(0, 1)
+
     near_sems, far_sems, deep_sems, last_sems = (near_s, near_r), (far_s, far_r), (deep_s, deep_r), (last_s, last_r)
-    sources = [(g_qkv, at) for at in range(0, g_qkv.shape[1], width)] + [(g_out, 0)]
-    sizes = [width] * len(sources)
-    starts = [width * at for at in range(len(sources))]
+    sources = [(g_out, 0)] + [(g_qkv, at) for at in range(0, g_qkv.shape[1], width)]
+    theirs = pl.multiple_of((1 - core) * half, half)
+    ours = pl.multiple_of(core * half, half)
+
+    def cols_of(at):
+        return pl.ds(width * at, width)
+
+    def to_core(at):
+        ref, lane = sources[at]
+        for block in range(dps):
+            near_out[block, :, cols_of(at)] = ref[pl.ds(block * rows + theirs, half), lane : lane + width].astype(BF)
+        return send(near_out.at[:, :, cols_of(at)], near_in.at[:, :, cols_of(at)], near_sems, 2 + at, near)
+
+    first = [to_core(0)]
+
+    def input_step(image, _):
+        swap(image, 0).wait_recv()
+        swap(image, 1).wait_recv()
+        input_image(
+            token_half, image, x_ref, dh_ref, dq_ref, dk_ref, dk_got, dv_ref, dv_got, vec, w_qkv, dx_ref, g_qkv, g_vec
+        )
+        return 0
+
+    lax.fori_loop(0, images, input_step, 0)
+    for at in range(1, len(sources)):
+        first.append(to_core(at))
 
     deep = small_near.shape[2]
-    hosted = groups // 2
     tall = 2 * hosted
     router = 8 + tall
     bias_rows = [b_back[at // 2, at % 2] for at in range(tall)]
     bias_in = jnp.concatenate([b_in[at // 2, at % 2] for at in range(tall)], axis=0)
-    small = [g_one[0:4], g_two[0:3], jnp.zeros((1, width), F32)] + bias_rows + [g_router[...]]
+    small = [g_vec[...]] + bias_rows + [g_router[...]]
     spare = deep - router - g_router.shape[0]
     small = jnp.concatenate(small + ([jnp.zeros((spare, width), F32)] if spare else []), axis=0)
     for at in range(dps):
         small_near[0, at] = small[:, at * rows : (at + 1) * rows]
         bin_near[0, at] = bias_in[:, at * bin_near.shape[3] : (at + 1) * bin_near.shape[3]]
-    first = [
+    firsts = [
         send(small_near.at[0], small_near.at[1], near_sems, 0, near),
         send(bin_near.at[0], bin_near.at[1], near_sems, 1, near),
     ]
-    theirs = pl.multiple_of((1 - core) * half, half)
-    ours = pl.multiple_of(core * half, half)
+    second = []
     for at, (ref, lane) in enumerate(sources):
-        cols = pl.ds(starts[at], sizes[at])
-        for block in range(dps):
-            near_out[block, :, cols] = ref[pl.ds(block * rows + theirs, half), lane : lane + sizes[at]].astype(BF)
-        first.append(send(near_out.at[:, :, cols], near_in.at[:, :, cols], near_sems, 2 + at, near))
-    second = []
-    for copy in first[:2]:
+        cols = cols_of(at)
+        first[at].wait()
+        for step, peer in enumerate(peers):
+            target = lax.rem(dp + step + 1, dps)
+            block = ref[pl.ds(pl.multiple_of(target * rows, rows) + ours, half), lane : lane + width]
+            far_out[step, :, cols] = (block + near_in[target, :, cols].astype(F32)).astype(BF)
+            second.append(
+                send(far_out.at[step, :, cols], far_in.at[step, :, cols], far_sems, (2 + at) * dps + step, peer)
+            )
+    for copy in firsts:
         copy.wait()
     small_far[...] = small_near[0] + small_near[1]
     bin_far[...] = bin_near[0] + bin_near[1]
@@ -758,16 +838,21 @@
         target = lax.rem(dp + step + 1, dps)
         smalls.append(send(small_far.at[target], small_got.at[step], far_sems, step, peer))
         smalls.append(send(bin_far.at[target], bin_got.at[step], far_sems, dps + step, peer))
+    send_home(1, 0)
+    third = []
     for at, (ref, lane) in enumerate(sources):
-        cols = pl.ds(starts[at], sizes[at])
-        first[2 + at].wait()
-        for step, peer in enumerate(peers):
-            target = lax.rem(dp + step + 1, dps)
-            block = ref[pl.ds(pl.multiple_of(target * rows, rows) + ours, half), lane : lane + sizes[at]]
-            far_out[step, :, cols] = (block + near_in[target, :, cols].astype(F32)).astype(BF)
-            second.append(
-                send(far_out.at[step, :, cols], far_in.at[step, :, cols], far_sems, (2 + at) * dps + step, peer)
+        cols = cols_of(at)
+        mine = ref[pl.ds(pl.multiple_of(dp * rows, rows) + ours, half), lane : lane + width]
+        mine = mine + near_in[dp, :, cols].astype(F32)
+        for step in range(dps - 1):
+            second[at * (dps - 1) + step].wait()
+            mine = mine + far_in[step, :, cols].astype(F32)
+        deep_in[group, :, cols] = mine.astype(BF)
+        for step, peer in enumerate(others):
+            third.append(
+                send(deep_in.at[group, :, cols], deep_in.at[group, :, cols], deep_sems, at * groups + step, peer)
             )
+    send_home(1, 1)
     for copy in smalls:
         copy.wait()
     lone = small_far[dp]
@@ -777,27 +862,23 @@
         lone_in = lone_in + bin_got[step]
     small_deep[group] = lone
     bin_deep[group] = lone_in
-    third, deep_bin = [], []
+    deep_small = []
     for step, peer in enumerate(others):
-        third.append(send(small_deep.at[group], small_deep.at[group], deep_sems, step, peer))
-        deep_bin.append(
-            send(bin_deep.at[group], bin_deep.at[group], deep_sems, (1 + len(sources)) * groups + step, peer)
-        )
-    for at, (ref, lane) in enumerate(sources):
-        cols = pl.ds(starts[at], sizes[at])
-        mine = ref[pl.ds(pl.multiple_of(dp * rows, rows) + ours, half), lane : lane + sizes[at]]
-        mine = mine + near_in[dp, :, cols].astype(F32)
-        for step in range(dps - 1):
-            second[at * (dps - 1) + step].wait()
-            mine = mine + far_in[step, :, cols].astype(F32)
-        deep_in[group, :, cols] = mine.astype(BF)
-        for step, peer in enumerate(others):
-            third.append(
-                send(deep_in.at[group, :, cols], deep_in.at[group, :, cols], deep_sems, (1 + at) * groups + step, peer)
-            )
-    for copy in third[: groups - 1]:
-        copy.wait()
-    for copy in deep_bin:
+        slot = len(sources) * groups + step
+        deep_small.append(send(small_deep.at[group], small_deep.at[group], deep_sems, slot, peer))
+        deep_small.append(send(bin_deep.at[group], bin_deep.at[group], deep_sems, groups + slot, peer))
+    last = []
+    here = pl.ds(ours, half)
+    for at in range(len(sources)):
+        cols = cols_of(at)
+        for step in range(groups - 1):
+            third[at * (groups - 1) + step].wait()
+        done = deep_in[0, :, cols].astype(F32)
+        for source in range(1, groups):
+            done = done + deep_in[source, :, cols].astype(F32)
+        total[here, cols] = done
+        last.append(send(total.at[here, cols], total.at[here, cols], last_sems, at, near))
+    for copy in deep_small:
         copy.wait()
     lone = small_deep[0]
     for at in range(1, groups):
@@ -810,47 +891,42 @@
         kin = lax.rem(away, 2) == 0
         pick_in, pick_back = jnp.zeros(o_in.shape, F32), jnp.zeros(o_back.shape, F32)
         for which in range(hosted):
-            here = away // 2 == which
-            pick_in = jnp.where(here, bin_deep[at, 2 * which : 2 * which + 2], pick_in)
-            pick_back = jnp.where(here, small_deep[at, 8 + 2 * which : 10 + 2 * which], pick_back)
+            found = away // 2 == which
+            pick_in = jnp.where(found, bin_deep[at, 2 * which : 2 * which + 2], pick_in)
+            pick_back = jnp.where(found, small_deep[at, 8 + 2 * which : 10 + 2 * which], pick_back)
         grad_in = grad_in + jnp.where(kin, pick_in, 0.0)
         grad_back = grad_back + jnp.where(kin, pick_back, 0.0)
     o_in[...] = grad_in
     o_back[...] = grad_back
-    last = []
-    here = pl.ds(ours, half)
-    for at in range(len(sources)):
-        cols = pl.ds(starts[at], sizes[at])
-        for step in range(groups - 1):
-            third[(1 + at) * (groups - 1) + step].wait()
-        done = deep_in[0, :, cols].astype(F32)
-        for source in range(1, groups):
-            done = done + deep_in[source, :, cols].astype(F32)
-        total[here, cols] = done
-        last.append(send(total.at[here, cols], total.at[here, cols], last_sems, at, near))
-    for at in range(len(sources)):
-        last[at].wait()
-    o_qkv[...] = total[:, : 3 * width]
-    o_out[...] = total[:, 3 * width : 4 * width]
-
-
-def finish_kernel(count, g_in, g_back, *rest):
-    others, rest = rest[: 2 * count], rest[2 * count :]
-    _, o_in, o_back, sum_in, sum_back, sems_s, sems_r, local = rest
-    dp, group, core = lax.axis_index("dp"), lax.axis_index("expert"), lax.axis_index("context")
-    near = (dp, group, 1 - core)
-    greet([near])
-    copies = []
-    for at, (own, total, out) in enumerate(((g_in, sum_in, o_in), (g_back, sum_back, o_back))):
+    for copy in last:
+        copy.wait()
+    o_qkv[...] = total[:, width : 4 * width]
+    o_out[...] = total[:, :width]
+
+    stores = []
+    for which, (_, _, _, to, back, own, out) in enumerate(sets):
+        for part in range(2):
+            for at in range(hosted - 1):
+                home_in(which, part, at).wait_recv()
         value = own[...]
-        for other in others[at * count : (at + 1) * count]:
-            value = value + other[...].astype(F32)
-        total[...] = value
-        copies.append(send(total, out.at[core], (sems_s, sems_r), at, near))
-        here = pltpu.make_async_copy(total, out.at[core], local.at[at])
-        here.start()
-        copies.append(here)
-    for copy in copies:
+        for at in range(hosted - 1):
+            value = value + back[at].astype(F32)
+        whole = (sum_back, sum_in)[which]
+        whole[...] = value
+        stores.append(send(whole, out.at[core], (home_s, home_r), which, near))
+        copy = pltpu.make_async_copy(whole, out.at[core], home_sem.at[which])
+        copy.start()
+        stores.append(copy)
+    for which in range(2):
+        for part in range(2):
+            for at in range(hosted - 1):
+                home_out(which, part, at).wait_send()
+                for step in range(1, dps):
+                    sum_out(which, part, at, step).wait_send()
+    for image in range(images):
+        for which in range(2):
+            swap(image, which).wait_send()
+    for copy in stores:
         copy.wait()
 
 
@@ -869,7 +945,6 @@
     half_pad = up(half, 16)
     hosted = groups // 2
     context = lax.axis_index("context")
-    swap = [(0, 1), (1, 0)]
     V, A = pltpu.VMEM, pl.ANY
     dma = pltpu.SemaphoreType.DMA
     rows = w_qkv.shape[0]
@@ -932,11 +1007,6 @@
         moved=40 * tokens * width,
     )(x, w_qkv, w_out, w_router, vectors, b_in, b_back, route_rows, keys[:, None], keys[None, :], bias, w_in, w_back)
     qkv_all, out_all, router_rows, b_ins, b_backs, vec, slots, q, k, v, p, o, after, acts, *expert_w = made
-    qkv_all = qkv_all.reshape(width, 3 * width)
-    out_all = out_all.reshape(width, width)
-    row = ((half, width), lambda i: (i, 0))
-    cube = ((1, keys_pad, width), lambda i: (i, 0, 0))
-    prob = ((1, HEADS, half, keys_pad), lambda i: (i, 0, 0, 0))
 
     rows_all = 4 * cap_pad
     deep = hosted * cap_pad
@@ -999,71 +1069,51 @@
     )(acts, grad, after, router_rows, route_rows, slots, b_ins, b_backs, *expert_w)
     back_rows, output, g_router, g_in, g_back, g_in_other, g_back_other, g_b_in, g_b_back, *_ = made
 
-    others = []
-    for part in (g_in_other, g_back_other):
-        part = lax.psum_scatter(part, "dp", scatter_dimension=1, tiled=True)
-        for step in range(1, hosted):
-            perm = [(at, (at + 2 * step) % groups) for at in range(groups)]
-            others.append(lax.ppermute(part[step - 1], "expert", perm))
-
-    halves = ((2, half, width), lambda i: (0, i, 0))
-    fixed = lambda i: (0, 0)
-    dh, dq, dk, dv, g_out, g_vec_two = call(
-        backward_kernel,
-        "backward",
-        (images,),
-        [row, row, row, row, None, None, row, cube, cube, prob],
-        [
-            (row, ((tokens, width), F32)),
-            (row, ((tokens, width), BF)),
-            (halves, ((2, tokens, width), BF)),
-            (halves, ((2, tokens, width), BF)),
-            (((width, width), fixed), ((width, width), F32)),
-            (((8, width), fixed), ((8, width), F32)),
-        ],
-        flops=2 * tokens * width * (2 * width + 8 * keys_pad),
-        moved=30 * tokens * width,
-    )(grad, back_rows, after, o, vec, out_all, q, k, v, p)
-
-    dk_got = lax.ppermute(dk[1], "context", swap)
-    dv_got = lax.ppermute(dv[1], "context", swap)
-    own_half = ((1, half, width), lambda i: (0, i, 0))
-    dx, g_qkv, g_vec_one = call(
-        input_kernel,
-        "input",
-        (images,),
-        [row, row, row, own_half, row, own_half, row, None, None],
-        [
-            (row, ((tokens, width), BF)),
-            (((width, 3 * width), fixed), ((width, 3 * width), F32)),
-            (((8, width), fixed), ((8, width), F32)),
-        ],
-        flops=12 * tokens * width * width,
-        moved=20 * tokens * width,
-    )(x, dh, dq, dk, dk_got, dv, dv_got, vec, qkv_all)
-
     wide = 4 * width
     halves_of = rows // 2
     small = up(8 + 2 * hosted + experts, 8)
-    grad_qkv, grad_out, grad_router, grad_vec, grad_b_in, grad_b_back = comm_call(
-        partial(reduce_kernel, dps, groups),
-        "reduce",
+    kin_slots = 4 * (hosted - 1)
+    made = comm_call(
+        partial(back_kernel, dps, groups, images),
+        "back",
         1,
-        [V] * 7,
+        [V] * 16 + [A] * 3,
         [
+            ((tokens, width), BF, V),
             ((rows, 3 * width), F32, V),
             ((rows, width), F32, V),
             ((experts, rows), F32, V),
             ((7, rows), F32, V),
             ((per_device, rows_back), F32, V),
             ((per_device, rows), F32, V),
+            (w_in.shape, F32, A),
+            (w_back.shape, F32, A),
+            ((hosted - 1, dps - 1, rows, ff), BF, A),
+            ((hosted - 1, dps - 1, rows_back, width), BF, A),
         ],
         [
+            pltpu.VMEM((rows, ff), F32),
+            pltpu.VMEM((rows_back, width), F32),
+            pltpu.VMEM((2, HEADS, half, keys_pad), BF),
+            pltpu.VMEM((tokens, width), F32),
+            pltpu.VMEM((tokens, width), BF),
+            pltpu.VMEM((2, tokens, width), BF),
+            pltpu.VMEM((2, tokens, width), BF),
+            pltpu.VMEM((tokens, width), BF),
+            pltpu.VMEM((tokens, width), BF),
+            pltpu.VMEM((width, width), F32),
+            pltpu.VMEM((width, 3 * width), F32),
+            pltpu.VMEM((8, width), F32),
+            pltpu.VMEM((dps, rows // 2, ff), BF),
+            pltpu.VMEM((dps, rows_back // 2, width), BF),
+            pltpu.VMEM((hosted - 1, rows, ff), BF),
+            pltpu.VMEM((hosted - 1, rows_back, width), BF),
+            pltpu.VMEM((hosted - 1, rows, ff), BF),
+            pltpu.VMEM((hosted - 1, rows_back, width), BF),
             pltpu.VMEM((dps, halves_of, wide), BF),
             pltpu.VMEM((dps, halves_of, wide), BF),
             pltpu.VMEM((dps - 1, halves_of, wide), BF),
             pltpu.VMEM((dps - 1, halves_of, wide), BF),
-            pltpu.VMEM((8, LANES), BF),
             pltpu.VMEM((groups, halves_of, wide), BF),
             pltpu.VMEM((rows, wide), F32),
             pltpu.VMEM((2, dps, small, rows), F32),
@@ -1076,19 +1126,17 @@
             pltpu.VMEM((groups, 2 * hosted, rows_back), F32),
             dma((6,)), dma((6,)), dma((6 * dps,)), dma((6 * dps,)),
             dma((6 * groups,)), dma((6 * groups,)), dma((4,)), dma((4,)),
+            dma((2,)), dma((2 * images,)), dma((2 * images,)), dma((kin_slots * dps,)), dma((kin_slots * dps,)),
+            dma((2,)), dma((kin_slots,)), dma((kin_slots,)), dma((2,)), dma((2,)), dma((2,)),
         ],
-        moved=20 * width * wide,
-    )(g_qkv, g_out, g_router, g_vec_one, g_vec_two, g_b_in, g_b_back)
-
-    grad_w_in, grad_w_back = comm_call(
-        partial(finish_kernel, hosted - 1),
-        "finish",
-        3,
-        [V] * (2 * hosted + 1),
-        [(w_in.shape, F32, A), (w_back.shape, F32, A)],
-        [pltpu.VMEM((rows, ff), F32), pltpu.VMEM((rows_back, width), F32), dma((2,)), dma((2,)), dma((2,))],
-        moved=16 * rows * ff,
-    )(g_in, g_back, *others, grad_vec)
+        flops=2 * tokens * width * (8 * width + 8 * keys_pad),
+        moved=60 * tokens * width,
+        vmem=62,
+    )(
+        grad, back_rows, after, o, vec, out_all, q, k, v, x, qkv_all, g_router, g_in, g_back, g_b_in, g_b_back,
+        p, g_in_other, g_back_other,
+    )
+    dx, grad_qkv, grad_out, grad_router, grad_vec, grad_b_in, grad_b_back, grad_w_in, grad_w_back, *_ = made
     return (
         output.reshape(images, half, width),
         dx.reshape(images, half, width),

time: 358 us -> 312 us (0.87)
  waiting for transfers between devices: 43.1 us -> 0 us
  Pallas kernels: 277 us -> 296 us
  between operations: 14.2 us -> 0.73 us
  starting transfers between devices: 5.11 us -> 0 us
    reduce_scatter x2 -> x0, waiting for transfers between devices: 42.4 us -> none  [shards(): part = lax.psum_scatter(part, 'dp', scatter_dimension=1, tiled=True)]
    pallas_call x4 -> x1, Pallas kernels: 82.3 us -> 102 us  [shards(): comm_call(partial(back_kernel, dps, groups, images), 'back', 1, [V] * 16...]
    ppermute x4 -> x0, starting transfers between devices: 5.03 us -> none  [the longest x2 4.79 us: shards(): others.append(lax.ppermute(part[step - 1], 'expert', perm))]
    unnamed x36 -> x31, local copies, waits for them, and re-layouts: 11.6 us -> 10.8 us
  transfers between devices with their start and end apart: 6 -> 0, of which waited for: 2 -> 0; matrix products, arithmetic and copies ran while one was open for 1% -> 0% of each run, Pallas kernels for 21% -> 0%
where the time goes in v5:
time: 312 us
  Pallas kernels  296 us (95%)
  local copies, waits for them, and re-layouts  11.6 us (4%)
  other arithmetic  3.62 us (1%)
    pallas_call x1, Pallas kernels, shards(): comm_call(partial(experts_kernel, groups, dps, images, cap_pad), 'experts...  121 us
    pallas_call x1, Pallas kernels, shards(): comm_call(partial(back_kernel, dps, groups, images), 'back', 1, [V] * 16...  102 us
    pallas_call x1, Pallas kernels, shards(): comm_call(partial(start_kernel, dps, groups, images, cap, cap_pad), 'fron...  73.3 us
    unnamed x31, local copies, waits for them, and re-layouts  10.8 us

profile of v5, /device:TPU:0, one launch (start us, length us, event | category | flops | bytes accessed | tf_op | source)
XLA Modules:
  0.0 311.9 jit_solution(11876614060685365281)
XLA Ops:
  0.6 1.3 bitcast_add_fusion.key_row
  1.9 0.7 multiply_bitcast_fusion
  2.6 0.7 compare_select_fusion
  3.3 0.1 slice_select_fusion.1
  3.4 0.1 pad_maximum_fusion
  3.5 0.6 broadcast_in_dim.15.bias
  4.1 1.4 copy.25.w_router
  5.5 0.2 copy.24
  5.7 0.8 iota_add_fusion.key_col
  6.5 73.3 %front.1 = (bf16[4,128,1536]{2,1,0:T(8,128)(2,1)}, bf16[4,128,512]{2,1,0:T(8,128)(2,1)}, bf16[8,512]{1,0:T(8,128)(2,1)}, bf16[2,4,2,512]{3,2,1,0:T(2,128)(2,1)},...) custom-call(bf16[888,512]{1,0:T(8,128)(2,1)} %bitcast.15, ...), custom_call_target="tpu_custom_call" | custom-call | flops 5935988736 | bytes 18186240 | tf_op jit(solution)/shard_map/front/pallas_call | solution.py:966
  79.8 121.0 %experts.1 = (f32[888,512]{1,0:T(8,128)}, bf16[888,512]{1,0:T(8,128)(2,1)}, f32[8,512]{1,0:T(8,128)}, f32[128,2048]{1,0:T(8,128)}, f32[512,512]{1,0:T(8,128)}, /...) custom-call(bf16[888,512]{1,0:T(8,128)(2,1)} %get-tuple-element.46.a, ...), custom_call_target="tpu_custom_call" | custom-call | flops 39460012032 | bytes 25870336 | tf_op jit(solution)/shard_map/experts/pallas_call | solution.py:1013
  200.8 0.0 copy-start.2
  200.8 101.7 %back.1 = (bf16[888,512]{1,0:T(8,128)(2,1)}, f32[128,1536]{1,0:T(8,128)}, f32[128,512]{1,0:T(8,128)}, f32[8,128]{1,0:T(8,128)}, f32[7,128]{1,0:T(8,128)}, /*inde...) custom-call(bf16[888,512]{1,0:T(8,128)(2,1)} %bitcast.18, ...), custom_call_target="tpu_custom_call" | custom-call | flops 8147435520 | bytes 27279360 | tf_op jit(solution)/shard_map/back/pallas_call | solution.py:1076
  302.5 0.0 copy-start.3
  302.5 0.0 copy-start.8
  302.5 0.0 copy-start.4
  302.5 0.0 copy-done.2
  302.5 0.9 copy.36
  303.4 0.5 copy-done.3
  304.0 0.0 copy-start.5
  304.0 0.0 copy-start.7
  304.0 0.0 copy-start.1
  304.0 0.9 copy.37
  304.9 0.0 copy-done.8
  304.9 0.6 copy.38
  305.5 0.0 copy-done.4
  305.5 0.9 copy.39
  306.4 0.0 copy-done.5
  306.4 0.7 copy.40
  307.1 0.0 copy-done.7
  307.1 0.6 copy.41
  307.7 0.0 copy-done.1
  307.7 0.0 copy-start.6
  307.7 0.0 copy-start
  307.7 1.3 copy.42
  309.0 0.0 copy-done.6
  309.0 0.6 copy.43
  309.6 0.4 copy-done
  310.0 0.0 copy-start.9
  310.0 1.3 copy.44
  311.4 0.0 copy-done.9
  311.4 0.6 copy.45
  (1 shorter events, 0.0 us)
Async XLA Ops:
  200.8 101.8 %copy-start.2 = (bf16[888,512]{1,0:T(8,128)(2,1)S(1)}, bf16[888,512]{1,0:T(8,128)(2,1)}, u32[]{:S(2)}) copy-start(bf16[888,512]{1,0:T(8,128)(2,1)} %get-tuple-element.56) | copy-start | bytes 2727940
  302.5 1.5 copy-start.3
  302.5 2.4 copy-start.8
  302.5 3.0 copy-start.4
  304.0 2.4 copy-start.5
  304.0 3.1 copy-start.7
  304.0 3.7 %copy-start.1 = (f32[2,128,2048]{2,1,0:T(8,128)S(1)}, f32[2,128,2048]{2,1,0:T(8,128)}, u32[]{:S(2)}) copy-start(f32[2,128,2048]{2,1,0:T(8,128)} %get-tuple-element.100) | copy-start | bytes 6291460
  307.7 1.3 copy-start.6
  307.7 2.4 copy-start
  310.0 1.3 copy-start.9

commit v6 on v5

--- a/solution.py
+++ b/solution.py
@@ -60,14 +60,14 @@
     groups, dps, images, cap_pad, acts, grad, after, router, routes, slots, b_in, b_back, *rest
 ):
     hosted = groups // 2
-    w_in, kin_in, w_back, kin_back, rest = *rest[:4], rest[4:]
-    back_rows, output, g_router, g_in, g_back, g_in_other, g_back_other, g_b_in, g_b_back = rest[:9]
-    w_in_far, w_back_far, rest = rest[9], rest[10], rest[11:]
+    w_in, kin_in, w_back, kin_back, grads, rest = *rest[:5], rest[5:]
+    back_rows, mixed, far_rows, g_router, g_in, g_back, g_in_other, g_back_other, g_b_in, g_b_back = rest[:10]
+    w_in_far, w_back_far, rest = rest[10], rest[11], rest[12:]
     tok, info, made_rows, w_in_v, w_back_v, rows_v, hidden, grad_pre, delta, slope = rest[:10]
     in_send, in_recv, back_send, back_recv, dots, dots_got, to_near, from_near, to_far, from_far = rest[10:20]
     places, x_s, x_r, w_sem, r_s, r_r, p_s, p_r, store_sem, load_sem, w_s, w_r, w_own = rest[20:]
     dp, group, core = lax.axis_index("dp"), lax.axis_index("expert"), lax.axis_index("context")
-    tokens, width = output.shape
+    tokens, width = mixed.shape
     ff = w_in_v.shape[1]
     rows_in, rows_back = width // dps, ff // dps
     mate = group + 1 - 2 * lax.rem(group, 2)
@@ -79,7 +79,7 @@
             device_id=target, device_id_type=MESH,
         )
 
-    pools = (info, tok.at[0], tok.at[1])
+    pools = (info, tok.at[0])
     moves = {}
     for at, pool in enumerate(pools):
         moves[at, 1] = remote(pool.at[0], pool.at[1], (x_s, x_r), 3 * at, near)
@@ -99,7 +99,17 @@
         part = far.at[at, pl.ds(pl.multiple_of(dp * size, size), size)]
         if step == 0:
             return pltpu.make_async_copy(kin.at[at], part, w_own.at[2 * at + which])
-        return remote(kin.at[at], part, (w_s, w_r), (2 * at + which) * dps + step, along(step))
+        target = (square(dp)[step - 1], group, core) if dps == 4 else along(step)
+        return remote(kin.at[at], part, (w_s, w_r), (2 * at + which) * dps + step - 1, target)
+
+    def onward(at, which):
+        kin, far = ((kin_in, w_in_far), (kin_back, w_back_far))[which]
+        return [
+            remote(ref, ref, (w_s, w_r), (2 * at + which) * dps + 2 + slot, (target, group, core))
+            for slot, (ref, target) in enumerate(relay(far.at[at], kin.shape[1], dp))
+        ]
+
+    direct = 3 if dps == 4 else dps
 
     def load(which, wait):
         for at in range(hosted):
@@ -112,8 +122,15 @@
             def _():
                 if at and not wait:
                     for part in range(2):
-                        for step in range(dps):
-                            gather(at - 1, part, step).wait()
+                        gather(at - 1, part, 0).wait()
+                        for step in range(1, direct):
+                            if dps == 4:
+                                gather(at - 1, part, step).wait_send()
+                            else:
+                                gather(at - 1, part, step).wait()
+                        if dps == 4:
+                            for copy in onward(at - 1, part):
+                                copy.wait()
                 for copy in copies:
                     copy.wait() if wait else copy.start()
 
@@ -134,6 +151,7 @@
     mine = (
         pltpu.make_async_copy(acts, tok.at[0, 0], load_sem.at[0]),
         pltpu.make_async_copy(grad, tok.at[1, 0], load_sem.at[1]),
+        pltpu.make_async_copy(grads, tok.at[1, pl.ds(1, 3)], load_sem.at[2]),
     )
     for copy in mine:
         copy.start()
@@ -144,7 +162,7 @@
         moves[1, hop].start()
     for at in range(hosted - 1):
         for part in range(2):
-            for step in range(dps):
+            for step in range(direct):
                 gather(at, part, step).start()
     logits = nt(router[...], tok[0, 0])
     logits = jnp.exp(logits - jnp.max(logits, axis=0, keepdims=True))
@@ -156,18 +174,18 @@
             jnp.where(routes[choice : choice + 1, :] == ids, probs, 0.0), axis=0, keepdims=True
         )
     info[0, 4:8, :] = jnp.zeros((4, tokens), F32)
-    mine[1].wait()
     for hop in (2, 1):
         moves[0, hop].start()
-        moves[2, hop].start()
+    mine[1].wait()
+    mine[2].wait()
     g_b_in[...] = jnp.zeros_like(g_b_in)
     g_b_back[...] = jnp.zeros_like(g_b_back)
 
     def near_out(at):
         return remote(to_near.at[at], from_near.at[at], (p_s, p_r), at, near)
 
-    def far_out(at):
-        return remote(to_far.at[at], from_far.at[at], (p_s, p_r), 4 + at, across)
+    def far_out():
+        return remote(to_far, from_far, (p_s, p_r), 4, across)
 
     def dots_out(source, target):
         return remote(dots.at[source], dots_got.at[source - 1], (p_s, p_r), 5 + source, target)
@@ -218,13 +236,12 @@
 
         def chunk(image, _):
             rows, part = summed(2, image)
-            to_far[0, rows, :] = (part[:, :width] + from_near[0, rows, :].astype(F32)).astype(BF)
-            to_far[1, rows, :] = (part[:, width:] + from_near[1, rows, :].astype(F32)).astype(BF)
+            to_far[rows, :] = (part[:, :width] + from_near[0, rows, :].astype(F32)).astype(BF)
+            far_rows[rows, :] = (part[:, width:] + from_near[1, rows, :].astype(F32)).astype(BF)
             return 0
 
         lax.fori_loop(0, images, chunk, 0)
-        far_out(0).start()
-        far_out(1).start()
+        far_out().start()
 
     def expert(which, _):
         load(which, True)
@@ -236,18 +253,18 @@
 
             @pl.when(jnp.logical_and(which == 0, source == 1))
             def _():
-                for at in range(3):
+                for at in range(2):
                     moves[at, 1].wait_recv()
 
             @pl.when(jnp.logical_and(which == 0, source == 2))
             def _():
-                for at in range(3):
+                for at in range(2):
                     moves[at, 2].wait_recv()
                     moves[at, 3].start()
 
             @pl.when(jnp.logical_and(which == 0, source == 3))
             def _():
-                for at in range(3):
+                for at in range(2):
                     moves[at, 3].wait_recv()
 
             rows = pl.ds(pl.multiple_of(source * cap_pad, 16), cap_pad)
@@ -284,6 +301,17 @@
                 grad_pre[rows, cols] = dz.astype(BF)
             made_rows[source, spot, :width] = nt(grad_pre[rows, :], w_in_v[...]).astype(BF)
 
+            if dps == 4:
+                for part in range(2):
+
+                    @pl.when(jnp.logical_and(which == 0, turn == 1 + part))
+                    def _():
+                        for at in range(hosted - 1):
+                            for step in range(1, direct):
+                                gather(at, part, step).wait_recv()
+                            for copy in onward(at, part):
+                                copy.start()
+
             @pl.when(jnp.logical_and(last == 1, source == 3))
             def _():
                 dots_out(3, diagonal).start()
@@ -362,14 +390,12 @@
     place(0)
     near_out(2).wait_recv()
     near_out(3).wait_recv()
-    far_out(0).wait_recv()
-    far_out(1).wait_recv()
+    far_out().wait_recv()
 
     def chunk(image, _):
         rows, part = summed(0, image)
-        back_rows[rows, :] += part[:, :width] + from_near[2, rows, :].astype(F32) + from_far[0, rows, :].astype(F32)
-        out = part[:, width:] + from_near[3, rows, :].astype(F32) + from_far[1, rows, :].astype(F32)
-        output[rows, :] = (after[rows, :] + out).astype(BF)
+        back_rows[rows, :] += part[:, :width] + from_near[2, rows, :].astype(F32) + from_far[rows, :].astype(F32)
+        mixed[rows, :] = after[rows, :] + part[:, width:] + from_near[3, rows, :].astype(F32)
         return 0
 
     lax.fori_loop(0, images, chunk, 0)
@@ -386,8 +412,7 @@
         copy.wait_send()
     for at in range(4):
         near_out(at).wait_send()
-    for at in range(2):
-        far_out(at).wait_send()
+    far_out().wait_send()
     for source, target in ((1, near), (2, across), (3, diagonal)):
         dots_out(source, target).wait_send()
 
@@ -516,6 +541,26 @@
     return copy
 
 
+def remote_copy(src, dst, sems, slot, device):
+    return pltpu.make_async_remote_copy(
+        src_ref=src, dst_ref=dst, send_sem=sems[0].at[slot], recv_sem=sems[1].at[slot],
+        device_id=device, device_id_type=MESH,
+    )
+
+
+def square(dp):
+    return dp + 1 - 2 * lax.rem(dp, 2), lax.rem(dp + 2, 4)
+
+
+def relay(ref, size, dp):
+    side, across = square(dp)
+    half = size // 2
+    return (
+        (ref.at[pl.ds(pl.multiple_of(across * size, size) + half, half)], side),
+        (ref.at[pl.ds(pl.multiple_of(side * size, size), half)], across),
+    )
+
+
 def greet(devices):
     barrier = pltpu.get_barrier_semaphore()
     for device in devices:
@@ -540,11 +585,11 @@
 
 def start_kernel(
     dps, groups, images, cap, cap_pad, x, w_qkv, w_out, w_router, vectors, b_in, b_back, routes, key_col, key_row, bias,
-    w_in, w_back,
+    w_in, w_back, grad,
     qkv_all, out_all, router_rows, b_in_all, back_all, vec, slots,
-    q_ref, k_ref, v_ref, p_ref, o_ref, h_ref, a_ref, in_all, in_kin, back_w_all, back_kin,
+    q_ref, k_ref, v_ref, p_ref, o_ref, h_ref, a_ref, in_all, in_kin, back_w_all, back_kin, grads,
     x_other, router_all, vec_all, p_all, w_in_f, w_back_f, w_in_v, w_back_v,
-    far_send, far_recv, near_send, near_recv, deep_send, deep_recv, w_s, w_r, local,
+    far_send, far_recv, near_send, near_recv, deep_send, deep_recv, w_s, w_r, local, rows_s, rows_r,
 ):
     dp, group, core = lax.axis_index("dp"), lax.axis_index("expert"), lax.axis_index("context")
     rows = w_qkv.shape[0]
@@ -559,7 +604,13 @@
     ]
     for copy in loads:
         copy.start()
-    greet(peers + kin + [near])
+    mate = group + 1 - 2 * lax.rem(group, 2)
+    across = (dp, mate, core)
+    greet(peers + kin + [near, across])
+    rows_out = [
+        send(grad, grads.at[1], (rows_s, rows_r), 1, across),
+        send(grad, grads.at[0], (rows_s, rows_r), 0, near),
+    ]
     far, close, deep = (far_send, far_recv), (near_send, near_recv), (deep_send, deep_recv)
     waits = [send(x, x_other, close, 0, near)]
     qkv_all[dp] = w_qkv[...].astype(BF)
@@ -581,7 +632,7 @@
             smalls.append(send(ref.at[dp], ref.at[dp], far, step * 6 + 2 + at, peer))
         for at, ref in enumerate((b_in_all, back_all)):
             biases.append(send(ref.at[0, dp], ref.at[0, dp], far, step * 6 + 4 + at, peer))
-    own_copies = []
+    own_copies, direct = [], ([], [])
     for at, (wide, low, out, kin_out) in enumerate(
         ((w_in_f, w_in_v, in_all, in_kin), (w_back_f, w_back_v, back_w_all, back_kin))
     ):
@@ -593,11 +644,30 @@
             own_copies.append(
                 send(low, kin_out.at[hosted - 2 - step], (w_s, w_r), at * (dps + hosted) + dps + step, peer)
             )
-        for step, peer in enumerate(peers):
-            own_copies.append(send(low, out.at[part], (w_s, w_r), at * (dps + hosted) + step, peer))
+        if dps == 4:
+            for slot, target in enumerate(square(dp)):
+                direct[at].append(
+                    send(low, out.at[part], (w_s, w_r), at * (dps + hosted) + slot, (target, group, core))
+                )
+        else:
+            for step, peer in enumerate(peers):
+                own_copies.append(send(low, out.at[part], (w_s, w_r), at * (dps + hosted) + step, peer))
         here = pltpu.make_async_copy(low, out.at[part], local.at[2 + at])
         here.start()
         own_copies.append(here)
+
+    def onward(at):
+        out, size = ((in_all, w_in_v.shape[0]), (back_w_all, w_back_v.shape[0]))[at]
+        return [
+            remote_copy(ref, ref, (w_s, w_r), at * (dps + hosted) + 2 + slot, (target, group, core))
+            for slot, (ref, target) in enumerate(relay(out, size, dp))
+        ]
+
+    def pass_on(at):
+        for copy in direct[at]:
+            copy.wait_recv()
+        for copy in onward(at):
+            copy.start()
 
     tokens = routes.shape[1]
     experts = w_router.shape[1]
@@ -637,24 +707,42 @@
             half, image, dps, x, x_other, bias, vec, qkv_all, out_all, q_ref, k_ref, v_ref, p_all, o_ref, h_ref, a_ref
         )
         pltpu.make_async_copy(p_all.at[image], p_ref.at[image], local.at[4]).start()
+        if dps == 4:
+
+            @pl.when(image == images - 2)
+            def _():
+                pass_on(0)
+
         return 0
 
     lax.fori_loop(0, images, image_step, 0)
+    if dps == 4:
+        pass_on(1)
+    rows_out[0].wait()
+    rows_out[0] = send(grads.at[1], grads.at[2], (rows_s, rows_r), 2, near)
     pltpu.make_async_copy(p_all, p_ref, local.at[4]).wait()
+    for copy in rows_out:
+        copy.wait()
     for copy in own_copies:
         copy.wait()
+    if dps == 4:
+        for at in range(2):
+            for copy in direct[at]:
+                copy.wait_send()
+            for copy in onward(at):
+                copy.wait()
 
 
 def back_kernel(
     dps, groups, images, grad, back_rows, h_ref, o_ref, vec, w_out, q_ref, k_ref, v_ref, x_ref, w_qkv,
-    g_router, g_in, g_back, b_in, b_back, p_all, in_other, back_other,
-    dx_ref, o_qkv, o_out, o_router, o_vec, o_in, o_back, w_in_sum, w_back_sum, in_recv, back_recv,
+    g_router, g_in, g_back, b_in, b_back, mixed, p_all, in_other, back_other, far_rows,
+    dx_ref, output, o_qkv, o_out, o_router, o_vec, o_in, o_back, w_in_sum, w_back_sum, in_recv, back_recv,
     sum_in, sum_back, p_two, dh_ref, dq_ref, dk_ref, dv_ref, dk_got, dv_got, g_out, g_qkv, g_vec,
     in_stage, back_stage, in_to, back_to, in_from, back_from,
     near_out, near_in, far_out, far_in, deep_in, total,
     small_near, small_far, small_got, small_deep, bin_near, bin_far, bin_got, bin_deep,
-    near_s, near_r, far_s, far_r, deep_s, deep_r, last_s, last_r,
-    p_sem, d_s, d_r, e_s, e_r, stage_sem, kin_s, kin_r, home_s, home_r, home_sem,
+    got_rows, near_s, near_r, far_s, far_r, deep_s, deep_r, last_s, last_r,
+    rows_s, rows_r, p_sem, d_s, d_r, e_s, e_r, stage_sem, kin_s, kin_r, home_s, home_r, home_sem,
 ):
     dp, group, core = lax.axis_index("dp"), lax.axis_index("expert"), lax.axis_index("context")
     tokens, width = dx_ref.shape
@@ -748,6 +836,8 @@
             for at in range(hosted - 1):
                 for step in range(1, dps):
                     sum_out(which, part, at, step).start()
+    mate = group + 1 - 2 * lax.rem(group, 2)
+    rows_out = send(far_rows, got_rows, (rows_s, rows_r), 0, (dp, mate, core))
     g_out[...] = jnp.zeros_like(g_out)
     g_qkv[...] = jnp.zeros_like(g_qkv)
     g_vec[...] = jnp.zeros_like(g_vec)
@@ -867,6 +957,8 @@
         slot = len(sources) * groups + step
         deep_small.append(send(small_deep.at[group], small_deep.at[group], deep_sems, slot, peer))
         deep_small.append(send(bin_deep.at[group], bin_deep.at[group], deep_sems, groups + slot, peer))
+    rows_out.wait()
+    output[...] = (mixed[...] + got_rows[...].astype(F32)).astype(BF)
     last = []
     here = pl.ds(ours, half)
     for at in range(len(sources)):
@@ -967,7 +1059,7 @@
         partial(start_kernel, dps, groups, images, cap, cap_pad),
         "front",
         0,
-        [V] * 11 + [A] * 2,
+        [V] * 11 + [A] * 3,
         [
             ((dps, rows, 3 * width), BF, V),
             ((dps, rows, width), BF, V),
@@ -987,6 +1079,7 @@
             ((hosted - 1, rows, ff), BF, A),
             ((ff, width), BF, A),
             ((hosted - 1, rows_back, width), BF, A),
+            ((3, tokens, width), BF, A),
         ],
         [
             pltpu.VMEM((tokens, width), BF),
@@ -1002,11 +1095,12 @@
         + [dma((1 + 2 * (dps - 1),))] * 2
         + [dma((2 * hosted,))] * 2
         + [dma((2 * (dps + hosted),))] * 2
-        + [dma((5,))],
+        + [dma((5,))]
+        + [dma((3,))] * 2,
         flops=2 * tokens * width * (8 * width + 4 * keys_pad),
         moved=40 * tokens * width,
-    )(x, w_qkv, w_out, w_router, vectors, b_in, b_back, route_rows, keys[:, None], keys[None, :], bias, w_in, w_back)
-    qkv_all, out_all, router_rows, b_ins, b_backs, vec, slots, q, k, v, p, o, after, acts, *expert_w = made
+    )(x, w_qkv, w_out, w_router, vectors, b_in, b_back, route_rows, keys[:, None], keys[None, :], bias, w_in, w_back, grad)
+    qkv_all, out_all, router_rows, b_ins, b_backs, vec, slots, q, k, v, p, o, after, acts, *expert_w, grads = made
 
     rows_all = 4 * cap_pad
     deep = hosted * cap_pad
@@ -1014,8 +1108,9 @@
         partial(experts_kernel, groups, dps, images, cap_pad),
         "experts",
         2,
-        [A, A, V, V, V, V, V, V] + [A] * 4,
+        [A, A, V, V, V, V, V, V] + [A] * 5,
         [
+            ((tokens, width), F32, V),
             ((tokens, width), F32, V),
             ((tokens, width), BF, V),
             ((experts, width), F32, V),
@@ -1047,18 +1142,18 @@
             pltpu.VMEM((3, hosted, 1, tokens), F32),
             pltpu.VMEM((4, tokens, width), BF),
             pltpu.VMEM((4, tokens, width), BF),
-            pltpu.VMEM((2, tokens, width), BF),
-            pltpu.VMEM((2, tokens, width), BF),
+            pltpu.VMEM((tokens, width), BF),
+            pltpu.VMEM((tokens, width), BF),
             pltpu.VMEM((tokens, LANES), F32),
-            dma((9,)),
-            dma((9,)),
+            dma((6,)),
+            dma((6,)),
             dma((2,)),
             dma((2 * dps,)),
             dma((2 * dps,)),
             dma((9,)),
             dma((9,)),
             dma((2 * dps,)),
-            dma((2,)),
+            dma((3,)),
             dma((2 * hosted * dps,)),
             dma((2 * hosted * dps,)),
             dma((2 * hosted,)),
@@ -1066,8 +1161,8 @@
         flops=14 * hosted * rows_all * width * ff,
         moved=20 * tokens * width + 8 * hosted * width * ff,
         vmem=63,
-    )(acts, grad, after, router_rows, route_rows, slots, b_ins, b_backs, *expert_w)
-    back_rows, output, g_router, g_in, g_back, g_in_other, g_back_other, g_b_in, g_b_back, *_ = made
+    )(acts, grad, after, router_rows, route_rows, slots, b_ins, b_backs, *expert_w, grads)
+    back_rows, mixed, far_rows, g_router, g_in, g_back, g_in_other, g_back_other, g_b_in, g_b_back, *_ = made
 
     wide = 4 * width
     halves_of = rows // 2
@@ -1077,8 +1172,9 @@
         partial(back_kernel, dps, groups, images),
         "back",
         1,
-        [V] * 16 + [A] * 3,
+        [V] * 17 + [A] * 4,
         [
+            ((tokens, width), BF, V),
             ((tokens, width), BF, V),
             ((rows, 3 * width), F32, V),
             ((rows, width), F32, V),
@@ -1124,8 +1220,9 @@
             pltpu.VMEM((dps, 2 * hosted, rows_back), F32),
             pltpu.VMEM((dps - 1, 2 * hosted, rows_back), F32),
             pltpu.VMEM((groups, 2 * hosted, rows_back), F32),
+            pltpu.VMEM((tokens, width), BF),
             dma((6,)), dma((6,)), dma((6 * dps,)), dma((6 * dps,)),
-            dma((6 * groups,)), dma((6 * groups,)), dma((4,)), dma((4,)),
+            dma((6 * groups,)), dma((6 * groups,)), dma((4,)), dma((4,)), dma((1,)), dma((1,)),
             dma((2,)), dma((2 * images,)), dma((2 * images,)), dma((kin_slots * dps,)), dma((kin_slots * dps,)),
             dma((2,)), dma((kin_slots,)), dma((kin_slots,)), dma((2,)), dma((2,)), dma((2,)),
         ],
@@ -1133,10 +1230,10 @@
         moved=60 * tokens * width,
         vmem=62,
     )(
-        grad, back_rows, after, o, vec, out_all, q, k, v, x, qkv_all, g_router, g_in, g_back, g_b_in, g_b_back,
-        p, g_in_other, g_back_other,
+        grad, back_rows, after, o, vec, out_all, q, k, v, x, qkv_all, g_router, g_in, g_back, g_b_in, g_b_back, mixed,
+        p, g_in_other, g_back_other, far_rows,
     )
-    dx, grad_qkv, grad_out, grad_router, grad_vec, grad_b_in, grad_b_back, grad_w_in, grad_w_back, *_ = made
+    dx, output, grad_qkv, grad_out, grad_router, grad_vec, grad_b_in, grad_b_back, grad_w_in, grad_w_back, *_ = made
     return (
         output.reshape(images, half, width),
         dx.reshape(images, half, width),

time: 312 us -> 298 us (0.955)
  Pallas kernels: 296 us -> 280 us
    pallas_call x1, Pallas kernels: 121 us -> 95.9 us  [shards(): comm_call(partial(experts_kernel, groups, dps, images, cap_pad), 'experts...]
    pallas_call x1, Pallas kernels: 73.3 us -> 80.1 us  [shards(): comm_call(partial(start_kernel, dps, groups, images, cap, cap_pad), 'fron...]
    unnamed x31 -> x29, local copies, waits for them, and re-layouts: 10.8 us -> 11.7 us
where the time goes in v6:
time: 298 us; the launch traced here: 297 us
  Pallas kernels  280 us (94%)
  local copies, waits for them, and re-layouts  12.5 us (4%)
  other arithmetic  3.62 us (1%)
    pallas_call x1, Pallas kernels, shards(): comm_call(partial(back_kernel, dps, groups, images), 'back', 1, [V] * 17...  104 us
    pallas_call x1, Pallas kernels, shards(): comm_call(partial(experts_kernel, groups, dps, images, cap_pad), 'experts...  95.9 us
    pallas_call x1, Pallas kernels, shards(): comm_call(partial(start_kernel, dps, groups, images, cap, cap_pad), 'fron...  80.1 us
    unnamed x29, local copies, waits for them, and re-layouts  11.7 us

profile of v6, /device:TPU:0, one launch (start us, length us, event | category | flops | bytes accessed | tf_op | source)
XLA Modules:
  0.0 297.2 jit_solution(16551695224206526384)
XLA Ops:
  0.6 1.3 bitcast_add_fusion.key_row
  1.9 0.7 multiply_bitcast_fusion
  2.6 0.7 compare_select_fusion
  3.3 0.1 slice_select_fusion.1
  3.4 0.1 pad_maximum_fusion
  3.5 0.6 broadcast_in_dim.15.bias
  4.1 1.4 copy.25.w_router
  5.5 0.2 copy.24
  5.7 0.8 iota_add_fusion.key_col
  6.5 80.1 %front.1 = (bf16[4,128,1536]{2,1,0:T(8,128)(2,1)}, bf16[4,128,512]{2,1,0:T(8,128)(2,1)}, bf16[8,512]{1,0:T(8,128)(2,1)}, bf16[2,4,2,512]{3,2,1,0:T(2,128)(2,1)},...) custom-call(bf16[888,512]{1,0:T(8,128)(2,1)} %bitcast.17, ...), custom_call_target="tpu_custom_call" | custom-call | flops 5935988736 | bytes 18186240 | tf_op jit(solution)/shard_map/front/pallas_call | solution.py:1058
  86.6 95.9 %experts.1 = (f32[888,512]{1,0:T(8,128)}, f32[888,512]{1,0:T(8,128)}, bf16[888,512]{1,0:T(8,128)(2,1)}, f32[8,512]{1,0:T(8,128)}, f32[128,2048]{1,0:T(8,128)}, /...) custom-call(bf16[888,512]{1,0:T(8,128)(2,1)} %get-tuple-element.49.a, ...), custom_call_target="tpu_custom_call" | custom-call | flops 39460012032 | bytes 25870336 | tf_op jit(solution)/shard_map/experts/pallas_call | solution.py:1107
  182.5 104.4 %back.1 = (bf16[888,512]{1,0:T(8,128)(2,1)}, bf16[888,512]{1,0:T(8,128)(2,1)}, f32[128,1536]{1,0:T(8,128)}, f32[128,512]{1,0:T(8,128)}, f32[8,128]{1,0:T(8,128)}...) custom-call(bf16[888,512]{1,0:T(8,128)(2,1)} %bitcast.16, ...), custom_call_target="tpu_custom_call" | custom-call | flops 8147435520 | bytes 27279360 | tf_op jit(solution)/shard_map/back/pallas_call | solution.py:1171
  286.9 0.0 copy-start.2
  286.9 0.0 copy-start.7
  286.9 0.0 copy-start.3
  286.9 2.3 copy.36
  289.2 0.0 copy-done.2
  289.2 0.0 copy-start.4
  289.2 0.0 copy-start.6
  289.2 0.0 copy-start.1
  289.2 0.9 copy.37
  290.1 0.0 copy-done.7
  290.1 0.6 copy.38
  290.7 0.0 copy-done.3
  290.7 0.9 copy.39
  291.6 0.0 copy-done.4
  291.6 0.7 copy.40
  292.3 0.0 copy-done.6
  292.3 0.6 copy.41
  292.9 0.0 copy-done.1
  292.9 0.0 copy-start.5
  292.9 0.0 copy-start
  292.9 1.3 copy.42
  294.2 0.0 copy-done.5
  294.2 0.6 copy.43
  294.8 0.4 copy-done
  295.3 0.0 copy-start.8
  295.3 1.3 copy.44
  296.6 0.0 copy-done.8
  296.6 0.6 copy.45
  (1 shorter events, 0.0 us)
Async XLA Ops:
  286.9 2.3 copy-start.2
  286.9 3.2 %copy-start.7 = (f32[7,128]{1,0:T(8,128)S(1)}, f32[7,128]{1,0:T(8,128)}, u32[]{:S(2)}) copy-start(f32[7,128]{1,0:T(8,128)} %get-tuple-element.102) | copy-start | bytes 10756
  286.9 3.8 %copy-start.3 = (f32[128,1536]{1,0:T(8,128)S(1)}, f32[128,1536]{1,0:T(8,128)}, u32[]{:S(2)}) copy-start(f32[128,1536]{1,0:T(8,128)} %get-tuple-element.103) | copy-start | bytes 2359300
  289.2 2.4 copy-start.4
  289.2 3.1 %copy-start.6 = (f32[8,128]{1,0:T(8,128)S(1)}, f32[8,128]{1,0:T(8,128)}, u32[]{:S(2)}) copy-start(f32[8,128]{1,0:T(8,128)} %get-tuple-element.83) | copy-start | bytes 12292
  289.2 3.7 %copy-start.1 = (f32[2,128,2048]{2,1,0:T(8,128)S(1)}, f32[2,128,2048]{2,1,0:T(8,128)}, u32[]{:S(2)}) copy-start(f32[2,128,2048]{2,1,0:T(8,128)} %get-tuple-element.106) | copy-start | bytes 6291460
  292.9 1.3 copy-start.5
  292.9 2.4 copy-start
  295.3 1.3 copy-start.8

commit v7 on v6

--- a/solution.py
+++ b/solution.py
@@ -65,7 +65,7 @@
     w_in_far, w_back_far, rest = rest[10], rest[11], rest[12:]
     tok, info, made_rows, w_in_v, w_back_v, rows_v, hidden, grad_pre, delta, slope = rest[:10]
     in_send, in_recv, back_send, back_recv, dots, dots_got, to_near, from_near, to_far, from_far = rest[10:20]
-    places, x_s, x_r, w_sem, r_s, r_r, p_s, p_r, store_sem, load_sem, w_s, w_r, w_own = rest[20:]
+    places, x_s, x_r, w_sem, r_s, r_r, p_s, p_r, store_sem, load_sem, w_s, w_r = rest[20:]
     dp, group, core = lax.axis_index("dp"), lax.axis_index("expert"), lax.axis_index("context")
     tokens, width = mixed.shape
     ff = w_in_v.shape[1]
@@ -97,8 +97,6 @@
         kin, far = ((kin_in, w_in_far), (kin_back, w_back_far))[which]
         size = kin.shape[1]
         part = far.at[at, pl.ds(pl.multiple_of(dp * size, size), size)]
-        if step == 0:
-            return pltpu.make_async_copy(kin.at[at], part, w_own.at[2 * at + which])
         target = (square(dp)[step - 1], group, core) if dps == 4 else along(step)
         return remote(kin.at[at], part, (w_s, w_r), (2 * at + which) * dps + step - 1, target)
 
@@ -113,16 +111,23 @@
 
     def load(which, wait):
         for at in range(hosted):
-            copies = (
-                pltpu.make_async_copy(w_in_far.at[at - 1] if at else w_in, w_in_v, w_sem.at[0]),
-                pltpu.make_async_copy(w_back_far.at[at - 1] if at else w_back, w_back_v, w_sem.at[1]),
-            )
+            copies = []
+            for part, (whole, kin, far, held) in enumerate(
+                ((w_in, kin_in, w_in_far, w_in_v), (w_back, kin_back, w_back_far, w_back_v))
+            ):
+                if at == 0:
+                    copies.append(pltpu.make_async_copy(whole, held, w_sem.at[part * dps]))
+                    continue
+                size = kin.shape[1]
+                for step in range(dps):
+                    here = pl.ds(pl.multiple_of(lax.rem(dp + step, dps) * size, size), size)
+                    src = far.at[at - 1, here] if step else kin.at[at - 1]
+                    copies.append(pltpu.make_async_copy(src, held.at[here], w_sem.at[part * dps + step]))
 
             @pl.when(which == at)
             def _():
                 if at and not wait:
                     for part in range(2):
-                        gather(at - 1, part, 0).wait()
                         for step in range(1, direct):
                             if dps == 4:
                                 gather(at - 1, part, step).wait_send()
@@ -162,7 +167,7 @@
         moves[1, hop].start()
     for at in range(hosted - 1):
         for part in range(2):
-            for step in range(direct):
+            for step in range(1, direct):
                 gather(at, part, step).start()
     logits = nt(router[...], tok[0, 0])
     logits = jnp.exp(logits - jnp.max(logits, axis=0, keepdims=True))
@@ -739,7 +744,7 @@
     dx_ref, output, o_qkv, o_out, o_router, o_vec, o_in, o_back, w_in_sum, w_back_sum, in_recv, back_recv,
     sum_in, sum_back, p_two, dh_ref, dq_ref, dk_ref, dv_ref, dk_got, dv_got, g_out, g_qkv, g_vec,
     in_stage, back_stage, in_to, back_to, in_from, back_from,
-    near_out, near_in, far_out, far_in, deep_in, total,
+    near_out, near_in, far_out, far_in, deep_in, deep_out, deep_all, total,
     small_near, small_far, small_got, small_deep, bin_near, bin_far, bin_got, bin_deep,
     got_rows, near_s, near_r, far_s, far_r, deep_s, deep_r, last_s, last_r,
     rows_s, rows_r, p_sem, d_s, d_r, e_s, e_r, stage_sem, kin_s, kin_r, home_s, home_r, home_sem,
@@ -775,6 +780,51 @@
         slot = ((which * 2 + part) * (hosted - 1) + at) * dps + step
         return remote(src, dst, (e_s, e_r), slot, peers[step - 1])
 
+    def piece_out(which, part, at, kind):
+        other, recv, stage = sets[which][:3]
+        size = recv.shape[2]
+        piece = size // 2
+        side, over = square(dp)
+        corner = lax.rem(side + 2, 4)
+        share = (corner, side, over)[kind]
+        via = (over if part == 0 else side, side, over)[kind]
+        place = (2, 0, 1)[kind]
+        if kind == part + 1:
+            src = stage.at[2 + part]
+        else:
+            src = other.at[at, pl.ds(pl.multiple_of(share * size, size) + part * piece, piece)]
+        dst = recv.at[at, place, pl.ds(part * piece, piece)]
+        slot = ((which * 2 + part) * (hosted - 1) + at) * dps + kind
+        return remote(src, dst, (e_s, e_r), slot, (via, group, core))
+
+    def at_once(which):
+        for at in range(hosted - 1):
+            for part, kind in ((0, 0), (1, 0), (1, 1), (0, 2)):
+                piece_out(which, part, at, kind).start()
+
+    def relayed(which):
+        other, recv, stage = sets[which][:3]
+        size = recv.shape[2]
+        piece = size // 2
+        for at in range(hosted - 1):
+            for part in range(2):
+                here = pl.ds(part * piece, piece)
+                share = square(dp)[part]
+                piece_out(which, part, at, 0).wait_recv()
+                own = other.at[at, pl.ds(pl.multiple_of(share * size, size) + part * piece, piece)]
+                copies = (
+                    pltpu.make_async_copy(recv.at[at, 2, here], stage.at[0], stage_sem.at[0]),
+                    pltpu.make_async_copy(own, stage.at[1], stage_sem.at[1]),
+                )
+                for copy in copies:
+                    copy.start()
+                for copy in copies:
+                    copy.wait()
+                if at:
+                    piece_out(which, part, at - 1, part + 1).wait_send()
+                stage[2 + part] = (stage[0].astype(F32) + stage[1].astype(F32)).astype(BF)
+                piece_out(which, part, at, part + 1).start()
+
     def home_out(which, part, at):
         to, back = sets[which][3:5]
         piece = to.shape[1] // 2
@@ -802,21 +852,29 @@
         size = recv.shape[2]
         piece = size // 2
         here = pl.ds(part * piece, piece)
+        count = 2 if dps == 4 else dps - 1
+        if dps == 4 and part == 0:
+            for side in range(2):
+                piece_out(which, side, hosted - 2, side + 1).wait_send()
         for at in range(hosted - 1):
-            for step in range(1, dps):
-                sum_out(which, part, at, step).wait_recv()
+            if dps == 4:
+                for kind in (1, 2):
+                    piece_out(which, part, at, kind).wait_recv()
+            else:
+                for step in range(1, dps):
+                    sum_out(which, part, at, step).wait_recv()
             own = other.at[at, pl.ds(pl.multiple_of(dp * size, size) + part * piece, piece)]
             copies = (
-                pltpu.make_async_copy(recv.at[at, :, here], stage.at[pl.ds(0, dps - 1)], stage_sem.at[0]),
-                pltpu.make_async_copy(own, stage.at[dps - 1], stage_sem.at[1]),
+                pltpu.make_async_copy(recv.at[at, pl.ds(0, count), here], stage.at[pl.ds(0, count)], stage_sem.at[0]),
+                pltpu.make_async_copy(own, stage.at[count], stage_sem.at[1]),
             )
             for copy in copies:
                 copy.start()
             for copy in copies:
                 copy.wait()
             value = stage[0].astype(F32)
-            for step in range(1, dps):
-                value = value + stage[step].astype(F32)
+            for step in range(count):
+                value = value + stage[step + 1].astype(F32)
             to[at, here, :] = value.astype(BF)
             home_out(which, part, at).start()
 
@@ -831,11 +889,14 @@
 
     load(0).start()
     greet(peers + others + [near])
-    for which in range(2):
-        for part in range(2):
-            for at in range(hosted - 1):
-                for step in range(1, dps):
-                    sum_out(which, part, at, step).start()
+    if dps == 4:
+        at_once(0)
+    else:
+        for which in range(2):
+            for part in range(2):
+                for at in range(hosted - 1):
+                    for step in range(1, dps):
+                        sum_out(which, part, at, step).start()
     mate = group + 1 - 2 * lax.rem(group, 2)
     rows_out = send(far_rows, got_rows, (rows_s, rows_r), 0, (dp, mate, core))
     g_out[...] = jnp.zeros_like(g_out)
@@ -856,14 +917,23 @@
         swap(image, 0).start()
         swap(image, 1).start()
 
+        if dps == 4:
+
+            @pl.when(image == 0)
+            def _():
+                relayed(0)
+                at_once(1)
+
         @pl.when(image == images - 2)
         def _():
             send_home(0, 0)
+            send_home(0, 1)
 
         return 0
 
     lax.fori_loop(0, images, back_step, 0)
-    send_home(0, 1)
+    if dps == 4:
+        relayed(1)
 
     near_sems, far_sems, deep_sems, last_sems = (near_s, near_r), (far_s, far_r), (deep_s, deep_r), (last_s, last_r)
     sources = [(g_out, 0)] + [(g_qkv, at) for at in range(0, g_qkv.shape[1], width)]
@@ -908,6 +978,8 @@
         send(small_near.at[0], small_near.at[1], near_sems, 0, near),
         send(bin_near.at[0], bin_near.at[1], near_sems, 1, near),
     ]
+    send_home(1, 0)
+    send_home(1, 1)
     second = []
     for at, (ref, lane) in enumerate(sources):
         cols = cols_of(at)
@@ -928,8 +1000,9 @@
         target = lax.rem(dp + step + 1, dps)
         smalls.append(send(small_far.at[target], small_got.at[step], far_sems, step, peer))
         smalls.append(send(bin_far.at[target], bin_got.at[step], far_sems, dps + step, peer))
-    send_home(1, 0)
     third = []
+    few = half // groups
+    split = few % 16 == 0
     for at, (ref, lane) in enumerate(sources):
         cols = cols_of(at)
         mine = ref[pl.ds(pl.multiple_of(dp * rows, rows) + ours, half), lane : lane + width]
@@ -937,12 +1010,18 @@
         for step in range(dps - 1):
             second[at * (dps - 1) + step].wait()
             mine = mine + far_in[step, :, cols].astype(F32)
-        deep_in[group, :, cols] = mine.astype(BF)
-        for step, peer in enumerate(others):
-            third.append(
-                send(deep_in.at[group, :, cols], deep_in.at[group, :, cols], deep_sems, at * groups + step, peer)
-            )
-    send_home(1, 1)
+        if split:
+            deep_out[:, cols] = mine.astype(BF)
+            deep_in[group, :few, cols] = deep_out[pl.ds(pl.multiple_of(group * few, few), few), cols]
+            for step, peer in enumerate(others):
+                to = pl.multiple_of(lax.rem(group + step + 1, groups) * few, few)
+                src = deep_out.at[pl.ds(to, few), cols]
+                third.append(send(src, deep_in.at[group, pl.ds(0, few), cols], deep_sems, at * groups + step, peer))
+        else:
+            deep_in[group, :, cols] = mine.astype(BF)
+            for step, peer in enumerate(others):
+                part = deep_in.at[group, :, cols]
+                third.append(send(part, part, deep_sems, at * groups + step, peer))
     for copy in smalls:
         copy.wait()
     lone = small_far[dp]
@@ -957,17 +1036,33 @@
         slot = len(sources) * groups + step
         deep_small.append(send(small_deep.at[group], small_deep.at[group], deep_sems, slot, peer))
         deep_small.append(send(bin_deep.at[group], bin_deep.at[group], deep_sems, groups + slot, peer))
-    rows_out.wait()
-    output[...] = (mixed[...] + got_rows[...].astype(F32)).astype(BF)
-    last = []
+    last, fourth = [], []
     here = pl.ds(ours, half)
-    for at in range(len(sources)):
+    for at in range(len(sources) if split else 0):
         cols = cols_of(at)
         for step in range(groups - 1):
             third[at * (groups - 1) + step].wait()
-        done = deep_in[0, :, cols].astype(F32)
+        done = deep_in[0, :few, cols].astype(F32)
         for source in range(1, groups):
-            done = done + deep_in[source, :, cols].astype(F32)
+            done = done + deep_in[source, :few, cols].astype(F32)
+        part = deep_all.at[pl.ds(pl.multiple_of(group * few, few), few), cols]
+        part[...] = done.astype(BF)
+        for step, peer in enumerate(others):
+            fourth.append(send(part, part, deep_sems, (6 + at) * groups + step, peer))
+    rows_out.wait()
+    output[...] = (mixed[...] + got_rows[...].astype(F32)).astype(BF)
+    for at in range(len(sources)):
+        cols = cols_of(at)
+        if split:
+            for step in range(groups - 1):
+                fourth[at * (groups - 1) + step].wait()
+            done = deep_all[:, cols].astype(F32)
+        else:
+            for step in range(groups - 1):
+                third[at * (groups - 1) + step].wait()
+            done = deep_in[0, :, cols].astype(F32)
+            for source in range(1, groups):
+                done = done + deep_in[source, :, cols].astype(F32)
         total[here, cols] = done
         last.append(send(total.at[here, cols], total.at[here, cols], last_sems, at, near))
     for copy in deep_small:
@@ -1013,13 +1108,43 @@
         for part in range(2):
             for at in range(hosted - 1):
                 home_out(which, part, at).wait_send()
-                for step in range(1, dps):
-                    sum_out(which, part, at, step).wait_send()
+                if dps == 4:
+                    for kind in (0, 2 - part):
+                        piece_out(which, part, at, kind).wait_send()
+                else:
+                    for step in range(1, dps):
+                        sum_out(which, part, at, step).wait_send()
     for image in range(images):
         for which in range(2):
             swap(image, which).wait_send()
     for copy in stores:
         copy.wait()
+
+
+def hand_over_kernel(count, *refs):
+    given, kept, held, (loads, stores) = refs[:count], refs[count : 2 * count], refs[2 * count : 3 * count], refs[3 * count :]
+    ins = [pltpu.make_async_copy(given[at], held[at], loads.at[at]) for at in range(count)]
+    outs = [pltpu.make_async_copy(held[at], kept[at], stores.at[at]) for at in range(count)]
+    for copy in ins:
+        copy.start()
+    for at in range(count):
+        ins[at].wait()
+        outs[at].start()
+    for copy in outs:
+        copy.wait()
+
+
+def hand_over(arrays):
+    return pl.pallas_call(
+        partial(hand_over_kernel, len(arrays)),
+        name="hand_over",
+        in_specs=[pl.BlockSpec(memory_space=pl.ANY)] * len(arrays),
+        out_specs=[pl.BlockSpec(memory_space=pl.ANY)] * len(arrays),
+        out_shape=[jax.ShapeDtypeStruct(array.shape, array.dtype) for array in arrays],
+        scratch_shapes=[pltpu.VMEM(array.shape, array.dtype) for array in arrays]
+        + [pltpu.SemaphoreType.DMA((len(arrays),))] * 2,
+        compiler_params=pltpu.CompilerParams(vmem_limit_bytes=63 * MIB),
+    )(*arrays)
 
 
 def shards(
@@ -1147,7 +1272,7 @@
             pltpu.VMEM((tokens, LANES), F32),
             dma((6,)),
             dma((6,)),
-            dma((2,)),
+            dma((2 * dps,)),
             dma((2 * dps,)),
             dma((2 * dps,)),
             dma((9,)),
@@ -1156,7 +1281,6 @@
             dma((3,)),
             dma((2 * hosted * dps,)),
             dma((2 * hosted * dps,)),
-            dma((2 * hosted,)),
         ],
         flops=14 * hosted * rows_all * width * ff,
         moved=20 * tokens * width + 8 * hosted * width * ff,
@@ -1211,6 +1335,8 @@
             pltpu.VMEM((dps - 1, halves_of, wide), BF),
             pltpu.VMEM((dps - 1, halves_of, wide), BF),
             pltpu.VMEM((groups, halves_of, wide), BF),
+            pltpu.VMEM((halves_of, wide), BF),
+            pltpu.VMEM((halves_of, wide), BF),
             pltpu.VMEM((rows, wide), F32),
             pltpu.VMEM((2, dps, small, rows), F32),
             pltpu.VMEM((dps, small, rows), F32),
@@ -1222,7 +1348,7 @@
             pltpu.VMEM((groups, 2 * hosted, rows_back), F32),
             pltpu.VMEM((tokens, width), BF),
             dma((6,)), dma((6,)), dma((6 * dps,)), dma((6 * dps,)),
-            dma((6 * groups,)), dma((6 * groups,)), dma((4,)), dma((4,)), dma((1,)), dma((1,)),
+            dma((10 * groups,)), dma((10 * groups,)), dma((4,)), dma((4,)), dma((1,)), dma((1,)),
             dma((2,)), dma((2 * images,)), dma((2 * images,)), dma((kin_slots * dps,)), dma((kin_slots * dps,)),
             dma((2,)), dma((kin_slots,)), dma((kin_slots,)), dma((2,)), dma((2,)), dma((2,)),
         ],
@@ -1234,6 +1360,8 @@
         p, g_in_other, g_back_other, far_rows,
     )
     dx, output, grad_qkv, grad_out, grad_router, grad_vec, grad_b_in, grad_b_back, grad_w_in, grad_w_back, *_ = made
+    passed = hand_over([output, dx, grad_vec, grad_qkv, grad_out, grad_w_in, grad_b_in, grad_w_back, grad_b_back])
+    output, dx, grad_vec, grad_qkv, grad_out, grad_w_in, grad_b_in, grad_w_back, grad_b_back = passed
     return (
         output.reshape(images, half, width),
         dx.reshape(images, half, width),

time: 298 us -> 287 us (0.963)
  local copies, waits for them, and re-layouts: 12.5 us -> 2.82 us
    unnamed x29 -> x4, local copies, waits for them, and re-layouts: 11.7 us -> 2.01 us
    pallas_call x1, Pallas kernels: 104 us -> 97.6 us  [shards(): comm_call(partial(back_kernel, dps, groups, images), 'back', 1, [V] * 17...]
    pallas_call x0 -> x1, Pallas kernels: none -> 5.64 us  [hand_over(): pl.pallas_call(partial(hand_over_kernel, len(arrays)), name='hand_over',...]
where the time goes in v7:
time: 287 us; the launch traced here: 286 us
  Pallas kernels  279 us (97%)
  other arithmetic  3.62 us (1%)
    pallas_call x1, Pallas kernels, shards(): comm_call(partial(back_kernel, dps, groups, images), 'back', 1, [V] * 17...  97.6 us
    pallas_call x1, Pallas kernels, shards(): comm_call(partial(experts_kernel, groups, dps, images, cap_pad), 'experts...  95.9 us
    pallas_call x1, Pallas kernels, shards(): comm_call(partial(start_kernel, dps, groups, images, cap, cap_pad), 'fron...  80.1 us

profile of v7, /device:TPU:0, one launch (start us, length us, event | category | flops | bytes accessed | tf_op | source)
XLA Modules:
  0.0 286.4 jit_solution(16289661975053758436)
XLA Ops:
  0.6 1.3 bitcast_add_fusion.key_row
  1.9 0.7 multiply_bitcast_fusion
  2.6 0.7 compare_select_fusion
  3.3 0.1 slice_select_fusion.1
  3.4 0.1 pad_maximum_fusion
  3.5 0.6 broadcast_in_dim.15.bias
  4.1 1.4 copy.25.w_router
  5.5 0.2 copy.24
  5.7 0.8 iota_add_fusion.key_col
  6.5 80.1 %front.1 = (bf16[4,128,1536]{2,1,0:T(8,128)(2,1)}, bf16[4,128,512]{2,1,0:T(8,128)(2,1)}, bf16[8,512]{1,0:T(8,128)(2,1)}, bf16[2,4,2,512]{3,2,1,0:T(2,128)(2,1)},...) custom-call(bf16[888,512]{1,0:T(8,128)(2,1)} %bitcast.15, ...), custom_call_target="tpu_custom_call" | custom-call | flops 5935988736 | bytes 18186240 | tf_op jit(solution)/shard_map/front/pallas_call | solution.py:1183
  86.6 95.9 %experts.1 = (f32[888,512]{1,0:T(8,128)}, f32[888,512]{1,0:T(8,128)}, bf16[888,512]{1,0:T(8,128)(2,1)}, f32[8,512]{1,0:T(8,128)}, f32[128,2048]{1,0:T(8,128)}, /...) custom-call(bf16[888,512]{1,0:T(8,128)(2,1)} %get-tuple-element.58.a, ...), custom_call_target="tpu_custom_call" | custom-call | flops 39460012032 | bytes 25870336 | tf_op jit(solution)/shard_map/experts/pallas_call | solution.py:1232
  182.5 97.6 %back.1 = (bf16[888,512]{1,0:T(8,128)(2,1)}, bf16[888,512]{1,0:T(8,128)(2,1)}, f32[128,1536]{1,0:T(8,128)}, f32[128,512]{1,0:T(8,128)}, f32[8,128]{1,0:T(8,128)}...) custom-call(bf16[888,512]{1,0:T(8,128)(2,1)} %bitcast.14, ...), custom_call_target="tpu_custom_call" | custom-call | flops 8147435520 | bytes 27279360 | tf_op jit(solution)/shard_map/back/pallas_call | solution.py:1295
  280.1 0.0 copy-start
  280.1 5.6 %hand_over.1 = (bf16[888,512]{1,0:T(8,128)(2,1)}, bf16[888,512]{1,0:T(8,128)(2,1)}, f32[7,128]{1,0:T(8,128)}, f32[128,1536]{1,0:T(8,128)}, f32[128,512]{1,0:T(8,...) custom-call(bf16[888,512]{1,0:T(8,128)(2,1)} %get-tuple-element.87.refs_0_, ...), custom_call_target="tpu_custom_call" | custom-call | tf_op jit(solution)/shard_map/hand_over/pallas_call | solution.py:1138
  285.8 0.0 copy-done
  285.8 0.6 copy.27
  (1 shorter events, 0.0 us)
Async XLA Ops:
  280.1 5.7 %copy-start = (f32[8,128]{1,0:T(8,128)S(1)}, f32[8,128]{1,0:T(8,128)}, u32[]{:S(2)}) copy-start(f32[8,128]{1,0:T(8,128)} %get-tuple-element.101) | copy-start | bytes 12292

commit v8 on v7

--- a/solution.py
+++ b/solution.py
@@ -589,7 +589,7 @@
 
 
 def start_kernel(
-    dps, groups, images, cap, cap_pad, x, w_qkv, w_out, w_router, vectors, b_in, b_back, routes, key_col, key_row, bias,
+    dps, groups, images, cap, cap_pad, x, w_qkv, w_out, w_router, vectors, b_in, b_back, routes, priority, bias,
     w_in, w_back, grad,
     qkv_all, out_all, router_rows, b_in_all, back_all, vec, slots,
     q_ref, k_ref, v_ref, p_ref, o_ref, h_ref, a_ref, in_all, in_kin, back_w_all, back_kin, grads,
@@ -624,8 +624,7 @@
     for step, peer in enumerate(peers):
         copies.append(send(qkv_all.at[dp, own], qkv_all.at[dp, own], far, step * 6, peer))
     out_all[dp] = w_out[...].astype(BF)
-    spare = router_all.shape[2] - w_router.shape[1]
-    router_all[dp] = jnp.concatenate([w_router[...], jnp.zeros((rows, spare), F32)], axis=1).astype(BF)
+    router_all[dp] = w_router[...].astype(BF)
     vec_all[dp] = jnp.concatenate([vectors[...], jnp.zeros((1, rows), F32)], axis=0).astype(BF)
     b_in_all[0, dp] = b_in[...].astype(BF)
     back_all[0, dp] = b_back[...].astype(BF)
@@ -675,9 +674,16 @@
             copy.start()
 
     tokens = routes.shape[1]
-    experts = w_router.shape[1]
+    experts = w_router.shape[0]
     ids = iota((experts, tokens), 0)
-    before = jnp.where(key_col[...] < key_row[...], 1.0, 0.0).astype(BF)
+    order = priority[...].astype(F32)
+    high = jnp.floor(order * (1.0 / 256.0))
+    parts = jnp.concatenate([high, order - 256.0 * high, jnp.zeros((6, tokens), F32)], axis=0).astype(BF)
+    place = iota((8, LANES), 0)
+    weight = jnp.where(place == 0, 256.0, jnp.where(place == 1, 1.0, 0.0)).astype(BF)
+    column = tn(parts, weight)[:, 0:1]
+    tied = jnp.logical_and(column == order, iota((tokens, 1), 0) < iota((1, tokens), 1))
+    before = jnp.where(jnp.logical_or(column < order, tied), 1.0, 0.0).astype(BF)
     first = jnp.where(routes[0:1, :] == ids, 1.0, 0.0)
     second = jnp.where(routes[1:2, :] == ids, 1.0, 0.0)
     count = jnp.sum(first, axis=1, keepdims=True)
@@ -700,8 +706,7 @@
     for copy in smalls:
         copy.wait()
     vec[...] = jnp.concatenate([vec_all[at].astype(F32) for at in range(dps)], axis=1)
-    turned = [router_all[at].astype(F32).T[: w_router.shape[1]] for at in range(dps)]
-    router_rows[...] = jnp.concatenate(turned, axis=1).astype(BF)
+    router_rows[...] = jnp.concatenate([router_all[at].astype(F32) for at in range(dps)], axis=1).astype(BF)
     for copy in waits:
         copy.wait()
 
@@ -1170,7 +1175,6 @@
     x = inputs.reshape(tokens, width)
     grad = cotangent.reshape(tokens, width)
     route_rows = routes.reshape(tokens, 2).T
-    keys = priority.reshape(tokens) * tokens + jnp.arange(tokens, dtype=I32)
 
     mask = jnp.where(key_mask > 0, 0.0, -1e30).astype(F32)
     first, second = mask[:, :half], mask[:, half:]
@@ -1184,7 +1188,7 @@
         partial(start_kernel, dps, groups, images, cap, cap_pad),
         "front",
         0,
-        [V] * 11 + [A] * 3,
+        [V] * 10 + [A] * 3,
         [
             ((dps, rows, 3 * width), BF, V),
             ((dps, rows, width), BF, V),
@@ -1208,7 +1212,7 @@
         ],
         [
             pltpu.VMEM((tokens, width), BF),
-            pltpu.VMEM((dps, rows, LANES), BF),
+            pltpu.VMEM((dps, experts, rows), BF),
             pltpu.VMEM((dps, 8, rows), BF),
             pltpu.VMEM((images, HEADS, half, keys_pad), BF),
             pltpu.VMEM((rows, ff), F32),
@@ -1224,7 +1228,7 @@
         + [dma((3,))] * 2,
         flops=2 * tokens * width * (8 * width + 4 * keys_pad),
         moved=40 * tokens * width,
-    )(x, w_qkv, w_out, w_router, vectors, b_in, b_back, route_rows, keys[:, None], keys[None, :], bias, w_in, w_back, grad)
+    )(x, w_qkv, w_out, w_router.T, vectors, b_in, b_back, route_rows, priority.reshape(1, tokens), bias, w_in, w_back, grad)
     qkv_all, out_all, router_rows, b_ins, b_backs, vec, slots, q, k, v, p, o, after, acts, *expert_w, grads = made
 
     rows_all = 4 * cap_pad
@@ -1360,8 +1364,8 @@
         p, g_in_other, g_back_other, far_rows,
     )
     dx, output, grad_qkv, grad_out, grad_router, grad_vec, grad_b_in, grad_b_back, grad_w_in, grad_w_back, *_ = made
-    passed = hand_over([output, dx, grad_vec, grad_qkv, grad_out, grad_w_in, grad_b_in, grad_w_back, grad_b_back])
-    output, dx, grad_vec, grad_qkv, grad_out, grad_w_in, grad_b_in, grad_w_back, grad_b_back = passed
+    passed = hand_over([output, dx, grad_router, grad_vec, grad_qkv, grad_out, grad_w_in, grad_b_in, grad_w_back, grad_b_back])
+    output, dx, grad_router, grad_vec, grad_qkv, grad_out, grad_w_in, grad_b_in, grad_w_back, grad_b_back = passed
     return (
         output.reshape(images, half, width),
         dx.reshape(images, half, width),

time: 287 us -> 282 us (0.983)
  no operation moved by 1% of the time
where the time goes in v8:
time: 282 us; the launch traced here: 281 us
  Pallas kernels  279 us (99%)
    pallas_call x1, Pallas kernels, shards(): comm_call(partial(back_kernel, dps, groups, images), 'back', 1, [V] * 17...  97.6 us
    pallas_call x1, Pallas kernels, shards(): comm_call(partial(experts_kernel, groups, dps, images, cap_pad), 'experts...  95.9 us
    pallas_call x1, Pallas kernels, shards(): comm_call(partial(start_kernel, dps, groups, images, cap, cap_pad), 'fron...  79.9 us
    pallas_call x1, Pallas kernels, hand_over(): pl.pallas_call(partial(hand_over_kernel, len(arrays)), name='hand_over',...  5.66 us

profile of v8, /device:TPU:0, one launch (start us, length us, event | category | flops | bytes accessed | tf_op | source)
XLA Modules:
  0.0 281.4 jit_solution(16227966074510842635)
XLA Ops:
  0.6 0.7 compare_select_fusion
  1.4 0.1 slice_select_fusion.1
  1.4 0.1 pad_maximum_fusion
  1.5 0.6 broadcast_in_dim.13.bias
  2.1 79.9 %front.1 = (bf16[4,128,1536]{2,1,0:T(8,128)(2,1)}, bf16[4,128,512]{2,1,0:T(8,128)(2,1)}, bf16[8,512]{1,0:T(8,128)(2,1)}, bf16[2,4,2,512]{3,2,1,0:T(2,128)(2,1)},...) custom-call(bf16[888,512]{1,0:T(8,128)(2,1)} %bitcast.13, ...), custom_call_target="tpu_custom_call" | custom-call | flops 5935988736 | bytes 18186240 | tf_op jit(solution)/shard_map/front/pallas_call | solution.py:1187
  82.0 95.9 %experts.1 = (f32[888,512]{1,0:T(8,128)}, f32[888,512]{1,0:T(8,128)}, bf16[888,512]{1,0:T(8,128)(2,1)}, f32[8,512]{1,0:T(8,128)}, f32[128,2048]{1,0:T(8,128)}, /...) custom-call(bf16[888,512]{1,0:T(8,128)(2,1)} %get-tuple-element.59.a, ...), custom_call_target="tpu_custom_call" | custom-call | flops 39460012032 | bytes 25870336 | tf_op jit(solution)/shard_map/experts/pallas_call | solution.py:1236
  177.9 97.6 %back.1 = (bf16[888,512]{1,0:T(8,128)(2,1)}, bf16[888,512]{1,0:T(8,128)(2,1)}, f32[128,1536]{1,0:T(8,128)}, f32[128,512]{1,0:T(8,128)}, f32[8,128]{1,0:T(8,128)}...) custom-call(bf16[888,512]{1,0:T(8,128)(2,1)} %bitcast.12, ...), custom_call_target="tpu_custom_call" | custom-call | flops 8147435520 | bytes 27279360 | tf_op jit(solution)/shard_map/back/pallas_call | solution.py:1299
  275.5 5.7 %hand_over.1 = (bf16[888,512]{1,0:T(8,128)(2,1)}, bf16[888,512]{1,0:T(8,128)(2,1)}, f32[8,128]{1,0:T(8,128)}, f32[7,128]{1,0:T(8,128)}, f32[128,1536]{1,0:T(8,12...) custom-call(bf16[888,512]{1,0:T(8,128)(2,1)} %get-tuple-element.88.r, ...), custom_call_target="tpu_custom_call" | custom-call | tf_op jit(solution)/shard_map/hand_over/pallas_call | solution.py:1143
  (1 shorter events, 0.0 us)

commit v9 on v8

--- a/solution.py
+++ b/solution.py
@@ -589,11 +589,11 @@
 
 
 def start_kernel(
-    dps, groups, images, cap, cap_pad, x, w_qkv, w_out, w_router, vectors, b_in, b_back, routes, priority, bias,
+    dps, groups, images, cap, cap_pad, x, w_qkv, w_out, w_router, vectors, b_in, b_back, routes, priority, key_mask,
     w_in, w_back, grad,
     qkv_all, out_all, router_rows, b_in_all, back_all, vec, slots,
     q_ref, k_ref, v_ref, p_ref, o_ref, h_ref, a_ref, in_all, in_kin, back_w_all, back_kin, grads,
-    x_other, router_all, vec_all, p_all, w_in_f, w_back_f, w_in_v, w_back_v,
+    x_other, bias, router_all, vec_all, p_all, w_in_f, w_back_f, w_in_v, w_back_v,
     far_send, far_recv, near_send, near_recv, deep_send, deep_recv, w_s, w_r, local, rows_s, rows_r,
 ):
     dp, group, core = lax.axis_index("dp"), lax.axis_index("expert"), lax.axis_index("context")
@@ -711,6 +711,15 @@
         copy.wait()
 
     half = tokens // images
+    mask = jnp.where(key_mask[...] > 0, 0.0, -1e30)
+    first, second = mask[:, :half], mask[:, half:]
+    gap = bias.shape[2] // 2 - half
+    for part in range(2):
+        bias_part = jnp.where(core == part, first, second)
+        for image in range(images):
+            bias[image, :, part * (half + gap) : part * (half + gap) + half] = bias_part[image : image + 1]
+            if gap:
+                bias[image, :, part * (half + gap) + half : (part + 1) * (half + gap)] = jnp.full((1, gap), -1e30, F32)
 
     def image_step(image, _):
         forward_image(
@@ -1166,7 +1175,6 @@
     cap_pad = up(cap, 16)
     half_pad = up(half, 16)
     hosted = groups // 2
-    context = lax.axis_index("context")
     V, A = pltpu.VMEM, pl.ANY
     dma = pltpu.SemaphoreType.DMA
     rows = w_qkv.shape[0]
@@ -1176,12 +1184,6 @@
     grad = cotangent.reshape(tokens, width)
     route_rows = routes.reshape(tokens, 2).T
 
-    mask = jnp.where(key_mask > 0, 0.0, -1e30).astype(F32)
-    first, second = mask[:, :half], mask[:, half:]
-    own = jnp.where(context == 0, first, second)
-    other = jnp.where(context == 0, second, first)
-    off = jnp.full((images, half_pad - half), -1e30, F32)
-    bias = jnp.concatenate([own, off, other, off], axis=1)[:, None, :]
     keys_pad = 2 * half_pad
 
     made = comm_call(
@@ -1212,6 +1214,7 @@
         ],
         [
             pltpu.VMEM((tokens, width), BF),
+            pltpu.VMEM((images, 1, keys_pad), F32),
             pltpu.VMEM((dps, experts, rows), BF),
             pltpu.VMEM((dps, 8, rows), BF),
             pltpu.VMEM((images, HEADS, half, keys_pad), BF),
@@ -1228,7 +1231,7 @@
         + [dma((3,))] * 2,
         flops=2 * tokens * width * (8 * width + 4 * keys_pad),
         moved=40 * tokens * width,
-    )(x, w_qkv, w_out, w_router.T, vectors, b_in, b_back, route_rows, priority.reshape(1, tokens), bias, w_in, w_back, grad)
+    )(x, w_qkv, w_out, w_router.T, vectors, b_in, b_back, route_rows, priority.reshape(1, tokens), key_mask, w_in, w_back, grad)
     qkv_all, out_all, router_rows, b_ins, b_backs, vec, slots, q, k, v, p, o, after, acts, *expert_w, grads = made
 
     rows_all = 4 * cap_pad

time: 282 us -> 281 us (level)
  no operation moved by 1% of the time
where the time goes in v9:
time: 281 us; the launch traced here: 280 us
  Pallas kernels  279 us (99%)
    pallas_call x1, Pallas kernels, shards(): comm_call(partial(back_kernel, dps, groups, images), 'back', 1, [V] * 17...  97.6 us
    pallas_call x1, Pallas kernels, shards(): comm_call(partial(experts_kernel, groups, dps, images, cap_pad), 'experts...  95.9 us
    pallas_call x1, Pallas kernels, shards(): comm_call(partial(start_kernel, dps, groups, images, cap, cap_pad), 'fron...  80.2 us
    pallas_call x1, Pallas kernels, hand_over(): pl.pallas_call(partial(hand_over_kernel, len(arrays)), name='hand_over',...  5.66 us

profile of v9, /device:TPU:0, one launch (start us, length us, event | category | flops | bytes accessed | tf_op | source)
XLA Modules:
  0.0 280.2 jit_solution(4508725351318894405)
XLA Ops:
  0.6 80.2 %front.1 = (bf16[4,128,1536]{2,1,0:T(8,128)(2,1)}, bf16[4,128,512]{2,1,0:T(8,128)(2,1)}, bf16[8,512]{1,0:T(8,128)(2,1)}, bf16[2,4,2,512]{3,2,1,0:T(2,128)(2,1)},...) custom-call(bf16[888,512]{1,0:T(8,128)(2,1)} %bitcast.13, ...), custom_call_target="tpu_custom_call" | custom-call | flops 5935988736 | bytes 18186240 | tf_op jit(solution)/shard_map/front/pallas_call | solution.py:1189
  80.8 95.9 %experts.1 = (f32[888,512]{1,0:T(8,128)}, f32[888,512]{1,0:T(8,128)}, bf16[888,512]{1,0:T(8,128)(2,1)}, f32[8,512]{1,0:T(8,128)}, f32[128,2048]{1,0:T(8,128)}, /...) custom-call(bf16[888,512]{1,0:T(8,128)(2,1)} %get-tuple-element.59.a, ...), custom_call_target="tpu_custom_call" | custom-call | flops 39460012032 | bytes 25870336 | tf_op jit(solution)/shard_map/experts/pallas_call | solution.py:1239
  176.8 97.6 %back.1 = (bf16[888,512]{1,0:T(8,128)(2,1)}, bf16[888,512]{1,0:T(8,128)(2,1)}, f32[128,1536]{1,0:T(8,128)}, f32[128,512]{1,0:T(8,128)}, f32[8,128]{1,0:T(8,128)}...) custom-call(bf16[888,512]{1,0:T(8,128)(2,1)} %bitcast.12, ...), custom_call_target="tpu_custom_call" | custom-call | flops 8147435520 | bytes 27279360 | tf_op jit(solution)/shard_map/back/pallas_call | solution.py:1302
  274.3 5.7 %hand_over.1 = (bf16[888,512]{1,0:T(8,128)(2,1)}, bf16[888,512]{1,0:T(8,128)(2,1)}, f32[8,128]{1,0:T(8,128)}, f32[7,128]{1,0:T(8,128)}, f32[128,1536]{1,0:T(8,12...) custom-call(bf16[888,512]{1,0:T(8,128)(2,1)} %get-tuple-element.88.r, ...), custom_call_target="tpu_custom_call" | custom-call | tf_op jit(solution)/shard_map/hand_over/pallas_call | solution.py:1152
